TPU v7x, 32 devices: a whole 2x2x4 slice. The times are simulated.
32 devices in a mesh: shard: 8 (over y, x, core), rep: 4 (over z).
Axes of the slice: x: 2, y: 2, z: 4, core: 2. Of those that a mesh axis runs over, the one named last changes fastest.
Arguments:
- inputs: bfloat16 [32, 1024, 768], P(('shard', 'rep')), may hold values from -6 to 6
- seq_lens: int32 [32], P(('shard', 'rep')), may hold values from 1 to 1024, 20480 in all
- pass_idx: int32 [32], P(('shard', 'rep')), may hold values from 0 to 4
- pass_table: bfloat16 [5, 768], P(None, 'shard'), may hold values from -3 to 3
- gain_attn: bfloat16 [768], P('shard'), may hold values from 0.099609375 to 1.8984375
- w_qkv: bfloat16 [768, 2304], P('shard'), may hold values from -0.21875 to 0.21875
- w_out: bfloat16 [768, 768], P('shard'), may hold values from -1.75 to 1.75
- gain_mlp: bfloat16 [768], P('shard'), may hold values from 0.099609375 to 1.8984375
- w_up: bfloat16 [768, 3072], P('shard'), may hold values from -0.21875 to 0.21875
- w_down: bfloat16 [3072, 768], P('shard'), may hold values from -0.109375 to 0.109375
- cotangent: bfloat16 [32, 1024, 768], P(('shard', 'rep')), may hold values from -6 to 6
Outputs:
- outputs: bfloat16 [32, 1024, 768], P(('shard', 'rep'))
- grad_input: float32 [32, 1024, 768], P(('shard', 'rep'))
- grad_table: float32 [5, 768], P(None, 'shard')
- grad_gain_attn: float32 [768], P('shard')
- grad_qkv: float32 [768, 2304], P('shard')
- grad_out: float32 [768, 768], P('shard')
- grad_gain_mlp: float32 [768], P('shard')
- grad_up: float32 [768, 3072], P('shard')
- grad_down: float32 [3072, 768], P('shard')
Inputs may be any that keep to these rules, and one draw needn't show every extreme that they name: Tokens from position seq_lens of a slot on are padding; in every draw some slot holds exactly 1024 real tokens. `pass_idx`: the repetition of the block that a slot is in.
All inputs are finite; a program needn't handle non-finite values. No bound on the sum of `seq_lens` on one device may be relied on, other than what follows from the above.
Results may differ from a plain program's by a relative error of at most 0.011.
Values may be sent and summed in bfloat16 or wider, within the bound.
A program may use at most 192 MiB of HBM per device.

v0:
```python
import math

import jax
import jax.numpy as jnp
from jax import lax
from jax.sharding import PartitionSpec as P

HEADS = 12
HEAD_DIM = 64


EPSILON = 1e-05
MASKED = -1e30


def layer_norm(values, scaling):
    average = jnp.mean(values, axis=-1, keepdims=True)
    centred = values - average
    variance = jnp.mean(centred * centred, axis=-1, keepdims=True)
    return centred * lax.rsqrt(variance + EPSILON) * scaling


def gelu_curve(values):
    inside_term = math.sqrt(2.0 / math.pi) * (values + 0.044715 * values * values * values)
    return 0.5 * values * (1.0 + jnp.tanh(inside_term))


def causal_allowed(first_row, block_rows, key_places, live_length):
    query_places = first_row + jnp.arange(block_rows, dtype=jnp.int32)
    return (key_places[None, :] <= query_places[:, None]) & (key_places[None, :] < live_length)


def regroup_heads(stacked, seq_count, group_count):
    shaped = stacked.reshape((seq_count, group_count) + stacked.shape[1:])
    shaped = jnp.transpose(shaped, (0, 2, 1, 3, 4))
    return shaped.reshape(
        seq_count, shaped.shape[1], group_count * shaped.shape[3], shaped.shape[4]
    )


def attention_forward(queries, all_keys, all_values, seq_lens):
    seq_count, seq_length, head_count, head_width = queries.shape
    group_heads = math.gcd(head_count, 4)
    group_count = head_count // group_heads
    block_rows = min(512, seq_length)
    score_scale = head_width ** (-0.5)
    key_places = jnp.arange(seq_length, dtype=jnp.int32)

    def one_group(flat_index):
        seq_index = flat_index // group_count
        first_head = flat_index % group_count * group_heads
        live_length = seq_lens[seq_index]
        key_part = lax.dynamic_slice(
            all_keys, (seq_index, 0, first_head, 0), (1, seq_length, group_heads, head_width)
        )[0]
        value_part = lax.dynamic_slice(
            all_values, (seq_index, 0, first_head, 0), (1, seq_length, group_heads, head_width)
        )[0]
        outputs_list = []
        sums_list = []
        for block_index in range(seq_length // block_rows):
            first_row = block_index * block_rows
            query_part = lax.dynamic_slice(
                queries,
                (seq_index, first_row, first_head, 0),
                (1, block_rows, group_heads, head_width),
            )[0]
            scores = (
                jnp.einsum("qhd,khd->hqk", query_part, key_part, preferred_element_type=jnp.float32)
                * score_scale
            )
            allowed = causal_allowed(first_row, block_rows, key_places, live_length)
            scores = jnp.where(allowed[None], scores, MASKED)
            row_top = jnp.max(scores, axis=-1, keepdims=True)
            weights = jnp.exp(scores - row_top)
            row_total = jnp.sum(weights, axis=-1, keepdims=True)
            shares = (weights / row_total).astype(jnp.bfloat16)
            mixed_rows = jnp.einsum(
                "hqk,khd->qhd", shares, value_part, preferred_element_type=jnp.float32
            )
            outputs_list.append(mixed_rows.astype(jnp.bfloat16))
            sums_list.append((row_top + jnp.log(row_total))[..., 0])
        return (jnp.concatenate(outputs_list, 0), jnp.concatenate(sums_list, 1))

    attended, log_sums = lax.map(one_group, jnp.arange(seq_count * group_count, dtype=jnp.int32))
    return (regroup_heads(attended, seq_count, group_count), log_sums)


def attention_backward(queries, all_keys, all_values, seq_lens, log_sums, attended_grad):
    seq_count, seq_length, head_count, head_width = queries.shape
    group_heads = math.gcd(head_count, 4)
    group_count = head_count // group_heads
    block_rows = min(512, seq_length)
    score_scale = head_width ** (-0.5)
    key_places = jnp.arange(seq_length, dtype=jnp.int32)

    def one_group(flat_index):
        seq_index = flat_index // group_count
        first_head = flat_index % group_count * group_heads
        live_length = seq_lens[seq_index]
        key_part = lax.dynamic_slice(
            all_keys, (seq_index, 0, first_head, 0), (1, seq_length, group_heads, head_width)
        )[0]
        value_part = lax.dynamic_slice(
            all_values, (seq_index, 0, first_head, 0), (1, seq_length, group_heads, head_width)
        )[0]
        sums_part = log_sums[flat_index]
        key_grad = jnp.zeros((seq_length, group_heads, head_width), jnp.float32)
        value_grad = jnp.zeros((seq_length, group_heads, head_width), jnp.float32)
        query_grads = []
        for block_index in range(seq_length // block_rows):
            first_row = block_index * block_rows
            query_part = lax.dynamic_slice(
                queries,
                (seq_index, first_row, first_head, 0),
                (1, block_rows, group_heads, head_width),
            )[0]
            grad_part = lax.dynamic_slice(
                attended_grad,
                (seq_index, first_row, first_head, 0),
                (1, block_rows, group_heads, head_width),
            )[0]
            scores = (
                jnp.einsum("qhd,khd->hqk", query_part, key_part, preferred_element_type=jnp.float32)
                * score_scale
            )
            allowed = causal_allowed(first_row, block_rows, key_places, live_length)
            scores = jnp.where(allowed[None], scores, MASKED)
            shares = jnp.exp(scores - sums_part[:, first_row : first_row + block_rows, None])
            share_grad = jnp.einsum(
                "qhd,khd->hqk", grad_part, value_part, preferred_element_type=jnp.float32
            )
            value_grad = value_grad + jnp.einsum(
                "hqk,qhd->khd",
                shares.astype(jnp.bfloat16),
                grad_part,
                preferred_element_type=jnp.float32,
            )
            inner_sum = jnp.sum(share_grad * shares, axis=-1, keepdims=True)
            score_grad = (shares * (share_grad - inner_sum)).astype(jnp.bfloat16)
            query_rows = (
                jnp.einsum("hqk,khd->qhd", score_grad, key_part, preferred_element_type=jnp.float32)
                * score_scale
            )
            query_grads.append(query_rows.astype(jnp.bfloat16))
            key_grad = key_grad + jnp.einsum(
                "hqk,qhd->khd", score_grad, query_part, preferred_element_type=jnp.float32
            )
        return (
            jnp.concatenate(query_grads, 0),
            (key_grad * score_scale).astype(jnp.bfloat16),
            value_grad.astype(jnp.bfloat16),
        )

    query_grad, key_grad, value_grad = lax.map(
        one_group, jnp.arange(seq_count * group_count, dtype=jnp.int32)
    )
    return (
        regroup_heads(query_grad, seq_count, group_count),
        regroup_heads(key_grad, seq_count, group_count),
        regroup_heads(value_grad, seq_count, group_count),
    )


def body(
    inputs,
    seq_lens,
    pass_idx,
    pass_table,
    gain_attn,
    w_qkv,
    w_out,
    gain_mlp,
    w_up,
    w_down,
    cotangent,
):
    seq_count, seq_length, model_width = inputs.shape
    row_count = seq_count * seq_length
    pass_rows, attn_gain, qkv_weight, out_weight = (
        lax.all_gather(pass_table, "shard", axis=1, tiled=True),
        lax.all_gather(gain_attn, "shard", axis=0, tiled=True),
        lax.all_gather(w_qkv, "shard", axis=0, tiled=True),
        lax.all_gather(w_out, "shard", axis=0, tiled=True),
    )
    pass_count = pass_rows.shape[0]
    chosen = (pass_idx[:, None] == jnp.arange(pass_count, dtype=jnp.int32)[None, :]).astype(
        jnp.bfloat16
    )
    pass_added = jnp.dot(chosen, pass_rows, preferred_element_type=jnp.float32)
    entered = (inputs.astype(jnp.float32) + pass_added[:, None, :]).reshape(row_count, model_width)
    first_gain = attn_gain.astype(jnp.float32)
    normed = layer_norm(entered, first_gain).astype(jnp.bfloat16)
    joined = jnp.dot(normed, qkv_weight, preferred_element_type=jnp.float32).astype(jnp.bfloat16)
    joined = joined.reshape(seq_count, seq_length, 3, HEADS, HEAD_DIM)
    queries = joined[:, :, 0]
    all_keys = joined[:, :, 1]
    all_values = joined[:, :, 2]
    attended, log_sums = attention_forward(queries, all_keys, all_values, seq_lens)
    attended = attended.reshape(row_count, model_width)
    branch = jnp.dot(attended, out_weight, preferred_element_type=jnp.float32)
    hidden = entered + branch
    mlp_gain, up_weight, down_weight = (
        lax.all_gather(gain_mlp, "shard", axis=0, tiled=True),
        lax.all_gather(w_up, "shard", axis=0, tiled=True),
        lax.all_gather(w_down, "shard", axis=0, tiled=True),
    )
    second_gain = mlp_gain.astype(jnp.float32)
    second = layer_norm(hidden, second_gain).astype(jnp.bfloat16)
    rising = jnp.dot(second, up_weight, preferred_element_type=jnp.float32)
    active = gelu_curve(rising).astype(jnp.bfloat16)
    result = hidden + jnp.dot(active, down_weight, preferred_element_type=jnp.float32)
    outputs = result.astype(jnp.bfloat16).reshape(seq_count, seq_length, model_width)
    mlp_gain, up_weight, down_weight = (
        lax.all_gather(gain_mlp, "shard", axis=0, tiled=True),
        lax.all_gather(w_up, "shard", axis=0, tiled=True),
        lax.all_gather(w_down, "shard", axis=0, tiled=True),
    )
    second_gain = mlp_gain.astype(jnp.float32)
    out_grad = cotangent.reshape(row_count, model_width)
    down_grad = jnp.einsum("tf,td->fd", active, out_grad, preferred_element_type=jnp.float32)
    active_grad = jnp.einsum("td,fd->tf", out_grad, down_weight, preferred_element_type=jnp.float32)
    rising_grad = jax.vjp(gelu_curve, rising)[1](active_grad)[0].astype(jnp.bfloat16)
    up_grad = jnp.einsum("td,tf->df", second, rising_grad, preferred_element_type=jnp.float32)
    second_grad = jnp.einsum(
        "tf,df->td", rising_grad, up_weight, preferred_element_type=jnp.float32
    )
    hidden_part, mlp_gain_grad = jax.vjp(layer_norm, hidden, second_gain)[1](second_grad)
    hidden_grad = out_grad.astype(jnp.float32) + hidden_part
    mlp_gain_sum, up_sum, down_sum = (
        lax.psum_scatter(mlp_gain_grad, "shard", scatter_dimension=0, tiled=True),
        lax.psum_scatter(up_grad, "shard", scatter_dimension=0, tiled=True),
        lax.psum_scatter(down_grad, "shard", scatter_dimension=0, tiled=True),
    )
    attn_gain, qkv_weight, out_weight = (
        lax.all_gather(gain_attn, "shard", axis=0, tiled=True),
        lax.all_gather(w_qkv, "shard", axis=0, tiled=True),
        lax.all_gather(w_out, "shard", axis=0, tiled=True),
    )
    first_gain = attn_gain.astype(jnp.float32)
    branch_grad = hidden_grad.astype(jnp.bfloat16)
    out_weight_grad = jnp.einsum(
        "te,td->ed", attended, branch_grad, preferred_element_type=jnp.float32
    )
    attended_grad = jnp.einsum(
        "td,ed->te", branch_grad, out_weight, preferred_element_type=jnp.float32
    ).astype(jnp.bfloat16)
    attended_grad = attended_grad.reshape(seq_count, seq_length, HEADS, HEAD_DIM)
    query_grad, key_grad, value_grad = attention_backward(
        queries, all_keys, all_values, seq_lens, log_sums, attended_grad
    )
    joined_grad = jnp.stack((query_grad, key_grad, value_grad), axis=2).reshape(
        row_count, 3 * model_width
    )
    qkv_grad = jnp.einsum("td,te->de", normed, joined_grad, preferred_element_type=jnp.float32)
    normed_grad = jnp.einsum(
        "te,de->td", joined_grad, qkv_weight, preferred_element_type=jnp.float32
    )
    entered_part, attn_gain_grad = jax.vjp(layer_norm, entered, first_gain)[1](normed_grad)
    grad_input = (hidden_grad + entered_part).reshape(seq_count, seq_length, model_width)
    table_grad = jnp.dot(
        chosen.astype(jnp.float32).T, jnp.sum(grad_input, axis=1), precision=lax.Precision.HIGHEST
    )
    table_sum, attn_gain_sum, qkv_sum, out_sum = (
        lax.psum_scatter(table_grad, "shard", scatter_dimension=1, tiled=True),
        lax.psum_scatter(attn_gain_grad, "shard", scatter_dimension=0, tiled=True),
        lax.psum_scatter(qkv_grad, "shard", scatter_dimension=0, tiled=True),
        lax.psum_scatter(out_weight_grad, "shard", scatter_dimension=0, tiled=True),
    )
    table_sum, attn_gain_sum, qkv_sum, out_sum, mlp_gain_sum, up_sum, down_sum = lax.psum(
        (table_sum, attn_gain_sum, qkv_sum, out_sum, mlp_gain_sum, up_sum, down_sum), "rep"
    )
    return (
        outputs,
        grad_input,
        table_sum,
        attn_gain_sum,
        qkv_sum,
        out_sum,
        mlp_gain_sum,
        up_sum,
        down_sum,
    )


def solution(mesh):
    return jax.shard_map(
        body,
        mesh=mesh,
        in_specs=(
            P(("shard", "rep"), None, None),
            P(("shard", "rep")),
            P(("shard", "rep")),
            P(None, "shard"),
            P("shard"),
            P("shard", None),
            P("shard", None),
            P("shard"),
            P("shard", None),
            P("shard", None),
            P(("shard", "rep"), None, None),
        ),
        out_specs=(
            P(("shard", "rep"), None, None),
            P(("shard", "rep"), None, None),
            P(None, "shard"),
            P("shard"),
            P("shard", None),
            P("shard", None),
            P("shard"),
            P("shard", None),
            P("shard", None),
        ),
        check_vma=False,
    )
```

profile of v0, /device:TPU:0, one launch (start us, length us, event | category | flops | bytes accessed | tf_op | source)
XLA Modules:
  0.0 732.4 jit_solution(12806904935102294517)
XLA Ops:
  14.4 15.4 %all-reduce.7 = (bf16[768]{0:T(1024)(128)(2,1)S(1)}, bf16[768]{0:T(1024)(128)(2,1)S(1)}) all-reduce(bf16[768]{0:T(1024)(128)(2,1)S(1)} %dynamic-update-slice, bf16[768]{0:T(1024)(128)(2,1)S(1)} %dynamic-update-slice.1), channel_id=1, replica_groups=mesh['shard'=8,'rep'=4] {'shard'}, use_global_device_ids=true, to_apply=%add | all-reduce | flops 1536 | bytes 6144
  30.4 8.2 %all-gather = bf16[8,96,5]{1,2,0:T(8,128)(2,1)S(1)} all-gather(bf16[1,96,5]{1,2,0:T(8,128)(2,1)} %bitcast.300), channel_id=1, replica_groups=mesh['shard'=8,'rep'=4] {'shard'}, dimensions={0}, use_global_device_ids=true | all-gather | bytes 8640 | tf_op jit(solution)/shard_map/all_gather | solution.py:181
  46.6 7.9 %convolution_convert_fusion = bf16[1024,2304]{1,0:T(8,128)(2,1)} fusion(bf16[768,2304]{1,0:T(8,128)(2,1)} %all-gather.6.cloned.1.call-done, bf16[1,1024,768]{1,2,0:T(8,128)(2,1)S(1)} %copy.43, f32[768]{0:T(1024)S(1)} %convert_element_type.136, f32[1024]{0:T(1024)S(1)} %fusion.152, f32[1024]{0:T(1024)S(1)} %broadcast_multiply_fusion.2, ...), kind=kOutput, calls=%fused_computation.152 | convolution fusion | flops 3630956544 | bytes 9844736 | tf_op jit(solution)/shard_map/dot_general | solution.py:194
  54.5 6.7 copy.45
  61.2 4.2 slice_bitcast_fusion
  66.8 51.3 %while.34 = (s32[]{:T(128)}, bf16[3,1024,4,64]{1,3,2,0:T(8,128)(2,1)}, f32[3,4,1024]{2,1,0:T(4,128)S(1)}, s32[3]{0:T(128)S(1)}, bf16[1,1024,12,64]{1,3,2,0:T(8,1...) while((s32[]{:T(128)}, ...), condition=%wide.region_7.8_spmd.clone.clone, body=%wide.region_2.7_spmd.clone.clone.sunk | while | flops 1127482880 | bytes 65184048 | solution.py:85
  72.8 4.6 fusion.230
  77.5 2.8 fusion.232
  80.3 2.8 fusion.231
  89.8 4.6 fusion.230
  94.5 2.8 fusion.232
  97.3 2.8 fusion.231
  106.9 4.6 fusion.230
  111.5 2.8 fusion.232
  114.3 2.8 fusion.231
  118.0 3.9 fusion.166
  124.0 11.5 %fusion.159 = f32[1024,3072]{1,0:T(8,128)} fusion(bf16[768,3072]{1,0:T(8,128)(2,1)} %all-gather.10.cloned.1.call-done, f32[1024,768]{0,1:T(8,128)} %copy-done.4, f32[768]{0:T(1024)S(1)} %copy-done.25, f32[1024]{0:T(1024)S(1)} %fusion.153, f32[1024]{0:T(1024)S(1)} %broadcast_multiply_fusion.1), kind=kOutput, calls=%fused_computation.213 | convolution fusion | flops 4834983936 | bytes 20458496 | tf_op jit(solution)/shard_map/dot_general | solution.py:210
  135.5 18.2 %all-gather.12.cloned.1.call-done = bf16[3072,768]{1,0:T(8,128)(2,1)} async-done(((bf16[384,768]{1,0:T(8,128)(2,1)}), bf16[3072,768]{1,0:T(8,128)(2,1)}) %all-gather.12.cloned.1.call-update) | async-done | bytes 4718608 | tf_op jit(solution)/shard_map/all_gather | solution.py:206
  153.7 16.9 %fusion.127 = bf16[1024,3072]{1,0:T(8,128)(2,1)S(1)} fusion(f32[1024,3072]{1,0:T(8,128)} %fusion.159, bf16[3072,768]{1,0:T(8,128)(2,1)} %all-gather.12.cloned.1.call-done, bf16[1,1024,768]{2,1,0:T(8,128)(2,1)} %param.25), kind=kOutput, calls=%fused_computation.147 | convolution fusion | flops 4907335680 | bytes 25165824 | tf_op jit(solution)/shard_map/td,fd->tf/dot_general | solution.py:222
  170.6 6.1 multiply_reduce_fusion.2
  180.4 2.9 fusion.167
  183.4 4.3 convolution_convert_fusion.1
  191.7 115.6 %while.35 = (s32[]{:T(128)}, bf16[3,1024,4,64]{1,3,2,0:T(8,128)(2,1)}, bf16[3,1024,4,64]{1,3,2,0:T(8,128)(2,1)}, bf16[3,1024,4,64]{1,3,2,0:T(8,128)(2,1)}, s32[3...) while((s32[]{:T(128)}, ...), condition=%wide.region_15.16_spmd.clone.clone, body=%wide.region_12.15_spmd.clone.clone.sunk | while | flops 2752247296 | bytes 167406032 | solution.py:155
  201.4 3.3 fusion.261
  204.7 5.4 multiply_reduce_fusion.10
  210.1 5.4 multiply_reduce_fusion.11
  215.5 8.4 %multiply_convert_fusion.9 = (bf16[4,512,1024]{2,1,0:T(8,128)(2,1)S(1)}, bf16[4,512,1024]{2,1,0:T(8,128)(2,1)S(1)}) fusion(f32[4,512,1024]{2,1,0:T(8,128)} %get-tuple-element.642, f32[4,512,1024]{2,1,0:T(8,128)S(1)} %fusion.251, f32[4,512]{1,0:T(4,128)S(1)} %get-tuple-element.643, f32[4,512]{1,0:T(4,128)S(1)} %get-tuple-element.640, ...), kind=kLoop, calls=%fused_computation.53.clone.1 | loop fusion | flops 25165824 | bytes 43024384 | tf_op jit(solution)/shard_map/while/body/eval_jaxpr/convert_element_type | solution.py:140
  239.9 3.3 fusion.261
  243.1 5.4 multiply_reduce_fusion.10
  248.5 5.4 multiply_reduce_fusion.11
  253.9 8.3 %multiply_convert_fusion.9 = (bf16[4,512,1024]{2,1,0:T(8,128)(2,1)S(1)}, bf16[4,512,1024]{2,1,0:T(8,128)(2,1)S(1)}) fusion(f32[4,512,1024]{2,1,0:T(8,128)} %get-tuple-element.642, f32[4,512,1024]{2,1,0:T(8,128)S(1)} %fusion.251, f32[4,512]{1,0:T(4,128)S(1)} %get-tuple-element.643, f32[4,512]{1,0:T(4,128)S(1)} %get-tuple-element.640, ...), kind=kLoop, calls=%fused_computation.53.clone.1 | loop fusion | flops 25165824 | bytes 43024384 | tf_op jit(solution)/shard_map/while/body/eval_jaxpr/convert_element_type | solution.py:140
  278.3 3.3 fusion.261
  281.6 5.4 multiply_reduce_fusion.10
  287.0 5.4 multiply_reduce_fusion.11
  292.4 8.3 %multiply_convert_fusion.9 = (bf16[4,512,1024]{2,1,0:T(8,128)(2,1)S(1)}, bf16[4,512,1024]{2,1,0:T(8,128)(2,1)S(1)}) fusion(f32[4,512,1024]{2,1,0:T(8,128)} %get-tuple-element.642, f32[4,512,1024]{2,1,0:T(8,128)S(1)} %fusion.251, f32[4,512]{1,0:T(4,128)S(1)} %get-tuple-element.643, f32[4,512]{1,0:T(4,128)S(1)} %get-tuple-element.640, ...), kind=kLoop, calls=%fused_computation.53.clone.1 | loop fusion | flops 25165824 | bytes 43024384 | tf_op jit(solution)/shard_map/while/body/eval_jaxpr/convert_element_type | solution.py:140
  312.3 6.4 fusion.135
  319.4 10.5 %fusion.158 = f32[768,3072]{1,0:T(8,128)} fusion(bf16[1024,3072]{1,0:T(8,128)(2,1)} %copy-done.43, f32[1024,768]{0,1:T(8,128)} %copy-done.4, f32[768]{0:T(1024)S(1)} %copy-done.26, f32[1024]{0:T(1024)S(1)} %copy-done.28, f32[1024]{0:T(1024)S(1)} %copy-done.24), kind=kOutput, calls=%fused_computation.212 | convolution fusion | flops 4834983936 | bytes 18885632 | tf_op jit(solution)/shard_map/td,tf->df/dot_general | solution.py:224
  331.6 13.6 %fusion.137 = f32[3072,768]{1,0:T(8,128)} fusion(bf16[1,1024,768]{2,1,0:T(8,128)(2,1)S(1)} %copy-done.18, f32[1024,3072]{1,0:T(8,128)} %fusion.159), kind=kOutput, calls=%fused_computation.180 | convolution fusion | flops 4860149760 | bytes 23592960 | tf_op jit(solution)/shard_map/tf,td->fd/dot_general | solution.py:221
  345.2 6.9 multiply_reduce_fusion.4
  354.6 3.6 multiply_reduce_fusion.3
  359.3 25.2 %reduce-scatter.8.cloned.1.call-done = f32[96,2304]{1,0:T(8,128)} async-done(((f32[768,2304]{1,0:T(8,128)}), f32[96,2304]{1,0:T(8,128)}) %reduce-scatter.8.cloned.1.call-update) | async-done | bytes 884752 | tf_op jit(solution)/shard_map/reduce_scatter | solution.py:267
  384.5 80.3 %reduce-scatter.12.cloned.1.call-done = f32[96,3072]{1,0:T(8,128)} async-done(((f32[768,3072]{1,0:T(8,128)}), f32[96,3072]{1,0:T(8,128)}) %reduce-scatter.12.cloned.1.call-update) | async-done | bytes 1179664 | tf_op jit(solution)/shard_map/reduce_scatter | solution.py:232
  464.8 80.3 %reduce-scatter.14.cloned.1.call-done = f32[384,768]{1,0:T(8,128)} async-done(((f32[3072,768]{1,0:T(8,128)}), f32[384,768]{1,0:T(8,128)}) %reduce-scatter.14.cloned.1.call-update) | async-done | bytes 1179664 | tf_op jit(solution)/shard_map/reduce_scatter | solution.py:233
  545.9 11.3 %fusion.148 = bf16[1,1024,768]{1,2,0:T(8,128)(2,1)} fusion(f32[1024,768]{0,1:T(8,128)S(1)} %copy-done.6, bf16[3072,768]{1,0:T(8,128)(2,1)} %all-gather.12.cloned.1.call-done, f32[1024,3072]{1,0:T(8,128)} %fusion.159), kind=kOutput, calls=%fused_computation.191 | convolution fusion | flops 4861722624 | bytes 22020096 | tf_op jit(solution)/shard_map/dot_general | solution.py:212
  559.9 12.7 %all-reduce.4 = (f32[768]{0:T(1024)S(1)}, f32[768]{0:T(1024)S(1)}) all-reduce(f32[768]{0:T(1024)S(1)} %get-tuple-element.416, f32[768]{0:T(1024)S(1)} %copy-done.42), channel_id=3, replica_groups=mesh['shard'=8,'rep'=4] {'shard'}, use_global_device_ids=true, to_apply=%region_22.23.clone | all-reduce | flops 1536 | bytes 12288
  575.1 7.6 %reduce-scatter.16.cloned.1.call-done = f32[96,5]{1,0:T(8,128)} async-done(((f32[768,5]{1,0:T(8,128)}), f32[96,5]{1,0:T(8,128)}) %reduce-scatter.16.cloned.1.call-update) | async-done | bytes 1936
  583.6 12.6 %all-reduce.5 = (f32[5,96]{1,0:T(8,128)}, f32[96]{0:T(128)}, f32[96]{0:T(128)}) all-reduce(f32[5,96]{1,0:T(8,128)S(1)} %copy.58, f32[96]{0:T(128)S(1)} %dynamic-slice.3, f32[96]{0:T(128)S(1)} %dynamic-slice.5), channel_id=1, replica_groups=mesh['shard'=8,'rep'=4] {'rep'}, use_global_device_ids=true, to_apply=%region_20.21 | all-reduce | flops 672 | bytes 5376 | tf_op jit(solution)/shard_map/psum | solution.py:270
  596.2 122.9 %all-reduce.10.cloned.1.call-done = (f32[96,2304]{1,0:T(8,128)}, f32[96,768]{1,0:T(8,128)}, f32[96,3072]{1,0:T(8,128)}, f32[384,768]{1,0:T(8,128)}) async-done(((f32[96,2304]{1,0:T(8,128)}, f32[96,768]{1,0:T(8,128)}, f32[96,3072]{1,0:T(8,128)}, f32[384,768]{1,0:T(8,128)}), (f32[96,2304]{1,0:T(8,128)}, f32[96,768]{1,0:T(8,128)}, f32[96,3072]{1,0:T(8,128)}, ...) | async-done | bytes 3538960 | tf_op jit(solution)/shard_map/psum | solution.py:270
  (250 shorter events, 106.4 us)
Async XLA Ops:
  7.2 39.4 %all-gather.6.cloned.1.call-start = ((), (), s32[]{:S(2)}) async-start(), calls=%async_computation.5 | async-start | bytes 3981312 | tf_op jit(solution)/shard_map/all_gather | solution.py:183
  7.9 110.1 %all-gather.8.cloned.1.call-start = ((), (), s32[]{:S(2)}) async-start(), calls=%async_computation.6 | async-start | bytes 1327104 | tf_op jit(solution)/shard_map/all_gather | solution.py:184
  8.7 115.4 %all-gather.10.cloned.1.call-start = ((), (), s32[]{:S(2)}) async-start(), calls=%async_computation.7 | async-start | bytes 5308416 | tf_op jit(solution)/shard_map/all_gather | solution.py:205
  9.4 144.3 %all-gather.12.cloned.1.call-start = ((), (), s32[]{:S(2)}) async-start(), calls=%async_computation.8 | async-start | bytes 5308416 | tf_op jit(solution)/shard_map/all_gather | solution.py:206
  10.0 349.3 %reduce-scatter.10.cloned.1.call-start = ((), (), s32[]{:S(2)}) async-start(), calls=%async_computation.10 | async-start | bytes 2654208 | tf_op jit(solution)/shard_map/reduce_scatter | solution.py:268
  29.8 16.8 %copy-start.34 = (f32[768]{0:T(1024)}, f32[768]{0:T(1024)S(1)}, u32[]{:S(2)}) copy-start(f32[768]{0:T(1024)S(1)} %convert_element_type.136) | copy-start | bytes 9220
  38.7 3.6 copy-start.17
  40.6 6.0 copy-start
  40.7 5.9 copy-start.29
  41.1 13.4 %copy-start.32 = (f32[1024]{0:T(1024)}, f32[1024]{0:T(1024)S(1)}, u32[]{:S(2)}) copy-start(f32[1024]{0:T(1024)S(1)} %broadcast_multiply_fusion.2) | copy-start | bytes 12292
  42.3 12.2 %copy-start.36 = (f32[1024]{0:T(1024)}, f32[1024]{0:T(1024)S(1)}, u32[]{:S(2)}) copy-start(f32[1024]{0:T(1024)S(1)} %fusion.152) | copy-start | bytes 12292
  66.8 51.3 %copy-start.30 = (f32[768]{0:T(1024)S(1)}, f32[768]{0:T(1024)}, u32[]{:S(2)}) copy-start(f32[768]{0:T(1024)} %copy-done.29) | copy-start | bytes 9220
  72.8 4.6 copy-start.2
  89.8 4.6 copy-start.2
  106.9 4.6 copy-start.2
  121.9 1.7 copy-start.4
  121.9 2.1 copy-start.25
  122.0 54.8 %copy-start.23 = (f32[1024]{0:T(1024)}, f32[1024]{0:T(1024)S(1)}, u32[]{:S(2)}) copy-start(f32[1024]{0:T(1024)S(1)} %broadcast_multiply_fusion.1) | copy-start | bytes 12292
  124.0 52.7 %copy-start.27 = (f32[1024]{0:T(1024)}, f32[1024]{0:T(1024)S(1)}, u32[]{:S(2)}) copy-start(f32[1024]{0:T(1024)S(1)} %fusion.153) | copy-start | bytes 12292
  153.7 16.9 %copy-start.5 = (f32[1024,768]{0,1:T(8,128)S(1)}, f32[1024,768]{0,1:T(8,128)}, u32[]{:S(2)}) copy-start(f32[1024,768]{0,1:T(8,128)} %copy-done.4) | copy-start | bytes 9437188
  153.7 16.9 %copy-start.14 = (bf16[768,3072]{1,0:T(8,128)(2,1)S(1)}, bf16[768,3072]{1,0:T(8,128)(2,1)}, u32[]{:S(2)}) copy-start(bf16[768,3072]{1,0:T(8,128)(2,1)} %all-gather.10.cloned.1.call-done) | copy-start | bytes 14155780
  170.6 6.1 copy-start.43
  177.5 1.7 copy-start.7
  177.6 1.7 copy-start.40
  178.1 2.3 copy-start.19
  183.3 201.2 %reduce-scatter.8.cloned.1.call-start = ((), (), s32[]{:S(2)}) async-start(), calls=%async_computation.9 | async-start | bytes 7962624 | tf_op jit(solution)/shard_map/reduce_scatter | solution.py:267
  201.4 3.3 copy-start.3
  239.9 3.3 copy-start.3
  278.3 3.3 copy-start.3
  307.3 5.0 copy-start.1
  307.3 5.0 copy-start.31
  307.3 4.9 copy-start.33
  307.4 4.9 copy-start.35
  307.4 4.9 copy-start.37
  310.1 2.2 copy-start.15
  318.7 146.1 %reduce-scatter.12.cloned.1.call-start = ((), (), s32[]{:S(2)}) async-start(), calls=%async_computation.11 | async-start | bytes 10616832 | tf_op jit(solution)/shard_map/reduce_scatter | solution.py:232
  330.0 215.2 %reduce-scatter.14.cloned.1.call-start = ((), (), s32[]{:S(2)}) async-start(), calls=%async_computation.12 | async-start | bytes 10616832 | tf_op jit(solution)/shard_map/reduce_scatter | solution.py:233
  345.2 237.6 %reduce-scatter.16.cloned.1.call-start = ((), (), s32[]{:S(2)}) async-start(), calls=%async_computation.13 | async-start | bytes 442368
  345.2 7.0 copy-start.39
  352.2 1.9 copy-start.8
  352.2 2.3 copy-start.10
  352.2 2.3 copy-start.41
  358.2 187.7 %copy-start.6 = (f32[1024,768]{0,1:T(8,128)S(1)}, f32[1024,768]{0,1:T(8,128)}, u32[]{:S(2)}) copy-start(f32[1024,768]{0,1:T(8,128)} %copy-done.4) | copy-start | bytes 9437188
  359.2 359.9 %all-reduce.10.cloned.1.call-start = ((), (), s32[]{:S(2)}) async-start(), calls=%async_computation.14 | async-start | bytes 7077888 | tf_op jit(solution)/shard_map/psum | solution.py:270
  545.9 14.0 %copy-start.42 = (f32[768]{0:T(1024)S(1)}, f32[768]{0:T(1024)}, u32[]{:S(2)}) copy-start(f32[768]{0:T(1024)} %get-tuple-element.414) | copy-start | bytes 9220
  557.1 15.6 %copy-start.11 = (f32[1,1024,768]{1,2,0:T(8,128)S(1)}, f32[1,1024,768]{1,2,0:T(8,128)}, u32[]{:S(2)}) copy-start(f32[1,1024,768]{1,2,0:T(8,128)} %get-tuple-element.487) | copy-start | bytes 9437188
  719.1 4.0 copy-start.22
  719.1 5.0 copy-start.21
  (16 other events, 19.4 us)
Sparse Core Ops, SparseCore 0:
  9.9 36.6 all-gather.5
  48.5 23.9 all-gather.7
  74.3 38.7 all-gather.9
  114.9 38.7 all-gather.11
  183.4 42.3 reduce-scatter.9
  318.8 65.6 reduce-scatter.7
  388.0 76.8 reduce-scatter.11
  468.3 76.8 reduce-scatter.13
  548.8 33.8 reduce-scatter.15
  585.2 133.8 all-reduce.9
where the time goes:
time: 738 us; the launch traced here: 732 us
  waiting for transfers between devices  340 us (46%)
  matrix products  200 us (27%)
  other arithmetic  62.3 us (8%)
  local copies, waits for them, and re-layouts  52.9 us (7%)
  blocking collectives  49 us (7%)
  between operations  17.1 us (2%)
  loops' own time  10.9 us (1%)
    psum x1, waiting for transfers between devices, body(): lax.psum((table_sum, attn_gain_sum, qkv_sum, out_sum, mlp_gain_sum, up_su...  123 us
    reduce_scatter x1, waiting for transfers between devices, body(): lax.psum_scatter(down_grad, 'shard', scatter_dimension=0, tiled=True)  80.3 us
    reduce_scatter x1, waiting for transfers between devices, body(): lax.psum_scatter(up_grad, 'shard', scatter_dimension=0, tiled=True)  80.3 us
    dot_general x6, matrix products, one_group(): jnp.einsum('qhd,khd->hqk', grad_part, value_part, preferred_element_type=...  32.4 us
    unnamed x96, local copies, waits for them, and re-layouts  29.9 us
    unnamed x2, blocking collectives  28.1 us
    reduce_scatter x1, waiting for transfers between devices, body(): lax.psum_scatter(qkv_grad, 'shard', scatter_dimension=0, tiled=True)  25.2 us
    convert_element_type x3, other arithmetic, one_group(): score_grad = (shares * (share_grad - inner_sum)).astype(jnp.bfloat16)  25 us
  transfers between devices with their start and end apart: 10, of which 7 were waited for; matrix products, arithmetic and copies ran while one was open for 37% of the time, Pallas kernels for 0%

commit v1 on v0

v1 whole, which is shorter than its diff:
```python
import functools
import math

import jax
import jax.numpy as jnp
from jax import lax
from jax.experimental import pallas as pl
from jax.experimental.pallas import tpu as pltpu
from jax.sharding import PartitionSpec as P

HEADS = 12
HEAD_DIM = 64
PAIR = 2 * HEAD_DIM
EPSILON = 1e-05
MASKED = -1e30
BF16 = jnp.bfloat16
F32 = jnp.float32
VMEM_LIMIT = 64 * 1024 * 1024 - 65536

NN = (((1,), (0,)), ((), ()))
NT = (((1,), (1,)), ((), ()))
TN = (((0,), (0,)), ((), ()))


def mm(a, b, dims=NN):
    return lax.dot_general(a, b, dims, preferred_element_type=F32)


def norm_parts(values):
    average = jnp.mean(values, axis=-1, keepdims=True)
    centred = values - average
    variance = jnp.mean(centred * centred, axis=-1, keepdims=True)
    scale = lax.rsqrt(variance + EPSILON)
    return centred * scale, scale


def norm_back(unit, scale, grad, gain):
    scaled = grad * gain
    part = scaled - jnp.mean(scaled, axis=-1, keepdims=True)
    return scale * (part - unit * jnp.mean(scaled * unit, axis=-1, keepdims=True))


def lanes_of(shape):
    return lax.broadcasted_iota(jnp.int32, shape, len(shape) - 1)


def head_only(values, head, zero_at=None):
    lanes = lanes_of(values.shape)
    own = (lanes < HEAD_DIM) if head == 0 else (lanes >= HEAD_DIM)
    return jnp.where(own, values, jnp.zeros_like(values)), own, lanes


def query_with_bias(query, head):
    kept, own, lanes = head_only(query * BF16(HEAD_DIM**-0.5), head)
    spot = HEAD_DIM if head == 0 else 0
    return jnp.where(lanes == spot, jnp.ones_like(kept), kept), kept


def key_with_bias(keys, bias, head):
    kept, own, lanes = head_only(keys, head)
    spot = HEAD_DIM if head == 0 else 0
    return jnp.where(lanes == spot, bias, kept), kept


def attention_front(length, joined, attended, log_sums, key_bias, pair, block):
    rows = attended.shape[0]
    width = attended.shape[1]
    at = pl.multiple_of(pair * PAIR, PAIR)
    keys = joined[:, pl.ds(width + at, PAIR)]
    values = joined[:, pl.ds(2 * width + at, PAIR)]
    bias = key_bias[...]
    biased = [key_with_bias(keys, bias, head)[0] for head in range(2)]
    for first in range(0, rows, block):
        live = first + block
        query = joined[pl.ds(first, block), pl.ds(at, PAIR)]
        mixed = []
        sums = []
        for head in range(2):
            asked, _ = query_with_bias(query, head)
            scores = mm(asked, biased[head][:live], NT)
            row_at = lax.broadcasted_iota(jnp.int32, (block, block), 0)
            key_at = lax.broadcasted_iota(jnp.int32, (block, block), 1)
            last = jnp.where(key_at <= row_at, scores[:, first:], MASKED)
            scores = last if first == 0 else jnp.concatenate([scores[:, :first], last], axis=1)
            top = jnp.max(scores, axis=-1, keepdims=True)
            weights = jnp.exp(scores - top)
            total = jnp.sum(weights, axis=-1, keepdims=True)
            mixed.append(mm(weights.astype(BF16), values[:live]) / total)
            sums.append(top + jnp.log(total))
        lanes = lanes_of(mixed[0].shape)
        attended[pl.ds(first, block), pl.ds(at, PAIR)] = jnp.where(
            lanes < HEAD_DIM, mixed[0], mixed[1]
        ).astype(BF16)
        log_sums[pair, pl.ds(first, block), :] = jnp.where(lanes < HEAD_DIM, sums[0], sums[1])


def fill_bias(length, key_bias):
    rows = key_bias.shape[0]
    places = lax.broadcasted_iota(jnp.int32, key_bias.shape, 0)
    key_bias[...] = jnp.where(places < length, 0.0, MASKED).astype(BF16)


def front_kernel(
    block, tile, length_ref, inputs, pass_row, gain, w_qkv, w_out,
    joined_out, attended_out, sums_out, hidden_out, normed, key_bias,
):
    rows, width = inputs.shape
    length = length_ref[0]
    fill_bias(length, key_bias)

    @pl.loop(0, rows // 256)
    def _(step):
        at = pl.ds(step * 256, 256)
        entered = inputs[at, :].astype(F32) + pass_row[0:1, :]
        normed[at, :] = (norm_parts(entered)[0] * gain[0:1, :]).astype(BF16)

    @pl.loop(0, 3)
    def _(part):
        columns = pl.ds(pl.multiple_of(part * width, width), width)

        @pl.loop(0, rows // tile)
        def _(step):
            at = pl.ds(step * tile, tile)
            joined_out[at, columns] = mm(normed[at, :], w_qkv[:, columns]).astype(BF16)

    @pl.loop(0, HEADS // 2)
    def _(pair):
        attention_front(length, joined_out, attended_out, sums_out, key_bias, pair, block)

    @pl.loop(0, rows // tile)
    def _(step):
        at = pl.ds(step * tile, tile)
        entered = inputs[at, :].astype(F32) + pass_row[0:1, :]
        hidden_out[at, :] = entered + mm(attended_out[at, :], w_out[...])


def gelu_both(values):
    outer = math.sqrt(2.0 / math.pi)
    square = values * values
    bent = jnp.tanh(outer * values * (1.0 + 0.044715 * square))
    half = 0.5 * (1.0 + bent)
    slope = half + 0.5 * values * (1.0 - bent * bent) * (outer * (1.0 + 3 * 0.044715 * square))
    return values * half, slope


def mlp_kernel(
    tile, chunk, hidden, cotangent, gain, w_up, w_down,
    outputs, hidden_grad, gain_grad, up_grad, down_grad,
    second, mixed, second_grad, active, rising_grad,
):
    rows, width = hidden.shape
    chunks = w_down.shape[0] // chunk

    @pl.loop(0, rows // 256)
    def _(step):
        at = pl.ds(step * 256, 256)
        second[at, :] = (norm_parts(hidden[at, :])[0] * gain[0:1, :]).astype(BF16)
        mixed[at, :] = hidden[at, :]
        second_grad[at, :] = jnp.zeros((256, width), F32)

    @pl.loop(0, chunks)
    def _(part):
        units = pl.ds(pl.multiple_of(part * chunk, chunk), chunk)

        @pl.loop(0, rows // tile)
        def _(step):
            at = pl.ds(step * tile, tile)
            rising = mm(second[at, :], w_up[:, units])
            active_grad = mm(cotangent[at, :], w_down[units, :], NT)
            bent, slope = gelu_both(rising)
            shown = bent.astype(BF16)
            moved = (slope * active_grad).astype(BF16)
            active[at, :] = shown
            rising_grad[at, :] = moved
            mixed[at, :] += mm(shown, w_down[units, :])
            second_grad[at, :] += mm(moved, w_up[:, units], NT)

        down_grad[units, :] = mm(active[...], cotangent[...], TN).astype(BF16)
        up_grad[:, units] = mm(second[...], rising_grad[...], TN).astype(BF16)

    gain_grad[...] = jnp.zeros_like(gain_grad)

    @pl.loop(0, rows // 256)
    def _(step):
        at = pl.ds(step * 256, 256)
        outputs[at, :] = mixed[at, :].astype(BF16)
        unit, scale = norm_parts(hidden[at, :])
        grad = second_grad[at, :]
        hidden_grad[at, :] = cotangent[at, :].astype(F32) + norm_back(unit, scale, grad, gain[0:1, :])
        gain_grad[0:1, :] += jnp.sum(grad * unit, axis=0, keepdims=True)


def attention_back(joined, log_rows, grads, joined_grad, key_bias, key_total, value_total, pair, block):
    rows = grads.shape[0]
    width = grads.shape[1]
    at = pl.multiple_of(pair * PAIR, PAIR)
    keys = joined[:, pl.ds(width + at, PAIR)]
    values = joined[:, pl.ds(2 * width + at, PAIR)]
    bias = key_bias[...]
    biased = [key_with_bias(keys, bias, head) for head in range(2)]
    key_total[...] = jnp.zeros_like(key_total)
    value_total[...] = jnp.zeros_like(value_total)
    for first in range(0, rows, block):
        live = first + block
        query = joined[pl.ds(first, block), pl.ds(at, PAIR)]
        grad = grads[pl.ds(first, block), pl.ds(at, PAIR)]
        query_grad = None
        for head in range(2):
            asked, asked_only = query_with_bias(query, head)
            grad_only = head_only(grad, head)[0]
            scores = mm(biased[head][0][:live], asked, NT)
            share_grad = mm(values[:live], grad_only, NT)
            log_sum = log_rows[pl.ds(pair * 2 + head, 1), pl.ds(first, block)]
            shares = jnp.exp(scores - log_sum)
            key_at = lax.broadcasted_iota(jnp.int32, (block, block), 0)
            row_at = lax.broadcasted_iota(jnp.int32, (block, block), 1)
            last = jnp.where(key_at <= row_at, shares[first:], 0.0)
            shares = last if first == 0 else jnp.concatenate([shares[:first], last], axis=0)
            inner = jnp.sum(share_grad * shares, axis=0, keepdims=True)
            score_grad = (shares * (share_grad - inner)).astype(BF16)
            value_total[:live, :] += mm(shares.astype(BF16), grad_only)
            key_total[:live, :] += mm(score_grad, asked_only)
            part = mm(score_grad, biased[head][1][:live], TN)
            query_grad = part if query_grad is None else query_grad + part
        joined_grad[pl.ds(first, block), pl.ds(at, PAIR)] = (
            query_grad * HEAD_DIM**-0.5
        ).astype(BF16)
    joined_grad[:, pl.ds(width + at, PAIR)] = key_total[...].astype(BF16)
    joined_grad[:, pl.ds(2 * width + at, PAIR)] = value_total[...].astype(BF16)


def back_kernel(
    block, tile, length_ref, inputs, pass_row, gain, w_qkv, w_out, joined, log_rows, attended, hidden_grad,
    grad_input, gain_grad, table_grad, qkv_grad, out_grad,
    branch_grad, attended_grad, normed, joined_grad, key_bias, key_total, value_total,
):
    rows, width = inputs.shape
    length = length_ref[0]
    fill_bias(length, key_bias)

    @pl.loop(0, rows // 256)
    def _(step):
        at = pl.ds(step * 256, 256)
        branch_grad[at, :] = hidden_grad[at, :].astype(BF16)
        entered = inputs[at, :].astype(F32) + pass_row[0:1, :]
        normed[at, :] = (norm_parts(entered)[0] * gain[0:1, :]).astype(BF16)

    @pl.loop(0, rows // tile)
    def _(step):
        at = pl.ds(step * tile, tile)
        attended_grad[at, :] = mm(branch_grad[at, :], w_out[...], NT).astype(BF16)

    out_grad[...] = mm(attended[...], branch_grad[...], TN).astype(BF16)

    @pl.loop(0, HEADS // 2)
    def _(pair):
        attention_back(
            joined, log_rows, attended_grad, joined_grad, key_bias, key_total, value_total, pair, block
        )

    @pl.loop(0, 3)
    def _(part):
        columns = pl.ds(pl.multiple_of(part * width, width), width)
        qkv_grad[:, columns] = mm(normed[...], joined_grad[:, columns], TN).astype(BF16)

    gain_grad[...] = jnp.zeros_like(gain_grad)
    table_grad[...] = jnp.zeros_like(table_grad)

    @pl.loop(0, rows // 256)
    def _(step):
        at = pl.ds(step * 256, 256)
        grad = mm(joined_grad[at, :], w_qkv[...], NT)
        unit, scale = norm_parts(inputs[at, :].astype(F32) + pass_row[0:1, :])
        total = hidden_grad[at, :] + norm_back(unit, scale, grad, gain[0:1, :])
        grad_input[at, :] = total
        gain_grad[0:1, :] += jnp.sum(grad * unit, axis=0, keepdims=True)
        table_grad[0:1, :] += jnp.sum(total, axis=0, keepdims=True)


def whole(count):
    return [pl.BlockSpec(memory_space=pltpu.VMEM)] * count


def call(kernel, outs, scratch, *args, scalars=0):
    specs = [pl.BlockSpec(memory_space=pltpu.SMEM)] * scalars + whole(len(args) - scalars)
    return pl.pallas_call(
        kernel,
        out_shape=[jax.ShapeDtypeStruct(shape, kind) for shape, kind in outs],
        in_specs=specs,
        out_specs=whole(len(outs)),
        scratch_shapes=[pltpu.VMEM(shape, kind) for shape, kind in scratch],
        compiler_params=pltpu.CompilerParams(vmem_limit_bytes=VMEM_LIMIT),
    )(*args)


def body(
    inputs, seq_lens, pass_idx, pass_table, gain_attn, w_qkv, w_out, gain_mlp, w_up, w_down, cotangent,
):
    _, rows, width = inputs.shape
    inputs2 = inputs[0]
    out_cot = cotangent[0]
    gather = functools.partial(lax.all_gather, axis_name="shard", tiled=True)
    table = gather(pass_table, axis=1)
    attn_gain = jnp.broadcast_to(gather(gain_attn, axis=0).astype(F32)[None, :], (8, width))
    mlp_gain = jnp.broadcast_to(gather(gain_mlp, axis=0).astype(F32)[None, :], (8, width))
    qkv_w = gather(w_qkv, axis=0)
    out_w = gather(w_out, axis=0)
    up_w = gather(w_up, axis=0)
    down_w = gather(w_down, axis=0)
    chosen = (pass_idx[:, None] == jnp.arange(table.shape[0], dtype=jnp.int32)[None, :]).astype(F32)
    pass_row = jnp.broadcast_to(
        jnp.sum(chosen[0][:, None] * table.astype(F32), axis=0, keepdims=True), (8, width)
    )
    block = 256
    tile = 512
    joined, attended, sums, hidden = call(
        functools.partial(front_kernel, block, tile),
        [((rows, 3 * width), BF16), ((rows, width), BF16), ((HEADS // 2, rows, PAIR), F32), ((rows, width), F32)],
        [((rows, width), BF16), ((rows, PAIR), BF16)],
        seq_lens, inputs2, pass_row, attn_gain, qkv_w, out_w, scalars=1,
    )
    chunk = 1024
    outputs, hidden_grad, mlp_gain_grad, up_grad, down_grad = call(
        functools.partial(mlp_kernel, tile, chunk),
        [((rows, width), BF16), ((rows, width), F32), ((8, width), F32), (up_w.shape, BF16), (down_w.shape, BF16)],
        [((rows, width), BF16), ((rows, width), F32), ((rows, width), F32), ((rows, chunk), BF16), ((rows, chunk), BF16)],
        hidden, out_cot, mlp_gain, up_w, down_w,
    )
    log_rows = jnp.stack([sums[:, :, 0], sums[:, :, HEAD_DIM]], axis=1).reshape(HEADS, rows)
    grad_input, attn_gain_grad, table_row, qkv_grad, out_grad = call(
        functools.partial(back_kernel, block, tile),
        [((rows, width), F32), ((8, width), F32), ((8, width), F32), (qkv_w.shape, BF16), (out_w.shape, BF16)],
        [((rows, width), BF16), ((rows, width), BF16), ((rows, width), BF16), ((rows, 3 * width), BF16),
         ((rows, PAIR), BF16), ((rows, PAIR), F32), ((rows, PAIR), F32)],
        seq_lens, inputs2, pass_row, attn_gain, qkv_w, out_w, joined, log_rows, attended, hidden_grad, scalars=1,
    )
    scatter = lambda grad, dim=0: lax.psum_scatter(grad, "shard", scatter_dimension=dim, tiled=True)
    up_part, down_part = scatter(up_grad), scatter(down_grad)
    out_part, qkv_part = scatter(out_grad), scatter(qkv_grad)
    small = jnp.concatenate(
        [chosen[0][:, None] * table_row[0:1], attn_gain_grad[0:1], mlp_gain_grad[0:1]], axis=0
    )
    small = lax.psum(scatter(small, 1), "rep")
    up_sum, down_sum, out_sum, qkv_sum = lax.psum((up_part, down_part, out_part, qkv_part), "rep")
    count = table.shape[0]
    return (
        outputs[None], grad_input[None], small[:count], small[count], qkv_sum.astype(F32), out_sum.astype(F32),
        small[count + 1], up_sum.astype(F32), down_sum.astype(F32),
    )


def solution(mesh):
    part = P(("shard", "rep"), None, None)
    return jax.shard_map(
        body,
        mesh=mesh,
        in_specs=(
            part, P(("shard", "rep")), P(("shard", "rep")), P(None, "shard"), P("shard"), P("shard", None),
            P("shard", None), P("shard"), P("shard", None), P("shard", None), part,
        ),
        out_specs=(
            part, part, P(None, "shard"), P("shard"), P("shard", None), P("shard", None), P("shard"),
            P("shard", None), P("shard", None),
        ),
        check_vma=False,
    )
```

time: 738 us -> 587 us (0.80)
  matrix products: 200 us -> 0 us
  Pallas kernels: 0 us -> 134 us
  other arithmetic: 62.3 us -> 7.18 us
  local copies, waits for them, and re-layouts: 52.9 us -> 16.1 us
  waiting for transfers between devices: 340 us -> 376 us
  blocking collectives: 49 us -> 36.3 us
  loops' own time: 10.9 us -> 0 us
    dot_general x55 -> x0, matrix products: 200 us -> none  [the longest x6 32.4 us: one_group(): jnp.einsum('qhd,khd->hqk', grad_part, value_part, preferred_element_type=...]
    pallas_call x0 -> x3, Pallas kernels: none -> 134 us  [call(): pl.pallas_call(kernel, out_shape=[jax.ShapeDtypeStruct(shape, kind) for s...]
    psum x1, waiting for transfers between devices: 123 us -> 64.8 us  [body(): lax.psum((up_part, down_part, out_part, qkv_part), 'rep')]
    all_gather x4, waiting for transfers between devices: 20.8 us -> 72.2 us  [the longest x1 39.8 us: body(): down_w = gather(w_down, axis=0)]
    unnamed x11, waiting for transfers between devices: 10.3 us -> 42.1 us
    unnamed x96 -> x17, local copies, waits for them, and re-layouts: 29.9 us -> 5.25 us
    reduce_sum x9 -> x1, other arithmetic: 20.6 us -> 0.08 us  [body(): jnp.sum(chosen[0][:, None] * table.astype(F32), axis=0, keepdims=True)]
    convert_element_type x6, other arithmetic: 26.2 us -> 6.96 us  [the longest x1 2.18 us: body(): up_sum.astype(F32)]
  transfers between devices with their start and end apart: 10 -> 10, of which waited for: 7 -> 8; matrix products, arithmetic and copies ran while one was open for 37% -> 3% of each run, Pallas kernels for 0% -> 6%
where the time goes in v1:
time: 587 us; the launch traced here: 586 us
  waiting for transfers between devices  376 us (64%)
  Pallas kernels  134 us (23%)
  blocking collectives  36.3 us (6%)
  between operations  16.2 us (3%)
  local copies, waits for them, and re-layouts  16.1 us (3%)
  other arithmetic  7.18 us (1%)
    reduce_scatter x4, waiting for transfers between devices, body(): lax.psum_scatter(grad, 'shard', scatter_dimension=dim, tiled=True)  197 us
    pallas_call x3, Pallas kernels, call(): pl.pallas_call(kernel, out_shape=[jax.ShapeDtypeStruct(shape, kind) for s...  134 us
    psum x1, waiting for transfers between devices, body(): lax.psum((up_part, down_part, out_part, qkv_part), 'rep')  64.8 us
    unnamed x11, waiting for transfers between devices  42.1 us
    all_gather x1, waiting for transfers between devices, body(): down_w = gather(w_down, axis=0)  39.8 us
    all_gather x1, waiting for transfers between devices, body(): qkv_w = gather(w_qkv, axis=0)  32.4 us
    unnamed x1, blocking collectives  13.9 us
    psum x1, blocking collectives, body(): small = lax.psum(scatter(small, 1), 'rep')  11.9 us
  transfers between devices with their start and end apart: 10, of which 8 were waited for; matrix products, arithmetic and copies ran while one was open for 3% of the time, Pallas kernels for 6%

profile of v1, /device:TPU:0, one launch (start us, length us, event | category | flops | bytes accessed | tf_op | source)
XLA Modules:
  0.0 586.3 jit_solution(16534963001749181365)
XLA Ops:
  7.2 0.7 all-gather.8.cloned.1.call-update
  7.9 0.0 all-gather.6.cloned.1.call-start
  8.0 0.7 all-gather.6.cloned.1.call-update
  8.7 0.7 all-gather.10.cloned.1.call-update
  9.4 0.5 all-gather.12.cloned.1.call-update
  10.0 0.0 reduce-scatter.10.cloned.1.call-start
  11.3 10.5 %all-gather = bf16[8,96,5]{1,2,0:T(8,128)(2,1)S(1)} all-gather(bf16[1,96,5]{1,2,0:T(8,128)(2,1)} %bitcast.25), channel_id=1, replica_groups=mesh['shard'=8,'rep'=4] {'shard'}, dimensions={0}, use_global_device_ids=true | all-gather | bytes 8640 | tf_op jit(solution)/shard_map/all_gather | solution.py:303
  21.9 0.1 reshape.48
  21.9 1.2 dynamic-slice
  23.8 0.8 dynamic-update-slice
  24.7 0.8 dynamic-update-slice.1
  25.5 13.9 %all-reduce.2 = (bf16[768]{0:T(1024)(128)(2,1)S(1)}, bf16[768]{0:T(1024)(128)(2,1)}) all-reduce(bf16[768]{0:T(1024)(128)(2,1)S(1)} %dynamic-update-slice, bf16[768]{0:T(1024)(128)(2,1)S(1)} %dynamic-update-slice.1), channel_id=1, replica_groups=mesh['shard'=8,'rep'=4] {'shard'}, use_global_device_ids=true, to_apply=%add | all-reduce | flops 1536 | bytes 6144
  39.4 0.5 copy-done.2
  39.9 0.1 multiply_reduce_fusion
  40.0 32.4 %all-gather.6.cloned.1.call-done.w_qkv = bf16[768,2304]{1,0:T(8,128)(2,1)} async-done(((bf16[96,2304]{1,0:T(8,128)(2,1)}), bf16[768,2304]{1,0:T(8,128)(2,1)}) %all-gather.6.cloned.1.call-update) | async-done | bytes 3538960 | tf_op jit(solution)/shard_map/all_gather | solution.py:306
  72.4 0.6 broadcast_in_dim.10.pass_row
  73.0 0.6 broadcast_in_dim.11.gain
  73.6 34.0 %shard_map.178 = (bf16[1024,2304]{1,0:T(8,128)(2,1)}, bf16[1024,768]{1,0:T(8,128)(2,1)}, f32[6,1024,128]{2,1,0:T(8,128)}, f32[1024,768]{1,0:T(8,128)}) custom-call(s32[1]{0:T(128)S(6)} %copy.37.length_ref, bf16[1024,768]{1,0:T(8,128)(2,1)} %bitcast.19, f32[8,768]{1,0:T(8,128)} %broadcast_in_dim.10.pass_row, f32[8,768]{1,0:T(8,128)} %broadcast_in_dim.11.gain, ...), custom_call_target="tpu_custom_call" | custom-call | tf_op jit(solution)/shard_map/pallas_call | solution.py:286
  107.7 5.4 slice_reduce_fusion.1
  113.2 0.7 reshape.35.log_rows
  113.9 39.8 %all-gather.12.cloned.1.call-done.w_down = bf16[3072,768]{1,0:T(8,128)(2,1)} async-done(((bf16[384,768]{1,0:T(8,128)(2,1)}), bf16[3072,768]{1,0:T(8,128)(2,1)}) %all-gather.12.cloned.1.call-update) | async-done | bytes 4718608 | tf_op jit(solution)/shard_map/all_gather | solution.py:309
  153.7 0.6 broadcast_in_dim.12.gain
  154.3 47.4 %shard_map.179 = (bf16[1024,768]{1,0:T(8,128)(2,1)}, f32[1024,768]{1,0:T(8,128)}, f32[8,768]{1,0:T(8,128)}, bf16[768,3072]{1,0:T(8,128)(2,1)}, bf16[3072,768]{1,0:T(8,128)(2,1)}) custom-call(f32[1024,768]{1,0:T(8,128)} %get-tuple-element.23.hidden, bf16[1024,768]{1,0:T(8,128)(2,1)} %bitcast.22, f32[8,768]{1,0:T(8,128)} %broadcast_in_dim.12.gain, ...), custom_call_target="tpu_custom_call" | custom-call | tf_op jit(solution)/shard_map/pallas_call | solution.py:286
  201.7 52.4 %shard_map.180 = (f32[1024,768]{1,0:T(8,128)}, f32[8,768]{1,0:T(8,128)}, f32[8,768]{1,0:T(8,128)}, bf16[768,2304]{1,0:T(8,128)(2,1)}, bf16[768,768]{1,0:T(8,128)(2,1)}) custom-call(s32[1]{0:T(128)S(6)} %copy.37.length_ref, bf16[1024,768]{1,0:T(8,128)(2,1)} %bitcast.20, f32[8,768]{1,0:T(8,128)} %broadcast_in_dim.10.pass_row, f32[8,768]{1,0:T(8,128)} %broadcast_in_dim.11.gain, ...), custom_call_target="tpu_custom_call" | custom-call | tf_op jit(solution)/shard_map/pallas_call | solution.py:286
  254.2 0.0 reduce-scatter.8.cloned.1.call-start
  254.2 0.5 reduce-scatter.8.cloned.1.call-update
  254.8 0.7 reduce-scatter.12.cloned.1.call-update
  255.5 0.7 reduce-scatter.14.cloned.1.call-update
  256.2 0.0 reduce-scatter.16.cloned.1.call-start
  256.3 0.7 slice.27
  257.0 0.7 slice.28
  257.8 0.8 slice_reduce_fusion.2
  258.5 0.1 broadcast_multiply_fusion
  258.6 0.9 copy.28
  259.6 0.0 all-reduce.6.cloned.1.call-start
  259.6 31.3 %reduce-scatter.10.cloned.1.call-done = bf16[96,768]{1,0:T(8,128)(2,1)} async-done(((bf16[768,768]{1,0:T(8,128)(2,1)}), bf16[96,768]{1,0:T(8,128)(2,1)}) %reduce-scatter.10.cloned.1.call-update) | async-done | bytes 147472 | tf_op jit(solution)/shard_map/reduce_scatter | solution.py:337
  291.0 51.3 %reduce-scatter.8.cloned.1.call-done = bf16[96,2304]{1,0:T(8,128)(2,1)} async-done(((bf16[768,2304]{1,0:T(8,128)(2,1)}), bf16[96,2304]{1,0:T(8,128)(2,1)}) %reduce-scatter.8.cloned.1.call-update) | async-done | bytes 442384 | tf_op jit(solution)/shard_map/reduce_scatter | solution.py:337
  342.3 57.2 %reduce-scatter.12.cloned.1.call-done = bf16[96,3072]{1,0:T(8,128)(2,1)} async-done(((bf16[768,3072]{1,0:T(8,128)(2,1)}), bf16[96,3072]{1,0:T(8,128)(2,1)}) %reduce-scatter.12.cloned.1.call-update) | async-done | bytes 589840 | tf_op jit(solution)/shard_map/reduce_scatter | solution.py:337
  399.6 57.3 %reduce-scatter.14.cloned.1.call-done = bf16[384,768]{1,0:T(8,128)(2,1)} async-done(((bf16[3072,768]{1,0:T(8,128)(2,1)}), bf16[384,768]{1,0:T(8,128)(2,1)}) %reduce-scatter.14.cloned.1.call-update) | async-done | bytes 589840 | tf_op jit(solution)/shard_map/reduce_scatter | solution.py:337
  456.8 37.5 %reduce-scatter.16.cloned.1.call-done = f32[96,7]{1,0:T(8,128)} async-done(((f32[768,7]{1,0:T(8,128)}), f32[96,7]{1,0:T(8,128)}) %reduce-scatter.16.cloned.1.call-update) | async-done | bytes 2704
  494.4 0.9 copy.29
  495.3 11.9 %psum.35 = f32[7,96]{1,0:T(8,128)S(1)} all-reduce(f32[7,96]{1,0:T(8,128)S(1)} %copy.29), channel_id=1, replica_groups=mesh['shard'=8,'rep'=4] {'rep'}, use_global_device_ids=true, to_apply=%region_2.0 | all-reduce | flops 672 | bytes 5376 | tf_op jit(solution)/shard_map/psum | solution.py:343
  507.1 0.5 slice_bitcast_fusion
  507.7 64.8 %all-reduce.6.cloned.1.call-done = (bf16[96,2304]{1,0:T(8,128)(2,1)}, bf16[96,768]{1,0:T(8,128)(2,1)}, bf16[96,3072]{1,0:T(8,128)(2,1)}, bf16[384,768]{1,0:T(8,128)(2,1)}) async-done(((bf16[96,2304]{1,0:T(8,128)(2,1)}, bf16[96,768]{1,0:T(8,128)(2,1)}, bf16[96,3072]{1,0:T(8,128)(2,1)}, bf16[384,768]{1,0:T(8,128)(2,1)}), (bf16[96,2304]{1,0:T(8,128)(2,1)}, bf16[96,768]{1,0:T(8,128)(2,1)}, ...) | async-done | bytes 1769488 | tf_op jit(solution)/shard_map/psum | solution.py:344
  572.5 1.7 convert_element_type.35
  574.2 2.0 convert_element_type.34
  576.2 2.2 convert_element_type.36
  578.3 1.1 convert_element_type.37
  (27 shorter events, 0.4 us)
Async XLA Ops:
  7.2 32.9 %all-gather.8.cloned.1.call-start = ((), (), s32[]{:S(2)}) async-start(), calls=%async_computation.6 | async-start | bytes 1327104 | tf_op jit(solution)/shard_map/all_gather | solution.py:307
  7.9 64.5 %all-gather.6.cloned.1.call-start = ((), (), s32[]{:S(2)}) async-start(), calls=%async_computation.5 | async-start | bytes 3981312 | tf_op jit(solution)/shard_map/all_gather | solution.py:306
  8.7 105.2 %all-gather.10.cloned.1.call-start = ((), (), s32[]{:S(2)}) async-start(), calls=%async_computation.7 | async-start | bytes 5308416 | tf_op jit(solution)/shard_map/all_gather | solution.py:308
  9.4 144.3 %all-gather.12.cloned.1.call-start = ((), (), s32[]{:S(2)}) async-start(), calls=%async_computation.8 | async-start | bytes 5308416 | tf_op jit(solution)/shard_map/all_gather | solution.py:309
  10.0 281.0 %reduce-scatter.10.cloned.1.call-start = ((), (), s32[]{:S(2)}) async-start(), calls=%async_computation.10 | async-start | bytes 1327104 | tf_op jit(solution)/shard_map/reduce_scatter | solution.py:337
  39.4 0.5 copy-start.2
  107.6 46.0 %copy-start.4 = (bf16[768]{0:T(1024)(128)(2,1)S(1)}, bf16[768]{0:T(1024)(128)(2,1)}, u32[]{:S(2)}) copy-start(bf16[768]{0:T(1024)(128)(2,1)} %get-tuple-element.40) | copy-start | bytes 4612
  254.2 88.2 %reduce-scatter.8.cloned.1.call-start = ((), (), s32[]{:S(2)}) async-start(), calls=%async_computation.9 | async-start | bytes 3981312 | tf_op jit(solution)/shard_map/reduce_scatter | solution.py:337
  254.7 144.8 %reduce-scatter.12.cloned.1.call-start = ((), (), s32[]{:S(2)}) async-start(), calls=%async_computation.11 | async-start | bytes 5308416 | tf_op jit(solution)/shard_map/reduce_scatter | solution.py:337
  255.5 3.0 copy-start.3
  255.5 201.3 %reduce-scatter.14.cloned.1.call-start = ((), (), s32[]{:S(2)}) async-start(), calls=%async_computation.12 | async-start | bytes 5308416 | tf_op jit(solution)/shard_map/reduce_scatter | solution.py:337
  256.2 238.1 %reduce-scatter.16.cloned.1.call-start = ((), (), s32[]{:S(2)}) async-start(), calls=%async_computation.13 | async-start | bytes 442368
  259.6 312.9 %all-reduce.6.cloned.1.call-start = ((), (), s32[]{:S(2)}) async-start(), calls=%async_computation.14 | async-start | bytes 3538944 | tf_op jit(solution)/shard_map/psum | solution.py:344
  507.1 72.3 %copy-start.1 = (f32[7,96]{1,0:T(8,128)}, f32[7,96]{1,0:T(8,128)S(1)}, u32[]{:S(2)}) copy-start(f32[7,96]{1,0:T(8,128)S(1)} %psum.35) | copy-start | bytes 8068
  572.5 5.9 %copy-start = (bf16[384,768]{1,0:T(8,128)(2,1)S(1)}, bf16[384,768]{1,0:T(8,128)(2,1)}, u32[]{:S(2)}) copy-start(bf16[384,768]{1,0:T(8,128)(2,1)} %get-tuple-element.44) | copy-start | bytes 1769476
Sparse Core Ops, SparseCore 0:
  9.9 26.7 all-gather.7
  38.5 33.8 all-gather.5
  74.3 38.7 all-gather.9
  114.8 38.8 all-gather.11
  254.3 36.6 reduce-scatter.9
  294.3 47.9 reduce-scatter.7
  345.8 53.7 reduce-scatter.11
  403.0 53.7 reduce-scatter.13
  460.5 33.8 reduce-scatter.15
  496.9 75.5 all-reduce.5

commit v2 on v1

--- a/solution.py
+++ b/solution.py
@@ -349,10 +349,944 @@
     )
 
 
+MESH = pl.DeviceIdType.MESH
+
+
+class Place:
+    def __init__(self):
+        self.me = lax.axis_index("shard")
+        self.z = lax.axis_index("rep")
+        self.core = lax.rem(self.me, 2)
+        self.x = lax.rem(self.me // 2, 2)
+        self.y = self.me // 4
+        self.by_x = self.me + 2 - 4 * self.x
+        self.by_y = self.me + 4 - 8 * self.y
+        self.by_core = self.me + 1 - 2 * self.core
+        self.by_both = self.by_x + 4 - 8 * self.y
+
+    def at(self, shard):
+        return (shard, self.z)
+
+
+def remote(src, dst, sends, recvs, index, device):
+    return pltpu.make_async_remote_copy(
+        src_ref=src, dst_ref=dst, send_sem=sends.at[index], recv_sem=recvs.at[index],
+        device_id=device, device_id_type=MESH,
+    )
+
+
+class Gather:
+    def __init__(self, place, own, block_of, half_of, sends, recvs, local, row):
+        self.place, self.own, self.block, self.half = place, own, block_of, half_of
+        self.sends, self.recvs, self.local, self.row = sends, recvs, local, row
+
+    def copy(self, slot, src, dst, shard):
+        return remote(src, dst, self.sends, self.recvs, (self.row, slot), self.place.at(shard))
+
+    def same(self, slot, ref, shard):
+        return self.copy(slot, ref, ref, shard)
+
+    def make(self, slot):
+        p, block, half = self.place, self.block, self.half
+        if slot < 3:
+            return self.copy(slot, self.own, block(p.me), (p.by_x, p.by_y, p.by_core)[slot])
+        if slot == 3:
+            return self.same(slot, half(p.by_x, 0), p.by_y)
+        if slot == 4:
+            return self.same(slot, half(p.by_y, 1), p.by_x)
+        if slot < 7:
+            return self.same(slot, block(p.by_x if slot == 5 else p.by_y), p.by_core)
+        return self.same(slot, half(p.by_both, slot - 7), p.by_core)
+
+    def here(self):
+        return pltpu.make_async_copy(self.own, self.block(self.place.me), self.local.at[self.row])
+
+    def start(self):
+        for slot in range(3):
+            self.make(slot).start()
+        self.here().start()
+
+    def relay(self):
+        self.make(0).wait_recv()
+        self.make(3).start()
+        self.make(5).start()
+        self.make(1).wait_recv()
+        self.make(4).start()
+        self.make(6).start()
+
+    def finish(self):
+        self.make(3).wait_recv()
+        self.make(7).start()
+        self.make(4).wait_recv()
+        self.make(8).start()
+
+    def ready(self):
+        for slot in (2, 5, 6, 7, 8):
+            self.make(slot).wait_recv()
+        self.here().wait()
+
+    def drain(self):
+        for slot in range(9):
+            self.make(slot).wait_send()
+
+
+def enter(place, shards, reps=()):
+    barrier = pltpu.get_barrier_semaphore()
+    for shard in shards:
+        pl.semaphore_signal(barrier, inc=1, device_id=(shard, place.z), device_id_type=MESH)
+    for rep in reps:
+        pl.semaphore_signal(barrier, inc=1, device_id=(place.me, rep), device_id_type=MESH)
+    pl.semaphore_wait(barrier, len(shards) + len(reps))
+
+
+def rows_block(ref, rows, lead=(), columns=slice(None)):
+    def block(shard):
+        return ref.at[lead + (pl.ds(pl.multiple_of(shard * rows, rows), rows), columns)]
+
+    def half(shard, part):
+        start = pl.multiple_of(shard * rows + part * (rows // 2), rows // 2)
+        return ref.at[lead + (pl.ds(start, rows // 2), columns)]
+
+    return block, half
+
+
+def attention_rows(joined, attended, log_rows, key_bias, pair, block):
+    rows = attended.shape[0]
+    columns = pl.ds(pl.multiple_of(pair * PAIR, PAIR), PAIR)
+    keys = joined[1, :, columns]
+    values = joined[2, :, columns]
+    bias = key_bias[...]
+    biased = [key_with_bias(keys, bias, head)[0] for head in range(2)]
+    for first in range(0, rows, block):
+        live = first + block
+        query = joined[0, pl.ds(first, block), columns]
+        mixed = []
+        sums = []
+        for head in range(2):
+            asked, _ = query_with_bias(query, head)
+            scores = mm(asked, biased[head][:live], NT)
+            row_at = lax.broadcasted_iota(jnp.int32, (block, block), 0)
+            key_at = lax.broadcasted_iota(jnp.int32, (block, block), 1)
+            last = jnp.where(key_at <= row_at, scores[:, first:], MASKED)
+            scores = last if first == 0 else jnp.concatenate([scores[:, :first], last], axis=1)
+            top = jnp.max(scores, axis=-1, keepdims=True)
+            weights = jnp.exp(scores - top)
+            total = jnp.sum(weights, axis=-1, keepdims=True)
+            mixed.append(mm(weights.astype(BF16), values[:live]) / total)
+            sums.append(top + jnp.log(total))
+        lanes = lanes_of(mixed[0].shape)
+        attended[pl.ds(first, block), columns] = jnp.where(lanes < HEAD_DIM, mixed[0], mixed[1]).astype(BF16)
+        turned = jnp.transpose(jnp.where(lanes < HEAD_DIM, sums[0], sums[1]))
+        log_rows[pl.ds(pair * 2, 1), pl.ds(first, block)] = turned[0:1]
+        log_rows[pl.ds(pair * 2 + 1, 1), pl.ds(first, block)] = turned[HEAD_DIM : HEAD_DIM + 1]
+
+
+def norm_rows(inputs, pass_row, gain, normed):
+    @pl.loop(0, inputs.shape[0] // 256)
+    def _(step):
+        at = pl.ds(step * 256, 256)
+        entered = inputs[at, :].astype(F32) + pass_row
+        normed[at, :] = (norm_parts(entered)[0] * gain).astype(BF16)
+
+
+def front_comm_kernel(
+    ahead, block, tile, group,
+    length_ref, pass_ref, inputs, small_own, qkv_own, out_own, up_own, down_own,
+    rows_out, log_out, joined_out, attended_out, hidden_out, qkv_out, out_out, up_out, down_out,
+    slots, normed, joined, attended, hidden, qkv_w, out_w, key_bias,
+    sends, recvs, local, small_sends, small_recvs, saves,
+):
+    place = Place()
+    rows, width = inputs.shape
+    shards = slots.shape[0]
+    part = qkv_own.shape[1]
+    groups = width // group
+    others = [lax.rem(place.me + shift, shards) for shift in range(1, shards)]
+    enter(place, others)
+
+    smalls = [
+        remote(small_own, slots.at[place.me], small_sends, small_recvs, shift, place.at(other))
+        for shift, other in enumerate(others)
+    ]
+    for copy in smalls:
+        copy.start()
+    mine = pltpu.make_async_copy(small_own, slots.at[place.me], small_sends.at[shards - 1])
+    mine.start()
+
+    pieces = []
+
+    def add(own, block_of, half_of):
+        pieces.append(Gather(place, own, block_of, half_of, sends, recvs, local, len(pieces)))
+
+    for index in range(groups):
+        columns = pl.ds(index * group, group)
+        add(qkv_own.at[:, :, columns], *rows_block(qkv_w, part, (slice(None),), columns))
+    add(out_own, *rows_block(out_w, part))
+    for index in range(ahead):
+        add(up_own.at[index], *rows_block(up_out, part, (index,)))
+        add(down_own.at[index], *rows_block(down_out, down_own.shape[1], (index,)))
+    count = len(pieces)
+
+    def tick(index):
+        if index + 2 < count:
+            pieces[index + 2].start()
+        if index < count:
+            pieces[index].relay()
+        if 0 <= index - 1 < count:
+            pieces[index - 1].finish()
+
+    pieces[0].start()
+    pieces[1].start()
+    fill_bias(length_ref[0], key_bias)
+    mine.wait()
+    for copy in smalls:
+        copy.wait_recv()
+    total = slots[0].astype(F32)
+    for shard in range(1, shards):
+        total = total + slots[shard].astype(F32)
+    places = lax.broadcasted_iota(jnp.int32, total.shape, 0)
+    pass_row = jnp.sum(jnp.where(places == pass_ref[0], total, 0.0), axis=0, keepdims=True)
+    rows_out[0:1, :] = pass_row
+    rows_out[1:3, :] = total[8:10]
+    rows_out[3:8, :] = jnp.zeros((5, width), F32)
+
+    tick(0)
+    norm_rows(inputs, rows_out[0:1, :], rows_out[1:2, :], normed)
+    tick(1)
+
+    def save(source, target, index):
+        return pltpu.make_async_copy(source, target, saves.at[index])
+
+    pairs = width // PAIR
+    per_group = group // PAIR
+
+    @pl.loop(0, pairs)
+    def _(pair):
+        for index in range(groups):
+            @pl.when(pair == index * per_group)
+            def _(index=index):
+                pieces[index].ready()
+
+        @pl.when(lax.rem(pair, per_group) == 0)
+        def _():
+            columns = pl.ds(pl.multiple_of(pair * PAIR, group), group)
+
+            @pl.loop(0, 3)
+            def _(plane):
+                joined[plane, :, columns] = mm(normed[...], qkv_w[plane, :, columns]).astype(BF16)
+
+        attention_rows(joined, attended, log_out, key_bias, pair, block)
+        for index in range(pairs):
+            @pl.when(pair == index)
+            def _(index=index):
+                tick(index + 2)
+
+    keep = [
+        save(joined, joined_out, 0), save(attended, attended_out, 1), save(qkv_w, qkv_out, 2),
+    ]
+    for copy in keep:
+        copy.start()
+    pieces[groups].ready()
+    keep.append(save(out_w, out_out, 3))
+    keep[-1].start()
+
+    @pl.loop(0, rows // tile)
+    def _(step):
+        at = pl.ds(step * tile, tile)
+        entered = inputs[at, :].astype(F32) + rows_out[0:1, :]
+        hidden[at, :] = entered + mm(attended[at, :], out_w[...])
+
+    keep.append(save(hidden, hidden_out, 4))
+    keep[-1].start()
+    for index in range(pairs + 2, count + 1):
+        tick(index)
+    for piece in pieces[groups + 1 :]:
+        piece.ready()
+    for piece in pieces:
+        piece.drain()
+    for copy in smalls:
+        copy.wait_send()
+    for copy in keep:
+        copy.wait()
+
+
+def any_spec(count):
+    return [pl.BlockSpec(memory_space=pl.ANY)] * count
+
+
+def smem_spec(count):
+    return [pl.BlockSpec(memory_space=pltpu.SMEM)] * count
+
+
+def vmem_spec(count):
+    return [pl.BlockSpec(memory_space=pltpu.VMEM)] * count
+
+
+def shaped(shape, kind):
+    return jax.ShapeDtypeStruct(shape, kind)
+
+
+def front_comm(ahead, seq_lens, pass_idx, inputs, small, qkv, out, up, down):
+    rows, width = inputs.shape
+    shards = width // out.shape[0]
+    chunk = up.shape[2]
+    group = 4 * HEAD_DIM
+    count = width // group + 1 + 2 * ahead
+    return pl.pallas_call(
+        functools.partial(front_comm_kernel, ahead, 256, 512, group),
+        out_shape=[
+            shaped((8, width), F32), shaped((16, rows), F32), shaped((3, rows, width), BF16),
+            shaped((rows, width), BF16), shaped((rows, width), F32), shaped((3, width, width), BF16),
+            shaped((width, width), BF16), shaped((ahead, width, chunk), BF16), shaped((ahead, chunk, width), BF16),
+        ],
+        in_specs=smem_spec(2) + vmem_spec(1) + any_spec(5),
+        out_specs=vmem_spec(2) + any_spec(7),
+        scratch_shapes=[
+            pltpu.VMEM((shards,) + small.shape, BF16), pltpu.VMEM((rows, width), BF16),
+            pltpu.VMEM((3, rows, width), BF16), pltpu.VMEM((rows, width), BF16), pltpu.VMEM((rows, width), F32),
+            pltpu.VMEM((3, width, width), BF16), pltpu.VMEM((width, width), BF16), pltpu.VMEM((rows, PAIR), BF16),
+            pltpu.SemaphoreType.DMA((count, 9)), pltpu.SemaphoreType.DMA((count, 9)), pltpu.SemaphoreType.DMA((count,)),
+            pltpu.SemaphoreType.DMA((shards,)), pltpu.SemaphoreType.DMA((shards,)), pltpu.SemaphoreType.DMA((5,)),
+        ],
+        compiler_params=pltpu.CompilerParams(
+            vmem_limit_bytes=VMEM_LIMIT, collective_id=1, has_side_effects=True
+        ),
+    )(seq_lens, pass_idx, inputs, small, qkv, out, up, down)
+
+
+class Scatter:
+    def __init__(self, place, grads, first, by_x, by_y, last, sends, recvs, row):
+        self.place, self.grads, self.first = place, grads, first
+        self.in_x, self.in_y, self.last = by_x, by_y, last
+        self.sends, self.recvs, self.row = sends, recvs, row
+        half = first.shape[-1] // 2
+        self.left, self.right = pl.ds(0, half), pl.ds(half, half)
+
+    def copy(self, slot, src, dst, shard):
+        return remote(src, dst, self.sends, self.recvs, (self.row, slot), self.place.at(shard))
+
+    def swap_copy(self):
+        p = self.place
+        return self.copy(0, self.grads.at[:, :, 1 - p.core], self.first, p.by_core)
+
+    def spread_copies(self):
+        p = self.place
+        return [
+            self.copy(1, self.first.at[:, 1 - p.x, :, self.left], self.in_x, p.by_x),
+            self.copy(2, self.first.at[1 - p.y, :, :, self.right], self.in_y, p.by_y),
+        ]
+
+    def fold_copies(self):
+        p = self.place
+        return [
+            self.copy(3, self.in_x.at[1 - p.y], self.last.at[:, self.left], p.by_y),
+            self.copy(4, self.in_y.at[1 - p.x], self.last.at[:, self.right], p.by_x),
+        ]
+
+    def swap(self):
+        self.swap_copy().start()
+
+    def merge(self, target=None):
+        p = self.place
+        target = self.first if target is None else target
+        self.swap_copy().wait_recv()
+        for y in range(2):
+            for x in range(2):
+                total = self.grads[y, x, p.core].astype(F32) + self.first[y, x].astype(F32)
+                target[y, x] = total.astype(BF16)
+
+    def spread(self):
+        for copy in self.spread_copies():
+            copy.start()
+
+    def fold(self):
+        p = self.place
+        for copy in self.spread_copies():
+            copy.wait_recv()
+        for other in range(2):
+            total = self.first[other, p.x, :, self.left].astype(F32) + self.in_x[other].astype(F32)
+            self.in_x[other] = total.astype(BF16)
+            total = self.first[p.y, other, :, self.right].astype(F32) + self.in_y[other].astype(F32)
+            self.in_y[other] = total.astype(BF16)
+        for copy in self.fold_copies():
+            copy.start()
+
+    def close(self, target):
+        p = self.place
+        for copy in self.fold_copies():
+            copy.wait_recv()
+        target[:, self.left] = (self.last[:, self.left].astype(F32) + self.in_x[p.y].astype(F32)).astype(BF16)
+        target[:, self.right] = (self.last[:, self.right].astype(F32) + self.in_y[p.x].astype(F32)).astype(BF16)
+
+    def drain(self, swapped=True, spread=True):
+        if swapped:
+            self.swap_copy().wait_send()
+        if spread:
+            for copy in self.spread_copies() + self.fold_copies():
+                copy.wait_send()
+
+
+def mlp_comm_kernel(
+    ahead, tile,
+    hidden, cotangent, rows_in, up_have, down_have, up_own, down_own,
+    outputs, hidden_grad, gain_grad, up_done, down_done, up_half, down_half,
+    up_w, down_w, second, mixed, active, rising_grad,
+    up_grads, up_first, up_x, up_y, up_last, down_grads, down_first, down_x, down_y, down_last,
+    gather_sends, gather_recvs, gather_local, up_sends, up_recvs, down_sends, down_recvs, loads,
+):
+    place = Place()
+    rows, width = hidden.shape
+    chunks, chunk = down_w.shape[0], down_w.shape[1]
+    enter(place, [place.by_x, place.by_y, place.by_core])
+    gain = rows_in[2:3, :]
+
+    pieces = []
+    for index in range(ahead, chunks):
+        for own, ref in ((up_own, up_w), (down_own, down_w)):
+            block, half = rows_block(ref, own.shape[1], (index,))
+            pieces.append(
+                Gather(place, own.at[index], block, half, gather_sends, gather_recvs, gather_local, len(pieces))
+            )
+    for piece in pieces:
+        piece.start()
+    have = []
+    for index in range(ahead):
+        for ref, weights in ((up_have, up_w), (down_have, down_w)):
+            have.append(pltpu.make_async_copy(ref.at[index], weights.at[index], loads.at[len(have)]))
+    for copy in have:
+        copy.start()
+
+    def up_message(index):
+        return Scatter(
+            place, up_grads.at[index], up_first.at[index], up_x.at[index], up_y.at[index], up_last.at[index],
+            up_sends, up_recvs, index,
+        )
+
+    def down_message(index):
+        return Scatter(
+            place, down_grads.at[index], down_first.at[index], down_x.at[index], down_y.at[index], down_last.at[index],
+            down_sends, down_recvs, index,
+        )
+
+    @pl.loop(0, rows // 256)
+    def _(step):
+        at = pl.ds(step * 256, 256)
+        second[at, :] = (norm_parts(hidden[at, :])[0] * gain).astype(BF16)
+        mixed[at, :] = hidden[at, :]
+        hidden_grad[at, :] = jnp.zeros((256, width), F32)
+
+    @pl.loop(0, chunks)
+    def _(part):
+        for index in range(ahead):
+            @pl.when(part == index)
+            def _(index=index):
+                have[2 * index].wait()
+                have[2 * index + 1].wait()
+        for index in range(ahead, chunks):
+            @pl.when(part == index)
+            def _(index=index):
+                pieces[2 * (index - ahead)].ready()
+                pieces[2 * (index - ahead) + 1].ready()
+
+        @pl.loop(0, rows // tile)
+        def _(step):
+            at = pl.ds(step * tile, tile)
+            rising = mm(second[at, :], up_w[part])
+            active_grad = mm(cotangent[at, :], down_w[part], NT)
+            bent, slope = gelu_both(rising)
+            shown = bent.astype(BF16)
+            moved = (slope * active_grad).astype(BF16)
+            active[at, :] = shown
+            rising_grad[at, :] = moved
+            mixed[at, :] += mm(shown, down_w[part])
+            hidden_grad[at, :] += mm(moved, up_w[part], NT)
+
+            @pl.when((part == 0) & (step == 0))
+            def _():
+                for piece in pieces[:2]:
+                    piece.relay()
+
+            @pl.when((part == 0) & (step == 1))
+            def _():
+                for piece in pieces[:2]:
+                    piece.finish()
+                for piece in pieces[2:]:
+                    piece.relay()
+
+            @pl.when((part > 0) & (step == 0))
+            def _():
+                message = up_message(part - 1)
+                message.merge()
+                message.spread()
+
+            @pl.when((part > 0) & (step == 1))
+            def _():
+                down_message(part - 1).fold()
+
+        down_grads[part] = mm(active[...], cotangent[...], TN).astype(BF16).reshape(down_grads.shape[1:])
+        down_message(part).swap()
+
+        @pl.when(part == 0)
+        def _():
+            for piece in pieces[2:]:
+                piece.finish()
+
+        @pl.when(part > 0)
+        def _():
+            up_message(part - 1).fold()
+
+        up_grads[part] = mm(second[...], rising_grad[...], TN).astype(BF16).reshape(up_grads.shape[1:])
+        up_message(part).swap()
+
+        @pl.when(part < chunks - 1)
+        def _():
+            message = down_message(part)
+            message.merge()
+            message.spread()
+
+        @pl.when(part > 0)
+        def _():
+            down_message(part - 1).close(down_done.at[part - 1])
+            up_message(part - 1).close(up_done.at[part - 1])
+
+    down_message(chunks - 1).merge(down_half)
+    gain_grad[...] = jnp.zeros_like(gain_grad)
+
+    @pl.loop(0, rows // 256)
+    def _(step):
+        at = pl.ds(step * 256, 256)
+        outputs[at, :] = mixed[at, :].astype(BF16)
+        unit, scale = norm_parts(hidden[at, :])
+        grad = hidden_grad[at, :]
+        hidden_grad[at, :] = cotangent[at, :].astype(F32) + norm_back(unit, scale, grad, gain)
+        gain_grad[0:1, :] += jnp.sum(grad * unit, axis=0, keepdims=True)
+
+    up_message(chunks - 1).merge(up_half)
+    for piece in pieces:
+        piece.drain()
+    for index in range(chunks):
+        up_message(index).drain(True, index < chunks - 1)
+        down_message(index).drain(True, index < chunks - 1)
+
+
+def scatter_scratch(count, part, columns):
+    return [
+        pltpu.VMEM((count, 2, 2, 2, part, columns), BF16), pltpu.VMEM((count, 2, 2, part, columns), BF16),
+        pltpu.VMEM((count, 2, part, columns // 2), BF16), pltpu.VMEM((count, 2, part, columns // 2), BF16),
+        pltpu.VMEM((count, part, columns), BF16),
+    ]
+
+
+def dma(*shapes):
+    return [pltpu.SemaphoreType.DMA(shape) for shape in shapes]
+
+
+def mlp_comm(ahead, hidden, cotangent, rows_in, up_have, down_have, up, down):
+    rows, width = hidden.shape
+    chunks, up_part, chunk = up.shape
+    down_part = down.shape[1]
+    late = 2 * (chunks - ahead)
+    return pl.pallas_call(
+        functools.partial(mlp_comm_kernel, ahead, 512),
+        out_shape=[
+            shaped((rows, width), BF16), shaped((rows, width), F32), shaped((8, width), F32),
+            shaped((chunks - 1, up_part, chunk), BF16), shaped((chunks - 1, down_part, width), BF16),
+            shaped((2, 2, up_part, chunk), BF16), shaped((2, 2, down_part, width), BF16),
+        ],
+        in_specs=vmem_spec(3) + any_spec(4),
+        out_specs=vmem_spec(7),
+        scratch_shapes=[
+            pltpu.VMEM((chunks, width, chunk), BF16), pltpu.VMEM((chunks, chunk, width), BF16),
+            pltpu.VMEM((rows, width), BF16), pltpu.VMEM((rows, width), F32),
+            pltpu.VMEM((rows, chunk), BF16), pltpu.VMEM((rows, chunk), BF16),
+        ]
+        + scatter_scratch(chunks, up_part, chunk)
+        + scatter_scratch(chunks, down_part, width)
+        + dma((late, 9), (late, 9), (late,), (chunks, 5), (chunks, 5), (chunks, 5), (chunks, 5), (2 * ahead,)),
+        compiler_params=pltpu.CompilerParams(
+            vmem_limit_bytes=VMEM_LIMIT, collective_id=2, has_side_effects=True
+        ),
+    )(hidden, cotangent, rows_in, up_have, down_have, up, down)
+
+
+class Column:
+    def __init__(self, place, block, inward, middle, outward, total, sends, recvs, row):
+        self.place, self.block, self.inward, self.middle = place, block, inward, middle
+        self.outward, self.total = outward, total
+        self.sends, self.recvs, self.row = sends, recvs, row
+        self.end = (place.z == 0) | (place.z == 3)
+
+    def copy(self, slot, src, dst, rep):
+        return remote(src, dst, self.sends, self.recvs, (self.row, slot), (self.place.me, rep))
+
+    def in_copy(self):
+        return self.copy(0, self.block, self.inward, 1 + self.place.z // 3)
+
+    def across_copy(self):
+        return self.copy(1, self.middle, self.outward, 3 - self.place.z)
+
+    def out_copy(self):
+        return self.copy(2, self.total, self.outward, 3 * (self.place.z - 1))
+
+    def begin(self):
+        @pl.when(self.end)
+        def _():
+            self.in_copy().start()
+
+    def cross(self):
+        @pl.when(jnp.logical_not(self.end))
+        def _():
+            self.in_copy().wait_recv()
+            self.middle[...] = (self.block[...].astype(F32) + self.inward[...].astype(F32)).astype(BF16)
+            self.across_copy().start()
+
+    def settle(self):
+        @pl.when(jnp.logical_not(self.end))
+        def _():
+            self.across_copy().wait_recv()
+            self.total[...] = (self.middle[...].astype(F32) + self.outward[...].astype(F32)).astype(BF16)
+            self.out_copy().start()
+
+    def finish(self):
+        @pl.when(self.end)
+        def _():
+            self.out_copy().wait_recv()
+            self.total[...] = self.outward[...]
+            self.in_copy().wait_send()
+
+        @pl.when(jnp.logical_not(self.end))
+        def _():
+            self.across_copy().wait_send()
+            self.out_copy().wait_send()
+
+
+def attention_columns(joined, log_rows, grads, joined_grad, key_bias, key_total, value_total, pair, block):
+    rows = grads.shape[0]
+    columns = pl.ds(pl.multiple_of(pair * PAIR, PAIR), PAIR)
+    keys = joined[1, :, columns]
+    values = joined[2, :, columns]
+    bias = key_bias[...]
+    biased = [key_with_bias(keys, bias, head) for head in range(2)]
+    key_total[...] = jnp.zeros_like(key_total)
+    value_total[...] = jnp.zeros_like(value_total)
+    for first in range(0, rows, block):
+        live = first + block
+        query = joined[0, pl.ds(first, block), columns]
+        grad = grads[pl.ds(first, block), columns]
+        query_grad = None
+        for head in range(2):
+            asked, asked_only = query_with_bias(query, head)
+            grad_only = head_only(grad, head)[0]
+            scores = mm(biased[head][0][:live], asked, NT)
+            share_grad = mm(values[:live], grad_only, NT)
+            log_sum = log_rows[pl.ds(pair * 2 + head, 1), pl.ds(first, block)]
+            shares = jnp.exp(scores - log_sum)
+            key_at = lax.broadcasted_iota(jnp.int32, (block, block), 0)
+            row_at = lax.broadcasted_iota(jnp.int32, (block, block), 1)
+            last = jnp.where(key_at <= row_at, shares[first:], 0.0)
+            shares = last if first == 0 else jnp.concatenate([shares[:first], last], axis=0)
+            inner = jnp.sum(share_grad * shares, axis=0, keepdims=True)
+            score_grad = (shares * (share_grad - inner)).astype(BF16)
+            value_total[:live, :] += mm(shares.astype(BF16), grad_only)
+            key_total[:live, :] += mm(score_grad, asked_only)
+            part = mm(score_grad, biased[head][1][:live], TN)
+            query_grad = part if query_grad is None else query_grad + part
+        joined_grad[0, pl.ds(first, block), columns] = (query_grad * HEAD_DIM**-0.5).astype(BF16)
+    joined_grad[1, :, columns] = key_total[...].astype(BF16)
+    joined_grad[2, :, columns] = value_total[...].astype(BF16)
+
+
+def back_comm_kernel(
+    block, tile, group,
+    length_ref, pass_ref, inputs, rows_in, out_w, log_rows, attended, hidden_grad, mlp_gain_grad,
+    up_done, down_done, up_half, down_half, qkv_in, joined_in,
+    grad_input, small_sum, up_total, down_total, attn_total,
+    qkv_w, joined, branch_grad, attended_grad, normed, joined_grad, key_bias, key_total, value_total,
+    grads, first, in_x, in_y, last, block_sum,
+    up_x, up_y, up_last, up_block, down_x, down_y, down_last, down_block,
+    up_in, up_mid, up_out, down_in, down_mid, down_out, attn_in, attn_mid, attn_out,
+    small_own, small_slots, small_plane, small_reps,
+    sends, recvs, up_sends, up_recvs, down_sends, down_recvs, z_sends, z_recvs,
+    plane_sends, plane_recvs, rep_sends, rep_recvs, loads,
+):
+    place = Place()
+    rows, width = inputs.shape
+    shards = small_slots.shape[0]
+    reps = small_reps.shape[0]
+    chunks = up_total.shape[0]
+    groups = width // group
+    pairs = width // PAIR
+    per_group = group // PAIR
+    others = [lax.rem(place.me + shift, shards) for shift in range(1, shards)]
+    others_z = [lax.rem(place.z + shift, reps) for shift in range(1, reps)]
+    enter(place, others, others_z)
+    take = [
+        pltpu.make_async_copy(joined_in, joined, loads.at[0]),
+        pltpu.make_async_copy(qkv_in, qkv_w, loads.at[1]),
+    ]
+    for copy in take:
+        copy.start()
+
+    up_late = Scatter(place, None, up_half, up_x, up_y, up_last, up_sends, up_recvs, 0)
+    down_late = Scatter(place, None, down_half, down_x, down_y, down_last, down_sends, down_recvs, 0)
+
+    def message(index):
+        return Scatter(
+            place, grads.at[index], first.at[index], in_x.at[index], in_y.at[index], last.at[index],
+            sends, recvs, index,
+        )
+
+    out_msg = message(0)
+    qkv_msg = [message(1 + index) for index in range(groups)]
+
+    lines = {}
+
+    def line(key, source, inward, middle, outward, total):
+        lines[key] = Column(place, source, inward, middle, outward, total, z_sends, z_recvs, len(lines))
+
+    for index in range(chunks):
+        final = index == chunks - 1
+        line(("d", index), down_block if final else down_done.at[index],
+             down_in.at[index], down_mid.at[index], down_out.at[index], down_total.at[index])
+        line(("u", index), up_block if final else up_done.at[index],
+             up_in.at[index], up_mid.at[index], up_out.at[index], up_total.at[index])
+    for index in range(1 + groups):
+        line(("a", index), block_sum.at[index], attn_in.at[index], attn_mid.at[index], attn_out.at[index],
+             attn_total.at[index])
+
+    down_late.spread()
+    up_late.spread()
+    for index in range(chunks - 1):
+        lines["d", index].begin()
+        lines["u", index].begin()
+
+    fill_bias(length_ref[0], key_bias)
+    norm_rows(inputs, rows_in[0:1, :], rows_in[1:2, :], normed)
+
+    @pl.loop(0, rows // tile)
+    def _(step):
+        at = pl.ds(step * tile, tile)
+        shown = hidden_grad[at, :].astype(BF16)
+        branch_grad[at, :] = shown
+        attended_grad[at, :] = mm(shown, out_w[...], NT).astype(BF16)
+
+    lines["d", 0].cross()
+    down_late.fold()
+    grads[0] = mm(attended[...], branch_grad[...], TN).astype(BF16).reshape(grads.shape[1:])
+    out_msg.swap()
+    for copy in take:
+        copy.wait()
+
+    def late_close(message, target, key):
+        message.close(target)
+        lines[key].begin()
+
+    def close(index):
+        message(index).close(block_sum.at[index])
+        lines["a", index].begin()
+
+    def send(index):
+        message(index).merge()
+        message(index).spread()
+
+    after_pair = [
+        lambda: (lines["u", 0].cross(), send(0), up_late.fold(), lines["d", 1].cross()),
+        lambda: (late_close(down_late, down_block, ("d", 2)), lines["u", 1].cross(), lines["d", 0].settle(),
+                 lines["u", 0].settle(), out_msg.fold()),
+        lambda: (send(1), late_close(up_late, up_block, ("u", 2)), lines["d", 2].cross(), lines["d", 1].settle(),
+                 lines["u", 1].settle(), lines["d", 0].finish(), lines["u", 0].finish()),
+        lambda: (close(0), qkv_msg[0].fold(), lines["u", 2].cross(), lines["d", 2].settle(),
+                 lines["d", 1].finish(), lines["u", 1].finish()),
+        lambda: (send(2), close(1), lines["a", 0].cross(), lines["u", 2].settle()),
+        lambda: (qkv_msg[1].fold(), lines["a", 1].cross(), lines["a", 0].settle(), lines["d", 2].finish(),
+                 lines["u", 2].finish()),
+    ]
+
+    @pl.loop(0, pairs)
+    def _(pair):
+        attention_columns(
+            joined, log_rows, attended_grad, joined_grad, key_bias, key_total, value_total, pair, block
+        )
+
+        @pl.when(lax.rem(pair, per_group) == per_group - 1)
+        def _():
+            index = pair // per_group
+            columns = pl.ds(pl.multiple_of(index * group, group), group)
+            for plane in range(3):
+                part = mm(normed[...], joined_grad[plane, :, columns], TN).astype(BF16)
+                grads[1 + index, :, :, :, :, pl.ds(plane * group, group)] = part.reshape(
+                    grads.shape[1:5] + (group,)
+                )
+            message(1 + index).swap()
+
+        for index in range(pairs):
+            @pl.when(pair == index)
+            def _(index=index):
+                after_pair[index]()
+
+    small_own[...] = jnp.zeros_like(small_own)
+
+    def after_rows(step):
+        @pl.when(step == 0)
+        def _():
+            send(3)
+            close(2)
+
+        @pl.when(step == 1)
+        def _():
+            lines["a", 1].settle()
+
+        @pl.when(step == 2)
+        def _():
+            qkv_msg[2].fold()
+            lines["a", 2].cross()
+
+    @pl.loop(0, rows // 256)
+    def _(step):
+        at = pl.ds(step * 256, 256)
+        grad = mm(joined_grad[0, at, :], qkv_w[0], NT)
+        grad = grad + mm(joined_grad[1, at, :], qkv_w[1], NT)
+        grad = grad + mm(joined_grad[2, at, :], qkv_w[2], NT)
+        unit, scale = norm_parts(inputs[at, :].astype(F32) + rows_in[0:1, :])
+        total = hidden_grad[at, :] + norm_back(unit, scale, grad, rows_in[1:2, :])
+        grad_input[at, :] = total
+        small_own[5:6, :] += jnp.sum(grad * unit, axis=0, keepdims=True)
+        small_own[0:1, :] += jnp.sum(total, axis=0, keepdims=True)
+        after_rows(step)
+
+    close(3)
+    places = lax.broadcasted_iota(jnp.int32, small_own.shape, 0)
+    own = small_own[...]
+    table = jnp.where((places == pass_ref[0]) & (places < 5), own[0:1], 0.0)
+    own = jnp.where(places == 5, own, table)
+    small_own[...] = jnp.where(places == 6, mlp_gain_grad[0:1], own)
+    small_slots[place.me] = small_own[...]
+    plane_copies = [
+        remote(small_own, small_slots.at[place.me], plane_sends, plane_recvs, shift, place.at(other))
+        for shift, other in enumerate(others)
+    ]
+    for copy in plane_copies:
+        copy.start()
+    lines["a", 2].settle()
+    lines["a", 3].cross()
+    for copy in plane_copies:
+        copy.wait_recv()
+    total = small_slots[0]
+    for shard in range(1, shards):
+        total = total + small_slots[shard]
+    small_plane[...] = total
+    small_reps[place.z] = total
+    rep_copies = [
+        remote(small_plane, small_reps.at[place.z], rep_sends, rep_recvs, shift, (place.me, other))
+        for shift, other in enumerate(others_z)
+    ]
+    for copy in rep_copies:
+        copy.start()
+    lines["a", 3].settle()
+    for copy in rep_copies:
+        copy.wait_recv()
+    total = small_reps[0]
+    for rep in range(1, reps):
+        total = total + small_reps[rep]
+    small_sum[...] = total
+    for index in range(1 + groups):
+        lines["a", index].finish()
+    for index in range(1 + groups):
+        message(index).drain()
+    up_late.drain(swapped=False)
+    down_late.drain(swapped=False)
+    for copy in plane_copies + rep_copies:
+        copy.wait_send()
+
+
+def back_comm(reps, seq_lens, pass_idx, inputs, rows_in, out_w, log_rows, attended, hidden_grad, mlp_gain_grad,
+              up_done, down_done, up_half, down_half, qkv_w, joined):
+    rows, width = inputs.shape
+    _, _, up_part, chunk = up_half.shape
+    down_part = down_half.shape[2]
+    chunks = up_done.shape[0] + 1
+    shards = width // up_part
+    group = 4 * HEAD_DIM
+    count = 1 + width // group
+    wide = 3 * group
+    vm = lambda *shape: pltpu.VMEM(shape, BF16)
+    return pl.pallas_call(
+        functools.partial(back_comm_kernel, 256, 512, group),
+        out_shape=[
+            shaped((rows, width), F32), shaped((8, width), F32), shaped((chunks, up_part, chunk), BF16),
+            shaped((chunks, down_part, width), BF16), shaped((count, up_part, wide), BF16),
+        ],
+        in_specs=smem_spec(2) + vmem_spec(11) + any_spec(2),
+        out_specs=vmem_spec(5),
+        scratch_shapes=[
+            vm(3, width, width), vm(3, rows, width), vm(rows, width), vm(rows, width), vm(rows, width),
+            vm(3, rows, width), vm(rows, PAIR), pltpu.VMEM((rows, PAIR), F32), pltpu.VMEM((rows, PAIR), F32),
+        ]
+        + scatter_scratch(count, up_part, wide)
+        + [
+            vm(count, up_part, wide),
+            vm(2, up_part, chunk // 2), vm(2, up_part, chunk // 2), vm(up_part, chunk), vm(up_part, chunk),
+            vm(2, down_part, width // 2), vm(2, down_part, width // 2), vm(down_part, width), vm(down_part, width),
+        ]
+        + [vm(chunks, up_part, chunk)] * 3
+        + [vm(chunks, down_part, width)] * 3
+        + [vm(count, up_part, wide)] * 3
+        + [
+            pltpu.VMEM((8, width), F32), pltpu.VMEM((shards, 8, width), F32), pltpu.VMEM((8, width), F32),
+            pltpu.VMEM((reps, 8, width), F32),
+        ]
+        + dma((count, 5), (count, 5), (1, 5), (1, 5), (1, 5), (1, 5), (2 * chunks + count, 3), (2 * chunks + count, 3),
+              (shards - 1,), (shards - 1,), (reps - 1,), (reps - 1,), (2,)),
+        compiler_params=pltpu.CompilerParams(
+            vmem_limit_bytes=VMEM_LIMIT, collective_id=3, has_side_effects=True
+        ),
+    )(seq_lens, pass_idx, inputs, rows_in, out_w, log_rows, attended, hidden_grad, mlp_gain_grad,
+      up_done, down_done, up_half, down_half, qkv_w, joined)
+
+
+def direct(reps, inputs, seq_lens, pass_idx, pass_table, gain_attn, w_qkv, w_out, gain_mlp, w_up, w_down, cotangent):
+    _, rows, width = inputs.shape
+    me = lax.axis_index("shard")
+    part = w_out.shape[0]
+    shards = width // part
+    slices = 3
+    passes = pass_table.shape[0]
+    lanes = w_up.shape[1] // (slices * shards)
+    own = jnp.concatenate(
+        [pass_table, jnp.zeros((8 - passes, part), BF16), gain_attn[None], gain_mlp[None], jnp.zeros((6, part), BF16)]
+    )
+    small = jnp.where(jnp.arange(width)[None, :] // part == me, jnp.tile(own, (1, shards)), BF16(0))
+    qkv = w_qkv.reshape(part, 3, width).transpose(1, 0, 2)
+    up = w_up.reshape(part, shards, slices, lanes).transpose(2, 0, 1, 3).reshape(slices, part, shards * lanes)
+    down = w_down.reshape(slices, w_down.shape[0] // slices, width)
+    ahead = 2
+    rows_in, log_rows, joined, attended, hidden, qkv_w, out_w, up_have, down_have = front_comm(
+        ahead, seq_lens, pass_idx, inputs[0], small, qkv, w_out, up, down
+    )
+    outputs, hidden_grad, mlp_gain_grad, up_done, down_done, up_half, down_half = mlp_comm(
+        ahead, hidden, cotangent[0], rows_in, up_have, down_have, up, down
+    )
+    grad_input, small_sum, up_total, down_total, attn_total = back_comm(
+        reps, seq_lens, pass_idx, inputs[0], rows_in, out_w, log_rows, attended, hidden_grad, mlp_gain_grad,
+        up_done, down_done, up_half, down_half, qkv_w, joined,
+    )
+    small_own = lax.dynamic_slice(small_sum, (0, me * part), (8, part))
+    up_grad = up_total.reshape(slices, part, shards, lanes).transpose(1, 2, 0, 3).reshape(w_up.shape)
+    down_grad = down_total.reshape(w_down.shape)
+    group = attn_total.shape[2] // 3
+    qkv_grad = attn_total[1:].reshape(width // group, part, 3, group).transpose(1, 2, 0, 3).reshape(w_qkv.shape)
+    return (
+        outputs[None], grad_input[None], small_own[:passes], small_own[5], qkv_grad.astype(F32),
+        attn_total[0].astype(F32), small_own[6], up_grad.astype(F32), down_grad.astype(F32),
+    )
+
+
 def solution(mesh):
+    shards, reps = mesh.shape["shard"], mesh.shape["rep"]
+    run = functools.partial(direct, reps) if (shards, reps) == (8, 4) else body
     part = P(("shard", "rep"), None, None)
     return jax.shard_map(
-        body,
+        run,
         mesh=mesh,
         in_specs=(
             part, P(("shard", "rep")), P(("shard", "rep")), P(None, "shard"), P("shard"), P("shard", None),

time: 587 us -> 238 us (0.41)
  waiting for transfers between devices: 376 us -> 0 us
  Pallas kernels: 134 us -> 214 us
  blocking collectives: 36.3 us -> 0 us
  between operations: 16.2 us -> 2.07 us
    reduce_scatter x4 -> x0, waiting for transfers between devices: 197 us -> none  [body(): lax.psum_scatter(grad, 'shard', scatter_dimension=dim, tiled=True)]
    pallas_call x3, Pallas kernels: 134 us -> 214 us  [the longest x1 87.7 us: back_comm(): pl.pallas_call(functools.partial(back_comm_kernel, 256, 512, group), out_...]
    all_gather x4 -> x0, waiting for transfers between devices: 72.2 us -> none  [the longest x1 39.8 us: body(): down_w = gather(w_down, axis=0)]
    psum x1 -> x0, waiting for transfers between devices: 64.8 us -> none  [body(): lax.psum((up_part, down_part, out_part, qkv_part), 'rep')]
    unnamed x11 -> x0, waiting for transfers between devices: 42.1 us -> none
    unnamed x1 -> x0, blocking collectives: 13.9 us -> none
    psum x1 -> x0, blocking collectives: 11.9 us -> none  [body(): small = lax.psum(scatter(small, 1), 'rep')]
    all_gather x1 -> x0, blocking collectives: 10.5 us -> none  [body(): table = gather(pass_table, axis=1)]
  transfers between devices with their start and end apart: 10 -> 0, of which waited for: 8 -> 0; matrix products, arithmetic and copies ran while one was open for 3% -> 0% of each run, Pallas kernels for 6% -> 0%
where the time goes in v2:
time: 238 us
  Pallas kernels  214 us (90%)
  local copies, waits for them, and re-layouts  17.4 us (7%)
  other arithmetic  4.48 us (2%)
    pallas_call x1, Pallas kernels, back_comm(): pl.pallas_call(functools.partial(back_comm_kernel, 256, 512, group), out_...  87.7 us
    pallas_call x1, Pallas kernels, front_comm(): pl.pallas_call(functools.partial(front_comm_kernel, ahead, 256, 512, grou...  67 us
    pallas_call x1, Pallas kernels, mlp_comm(): pl.pallas_call(functools.partial(mlp_comm_kernel, ahead, 512), out_shape=...  59.1 us
    unnamed x13, local copies, waits for them, and re-layouts  4.97 us

profile of v2, /device:TPU:0, one launch (start us, length us, event | category | flops | bytes accessed | tf_op | source)
XLA Modules:
  0.0 237.7 jit_solution(8795987108898747173)
XLA Ops:
  2.0 1.4 concatenate.3
  3.4 0.1 tile.10
  3.5 0.6 broadcast_select_fusion.small_own
  4.1 1.8 copy.32
  5.9 1.8 reshape.77
  7.7 0.1 copy.24
  7.8 1.1 reshape.78.up_own
  8.9 67.0 %shard_map.178 = (f32[8,768]{1,0:T(8,128)}, f32[16,1024]{1,0:T(8,128)}, bf16[3,1024,768]{2,1,0:T(8,128)(2,1)}, bf16[1024,768]{1,0:T(8,128)(2,1)}, f32[1024,768]{...) custom-call(s32[1]{0:T(128)S(6)} %copy.35.length_ref, ...), custom_call_target="tpu_custom_call" | custom-call | tf_op jit(solution)/shard_map/pallas_call | solution.py:635
  75.9 59.1 %shard_map.179 = (bf16[1024,768]{1,0:T(8,128)(2,1)}, f32[1024,768]{1,0:T(8,128)}, f32[8,768]{1,0:T(8,128)}, bf16[2,96,1024]{2,1,0:T(8,128)(2,1)}, bf16[2,128,768...) custom-call(f32[1024,768]{1,0:T(8,128)} %get-tuple-element.30.hidden, ...), custom_call_target="tpu_custom_call" | custom-call | tf_op jit(solution)/shard_map/pallas_call | solution.py:889
  135.0 87.7 %shard_map.180 = (f32[1024,768]{1,0:T(8,128)}, f32[8,768]{1,0:T(8,128)}, bf16[3,96,1024]{2,1,0:T(8,128)(2,1)}, bf16[3,128,768]{2,1,0:T(8,128)(2,1)}, bf16[4,96,768]{2,1,0:T(8,128)(2,1)}) custom-call(s32[1]{0:T(128)S(6)} %copy.35.length_ref, s32[1]{0:T(128)S(6)} %copy.36.pass_ref, bf16[1024,768]{1,0:T(8,128)(2,1)} %bitcast.39, ...), custom_call_target="tpu_custom_call" | custom-call | tf_op jit(solution)/shard_map/pallas_call | solution.py:1213
  222.6 0.8 constant_dynamic-slice_fusion
  223.4 0.0 copy-start.4
  223.4 0.5 slice_bitcast_fusion
  223.9 1.6 bitcast_convert_fusion.1
  225.6 1.1 slice_convert_fusion
  226.7 0.5 reshape.84
  227.1 0.0 copy-done.4
  227.2 0.6 copy.25
  227.8 0.0 copy-start.3
  227.8 1.5 reshape.80
  229.3 0.0 copy-done.3
  229.3 0.1 copy.28
  229.4 0.8 copy.31
  230.3 0.0 copy-start.2
  230.3 1.5 reshape.82
  231.7 0.0 copy-done.2
  231.7 0.0 copy-start.1
  231.8 1.1 bitcast_convert_fusion
  232.9 0.7 copy-done.1
  233.6 0.0 copy-start
  233.6 1.1 copy.37
  234.7 1.3 copy-done
  236.0 1.7 copy.38
  (4 shorter events, 0.0 us)
Async XLA Ops:
  223.4 3.7 %copy-start.4 = (f32[8,96]{1,0:T(8,128)}, f32[8,96]{1,0:T(8,128)S(1)}, u32[]{:S(2)}) copy-start(f32[8,96]{1,0:T(8,128)S(1)} %constant_dynamic-slice_fusion) | copy-start | bytes 9220
  227.8 1.5 copy-start.3
  230.3 1.5 copy-start.2
  231.7 1.8 copy-start.1
  233.6 2.5 %copy-start = (f32[1024,768]{1,0:T(8,128)S(1)}, f32[1024,768]{1,0:T(8,128)}, u32[]{:S(2)}) copy-start(f32[1024,768]{1,0:T(8,128)} %get-tuple-element.46) | copy-start | bytes 9437188

commit v3 on v2

--- a/solution.py
+++ b/solution.py
@@ -363,6 +363,8 @@
         self.by_y = self.me + 4 - 8 * self.y
         self.by_core = self.me + 1 - 2 * self.core
         self.by_both = self.by_x + 4 - 8 * self.y
+        self.side = lax.rem(self.z, 2)
+        self.by_z = self.z + 1 - 2 * self.side
 
     def at(self, shard):
         return (shard, self.z)
@@ -376,57 +378,72 @@
 
 
 class Gather:
-    def __init__(self, place, own, block_of, half_of, sends, recvs, local, row):
-        self.place, self.own, self.block, self.half = place, own, block_of, half_of
+    def __init__(self, place, part, fills, sends, recvs, local, row, shared):
+        self.place, self.part, self.fills, self.shared = place, part, fills, shared
         self.sends, self.recvs, self.local, self.row = sends, recvs, local, row
-
-    def copy(self, slot, src, dst, shard):
-        return remote(src, dst, self.sends, self.recvs, (self.row, slot), self.place.at(shard))
-
-    def same(self, slot, ref, shard):
-        return self.copy(slot, ref, ref, shard)
+        self.slots = 17 if shared else 9
+
+    def piece(self, shard, columns=None, other=False):
+        if not self.shared:
+            return self.part(shard, None, columns)
+        side = 1 - self.place.side if other else self.place.side
+        return self.part(shard, side, columns)
 
     def make(self, slot):
-        p, block, half = self.place, self.block, self.half
-        if slot < 3:
-            return self.copy(slot, self.own, block(p.me), (p.by_x, p.by_y, p.by_core)[slot])
-        if slot == 3:
-            return self.same(slot, half(p.by_x, 0), p.by_y)
-        if slot == 4:
-            return self.same(slot, half(p.by_y, 1), p.by_x)
-        if slot < 7:
-            return self.same(slot, block(p.by_x if slot == 5 else p.by_y), p.by_core)
-        return self.same(slot, half(p.by_both, slot - 7), p.by_core)
-
-    def here(self):
-        return pltpu.make_async_copy(self.own, self.block(self.place.me), self.local.at[self.row])
+        p = self.place
+        rep = p.z
+        if slot < 2:
+            ref, shard = self.piece(p.me), (p.by_x, p.by_y)[slot]
+        elif slot == 2:
+            ref, shard = self.part(p.me, None, None), p.by_core
+        elif slot == 3:
+            ref, shard = self.piece(p.by_x, 0), p.by_y
+        elif slot == 4:
+            ref, shard = self.piece(p.by_y, 1), p.by_x
+        else:
+            kind = (slot - 5) % 4
+            source = (p.by_x, p.by_y, p.by_both, p.by_both)[kind]
+            ref = self.piece(source, None if kind < 2 else kind - 2, slot >= 13)
+            shard = p.by_core
+            if 9 <= slot < 13:
+                shard, rep = p.me, p.by_z
+        return remote(ref, ref, self.sends, self.recvs, (self.row, slot), (shard, rep))
+
+    def fill(self):
+        for source, target in self.fills:
+            pltpu.make_async_copy(source, target, self.local.at[self.row]).start()
 
     def start(self):
+        own = self.part(self.place.me, None, None)
+        pltpu.make_async_copy(own, own, self.local.at[self.row]).wait()
         for slot in range(3):
             self.make(slot).start()
-        self.here().start()
+
+    def pass_on(self, slot, *targets):
+        self.make(slot).wait_recv()
+        for target in targets:
+            if target < self.slots:
+                self.make(target).start()
 
     def relay(self):
-        self.make(0).wait_recv()
-        self.make(3).start()
-        self.make(5).start()
-        self.make(1).wait_recv()
-        self.make(4).start()
-        self.make(6).start()
+        self.pass_on(0, 3, 5, 9)
+        self.pass_on(1, 4, 6, 10)
 
     def finish(self):
-        self.make(3).wait_recv()
-        self.make(7).start()
-        self.make(4).wait_recv()
-        self.make(8).start()
+        self.pass_on(3, 7, 11)
+        self.pass_on(4, 8, 12)
+
+    def across(self):
+        if self.shared:
+            for slot in range(9, 13):
+                self.pass_on(slot, slot + 4)
 
     def ready(self):
-        for slot in (2, 5, 6, 7, 8):
+        for slot in (2, 5, 6, 7, 8) + ((13, 14, 15, 16) if self.shared else ()):
             self.make(slot).wait_recv()
-        self.here().wait()
 
     def drain(self):
-        for slot in range(9):
+        for slot in range(self.slots):
             self.make(slot).wait_send()
 
 
@@ -439,15 +456,31 @@
     pl.semaphore_wait(barrier, len(shards) + len(reps))
 
 
-def rows_block(ref, rows, lead=(), columns=slice(None)):
-    def block(shard):
-        return ref.at[lead + (pl.ds(pl.multiple_of(shard * rows, rows), rows), columns)]
-
-    def half(shard, part):
-        start = pl.multiple_of(shard * rows + part * (rows // 2), rows // 2)
-        return ref.at[lead + (pl.ds(start, rows // 2), columns)]
-
-    return block, half
+def part_of(ref, rows, lead, start, width):
+    def part(shard, side, half):
+        count = rows if side is None else rows // 2
+        first = shard * rows if side is None else shard * rows + side * count
+        left, wide = (start, width) if half is None else (start + half * (width // 2), width // 2)
+        return ref.at[lead + (pl.ds(pl.multiple_of(first, count), count), pl.ds(left, wide))]
+
+    return part
+
+
+def up_fills(own, ref, index, place, shards):
+    part, chunk = own.shape[0], ref.shape[2]
+    lanes = chunk // shards
+    slices = own.shape[1] // chunk
+    rows = pl.ds(pl.multiple_of(place.me * part, part), part)
+    return [
+        (own.at[:, pl.ds((slices * shard + index) * lanes, lanes)], ref.at[index, rows, pl.ds(shard * lanes, lanes)])
+        for shard in range(shards)
+    ]
+
+
+def down_fills(own, ref, index, place, shards):
+    count = ref.shape[1] // shards
+    rows = pl.ds(pl.multiple_of(place.me * count, count), count)
+    return [(own.at[pl.ds(index * count, count), :], ref.at[index, rows, :])]
 
 
 def attention_rows(joined, attended, log_rows, key_bias, pair, block):
@@ -489,64 +522,88 @@
         normed[at, :] = (norm_parts(entered)[0] * gain).astype(BF16)
 
 
+def select_lanes(place, part, width):
+    rows = lax.broadcasted_iota(jnp.int32, (part, width), 0)
+    lanes = lax.broadcasted_iota(jnp.int32, (part, width), 1)
+    return lanes == rows + place.me * part
+
+
+SHARED = (False, True, True, False, True, True, False, True, True, False)
+
+
 def front_comm_kernel(
     ahead, block, tile, group,
-    length_ref, pass_ref, inputs, small_own, qkv_own, out_own, up_own, down_own,
-    rows_out, log_out, joined_out, attended_out, hidden_out, qkv_out, out_out, up_out, down_out,
-    slots, normed, joined, attended, hidden, qkv_w, out_w, key_bias,
+    length_ref, pass_ref, inputs, table_own, attn_gain_own, mlp_gain_own, qkv_own, out_own, up_own, down_own,
+    rows_out, log_out, normed_out, joined_out, attended_out, hidden_out, qkv_out, out_out, up_out, down_out,
+    slots, small_wide, small_own, normed, joined, attended, hidden, qkv_w, out_w, up_w, down_w, key_bias,
     sends, recvs, local, small_sends, small_recvs, saves,
 ):
     place = Place()
     rows, width = inputs.shape
     shards = slots.shape[0]
-    part = qkv_own.shape[1]
+    part = qkv_own.shape[0]
     groups = width // group
+
+    pieces = []
+
+    def add(part_at, fills):
+        row = len(pieces)
+        pieces.append(Gather(place, part_at, fills, sends, recvs, local, row, SHARED[row]))
+
+    own_rows = pl.ds(pl.multiple_of(place.me * part, part), part)
+    for index in range(groups):
+        columns = pl.ds(index * group, group)
+        fills = [
+            (qkv_own.at[:, pl.ds(plane * width + index * group, group)], qkv_w.at[plane, own_rows, columns])
+            for plane in range(3)
+        ]
+        add(part_of(qkv_w, part, (slice(None),), index * group, group), fills)
+    add(part_of(out_w, part, (), 0, width), [(out_own, out_w.at[own_rows, :])])
+    for index in range(ahead):
+        add(part_of(up_w, part, (index,), 0, up_w.shape[2]), up_fills(up_own, up_w, index, place, shards))
+        add(part_of(down_w, down_w.shape[1] // shards, (index,), 0, width),
+            down_fills(down_own, down_w, index, place, shards))
+    count = len(pieces)
+    for piece in pieces:
+        piece.fill()
+
+    chosen = select_lanes(place, part, width).astype(BF16)
+    small_wide[...] = jnp.zeros_like(small_wide)
+    small_wide[0 : table_own.shape[0], :] = mm(table_own[...], chosen)
+    small_wide[8:9, :] = mm(attn_gain_own[...], chosen)
+    small_wide[9:10, :] = mm(mlp_gain_own[...], chosen)
+    small_own[...] = small_wide[...].astype(BF16)
+    slots[place.me] = small_own[...]
+
     others = [lax.rem(place.me + shift, shards) for shift in range(1, shards)]
-    enter(place, others)
-
+    enter(place, others, [place.by_z])
     smalls = [
         remote(small_own, slots.at[place.me], small_sends, small_recvs, shift, place.at(other))
         for shift, other in enumerate(others)
     ]
+    pieces[0].start()
     for copy in smalls:
         copy.start()
-    mine = pltpu.make_async_copy(small_own, slots.at[place.me], small_sends.at[shards - 1])
-    mine.start()
-
-    pieces = []
-
-    def add(own, block_of, half_of):
-        pieces.append(Gather(place, own, block_of, half_of, sends, recvs, local, len(pieces)))
-
-    for index in range(groups):
-        columns = pl.ds(index * group, group)
-        add(qkv_own.at[:, :, columns], *rows_block(qkv_w, part, (slice(None),), columns))
-    add(out_own, *rows_block(out_w, part))
-    for index in range(ahead):
-        add(up_own.at[index], *rows_block(up_out, part, (index,)))
-        add(down_own.at[index], *rows_block(down_out, down_own.shape[1], (index,)))
-    count = len(pieces)
+    pieces[1].start()
 
     def tick(index):
+        if index < count:
+            pieces[index].relay()
         if index + 2 < count:
             pieces[index + 2].start()
-        if index < count:
-            pieces[index].relay()
         if 0 <= index - 1 < count:
             pieces[index - 1].finish()
-
-    pieces[0].start()
-    pieces[1].start()
+        if 0 <= index - 2 < count:
+            pieces[index - 2].across()
+
     fill_bias(length_ref[0], key_bias)
-    mine.wait()
     for copy in smalls:
         copy.wait_recv()
     total = slots[0].astype(F32)
     for shard in range(1, shards):
         total = total + slots[shard].astype(F32)
     places = lax.broadcasted_iota(jnp.int32, total.shape, 0)
-    pass_row = jnp.sum(jnp.where(places == pass_ref[0], total, 0.0), axis=0, keepdims=True)
-    rows_out[0:1, :] = pass_row
+    rows_out[0:1, :] = jnp.sum(jnp.where(places == pass_ref[0], total, 0.0), axis=0, keepdims=True)
     rows_out[1:3, :] = total[8:10]
     rows_out[3:8, :] = jnp.zeros((5, width), F32)
 
@@ -554,11 +611,20 @@
     norm_rows(inputs, rows_out[0:1, :], rows_out[1:2, :], normed)
     tick(1)
 
-    def save(source, target, index):
-        return pltpu.make_async_copy(source, target, saves.at[index])
-
+    keep = []
+
+    def save(source, target):
+        keep.append(pltpu.make_async_copy(source, target, saves.at[len(keep)]))
+        return keep[-1]
+
+    save(normed, normed_out).start()
     pairs = width // PAIR
     per_group = group // PAIR
+    joined_saves = [
+        save(joined.at[:, :, pl.ds(index * group, group)], joined_out.at[:, :, pl.ds(index * group, group)])
+        for index in range(groups)
+    ]
+    qkv_save = save(qkv_w, qkv_out)
 
     @pl.loop(0, pairs)
     def _(pair):
@@ -566,6 +632,8 @@
             @pl.when(pair == index * per_group)
             def _(index=index):
                 pieces[index].ready()
+                if index == groups - 1:
+                    qkv_save.start()
 
         @pl.when(lax.rem(pair, per_group) == 0)
         def _():
@@ -579,29 +647,25 @@
         for index in range(pairs):
             @pl.when(pair == index)
             def _(index=index):
+                if index % per_group == 0:
+                    joined_saves[index // per_group].start()
                 tick(index + 2)
 
-    keep = [
-        save(joined, joined_out, 0), save(attended, attended_out, 1), save(qkv_w, qkv_out, 2),
-    ]
-    for copy in keep:
-        copy.start()
+    save(attended, attended_out).start()
     pieces[groups].ready()
-    keep.append(save(out_w, out_out, 3))
-    keep[-1].start()
-
-    @pl.loop(0, rows // tile)
-    def _(step):
+    save(out_w, out_out).start()
+    for step in range(rows // tile):
         at = pl.ds(step * tile, tile)
         entered = inputs[at, :].astype(F32) + rows_out[0:1, :]
         hidden[at, :] = entered + mm(attended[at, :], out_w[...])
-
-    keep.append(save(hidden, hidden_out, 4))
-    keep[-1].start()
-    for index in range(pairs + 2, count + 1):
+        save(hidden.at[at, :], hidden_out.at[at, :]).start()
+        tick(pairs + 2 + step)
+    for index in range(pairs + 2 + rows // tile, count + 2):
         tick(index)
-    for piece in pieces[groups + 1 :]:
+    late = [(ref.at[index], target.at[index]) for index in range(ahead) for ref, target in ((up_w, up_out), (down_w, down_out))]
+    for piece, (source, target) in zip(pieces[groups + 1 :], late):
         piece.ready()
+        save(source, target).start()
     for piece in pieces:
         piece.drain()
     for copy in smalls:
@@ -626,32 +690,33 @@
     return jax.ShapeDtypeStruct(shape, kind)
 
 
-def front_comm(ahead, seq_lens, pass_idx, inputs, small, qkv, out, up, down):
+def front_comm(ahead, slices, seq_lens, pass_idx, inputs, table, attn_gain, mlp_gain, qkv, out, up, down):
     rows, width = inputs.shape
     shards = width // out.shape[0]
-    chunk = up.shape[2]
+    chunk = up.shape[1] // slices
     group = 4 * HEAD_DIM
     count = width // group + 1 + 2 * ahead
+    vm = lambda *shape: pltpu.VMEM(shape, BF16)
     return pl.pallas_call(
         functools.partial(front_comm_kernel, ahead, 256, 512, group),
         out_shape=[
-            shaped((8, width), F32), shaped((16, rows), F32), shaped((3, rows, width), BF16),
-            shaped((rows, width), BF16), shaped((rows, width), F32), shaped((3, width, width), BF16),
-            shaped((width, width), BF16), shaped((ahead, width, chunk), BF16), shaped((ahead, chunk, width), BF16),
+            shaped((8, width), F32), shaped((16, rows), F32), shaped((rows, width), BF16),
+            shaped((3, rows, width), BF16), shaped((rows, width), BF16), shaped((rows, width), F32),
+            shaped((3, width, width), BF16), shaped((width, width), BF16), shaped((ahead, width, chunk), BF16),
+            shaped((ahead, chunk, width), BF16),
         ],
-        in_specs=smem_spec(2) + vmem_spec(1) + any_spec(5),
-        out_specs=vmem_spec(2) + any_spec(7),
+        in_specs=smem_spec(2) + vmem_spec(4) + any_spec(4),
+        out_specs=vmem_spec(2) + any_spec(8),
         scratch_shapes=[
-            pltpu.VMEM((shards,) + small.shape, BF16), pltpu.VMEM((rows, width), BF16),
-            pltpu.VMEM((3, rows, width), BF16), pltpu.VMEM((rows, width), BF16), pltpu.VMEM((rows, width), F32),
-            pltpu.VMEM((3, width, width), BF16), pltpu.VMEM((width, width), BF16), pltpu.VMEM((rows, PAIR), BF16),
-            pltpu.SemaphoreType.DMA((count, 9)), pltpu.SemaphoreType.DMA((count, 9)), pltpu.SemaphoreType.DMA((count,)),
-            pltpu.SemaphoreType.DMA((shards,)), pltpu.SemaphoreType.DMA((shards,)), pltpu.SemaphoreType.DMA((5,)),
-        ],
+            vm(shards, 16, width), pltpu.VMEM((16, width), F32), vm(16, width), vm(rows, width), vm(3, rows, width),
+            vm(rows, width), pltpu.VMEM((rows, width), F32), vm(3, width, width), vm(width, width),
+            vm(ahead, width, chunk), vm(ahead, chunk, width), vm(rows, PAIR),
+        ]
+        + dma((count, 17), (count, 17), (count,), (shards,), (shards,), (9 + width // group + 2 * ahead,)),
         compiler_params=pltpu.CompilerParams(
             vmem_limit_bytes=VMEM_LIMIT, collective_id=1, has_side_effects=True
         ),
-    )(seq_lens, pass_idx, inputs, small, qkv, out, up, down)
+    )(seq_lens, pass_idx, inputs, table, attn_gain, mlp_gain, qkv, out, up, down)
 
 
 class Scatter:
@@ -727,34 +792,47 @@
 
 
 def mlp_comm_kernel(
-    ahead, tile,
+    ahead, tile, shards,
     hidden, cotangent, rows_in, up_have, down_have, up_own, down_own,
-    outputs, hidden_grad, gain_grad, up_done, down_done, up_half, down_half,
-    up_w, down_w, second, mixed, active, rising_grad,
+    outputs_out, hidden_grad_out, gain_grad, up_done_out, down_done_out, up_half, down_half,
+    outputs, hidden_grad, up_done, down_done, up_w, down_w, second, mixed, active, rising_grad,
     up_grads, up_first, up_x, up_y, up_last, down_grads, down_first, down_x, down_y, down_last,
-    gather_sends, gather_recvs, gather_local, up_sends, up_recvs, down_sends, down_recvs, loads,
+    gather_sends, gather_recvs, gather_local, up_sends, up_recvs, down_sends, down_recvs, loads, saves,
 ):
     place = Place()
     rows, width = hidden.shape
     chunks, chunk = down_w.shape[0], down_w.shape[1]
-    enter(place, [place.by_x, place.by_y, place.by_core])
     gain = rows_in[2:3, :]
 
     pieces = []
     for index in range(ahead, chunks):
-        for own, ref in ((up_own, up_w), (down_own, down_w)):
-            block, half = rows_block(ref, own.shape[1], (index,))
+        for kind in range(2):
+            row = len(pieces)
+            if kind == 0:
+                part_at = part_of(up_w, width // shards, (index,), 0, chunk)
+                fills = up_fills(up_own, up_w, index, place, shards)
+            else:
+                part_at = part_of(down_w, chunk // shards, (index,), 0, width)
+                fills = down_fills(down_own, down_w, index, place, shards)
             pieces.append(
-                Gather(place, own.at[index], block, half, gather_sends, gather_recvs, gather_local, len(pieces))
+                Gather(place, part_at, fills, gather_sends, gather_recvs, gather_local, row, SHARED[row + 4 + 2 * ahead])
             )
     for piece in pieces:
-        piece.start()
+        piece.fill()
     have = []
     for index in range(ahead):
         for ref, weights in ((up_have, up_w), (down_have, down_w)):
             have.append(pltpu.make_async_copy(ref.at[index], weights.at[index], loads.at[len(have)]))
     for copy in have:
         copy.start()
+    enter(place, [place.by_x, place.by_y, place.by_core], [place.by_z])
+    for piece in pieces:
+        piece.start()
+    keep = []
+
+    def save(source, target):
+        keep.append(pltpu.make_async_copy(source, target, saves.at[len(keep)]))
+        return keep[-1]
 
     def up_message(index):
         return Scatter(
@@ -813,6 +891,11 @@
                 for piece in pieces[2:]:
                     piece.relay()
 
+            @pl.when((part == 1) & (step == 0))
+            def _():
+                for piece in pieces[2:]:
+                    piece.across()
+
             @pl.when((part > 0) & (step == 0))
             def _():
                 message = up_message(part - 1)
@@ -828,6 +911,8 @@
 
         @pl.when(part == 0)
         def _():
+            for piece in pieces[:2]:
+                piece.across()
             for piece in pieces[2:]:
                 piece.finish()
 
@@ -850,6 +935,8 @@
             up_message(part - 1).close(up_done.at[part - 1])
 
     down_message(chunks - 1).merge(down_half)
+    save(up_done, up_done_out).start()
+    save(down_done, down_done_out).start()
     gain_grad[...] = jnp.zeros_like(gain_grad)
 
     @pl.loop(0, rows // 256)
@@ -860,6 +947,12 @@
         grad = hidden_grad[at, :]
         hidden_grad[at, :] = cotangent[at, :].astype(F32) + norm_back(unit, scale, grad, gain)
         gain_grad[0:1, :] += jnp.sum(grad * unit, axis=0, keepdims=True)
+        pltpu.make_async_copy(hidden_grad.at[at, :], hidden_grad_out.at[at, :], saves.at[4 + step]).start()
+
+    save(outputs, outputs_out).start()
+    for step in range(rows // 256):
+        at = pl.ds(step * 256, 256)
+        pltpu.make_async_copy(hidden_grad.at[at, :], hidden_grad_out.at[at, :], saves.at[4 + step]).wait()
 
     up_message(chunks - 1).merge(up_half)
     for piece in pieces:
@@ -867,6 +960,8 @@
     for index in range(chunks):
         up_message(index).drain(True, index < chunks - 1)
         down_message(index).drain(True, index < chunks - 1)
+    for copy in keep:
+        copy.wait()
 
 
 def scatter_scratch(count, part, columns):
@@ -881,28 +976,32 @@
     return [pltpu.SemaphoreType.DMA(shape) for shape in shapes]
 
 
-def mlp_comm(ahead, hidden, cotangent, rows_in, up_have, down_have, up, down):
+def mlp_comm(ahead, slices, hidden, cotangent, rows_in, up_have, down_have, up, down):
     rows, width = hidden.shape
-    chunks, up_part, chunk = up.shape
-    down_part = down.shape[1]
-    late = 2 * (chunks - ahead)
+    up_part, chunk = up.shape[0], up.shape[1] // slices
+    down_part = down.shape[0] // slices
+    shards = width // up_part
+    late = max(1, 2 * (slices - ahead))
+    vm = lambda *shape: pltpu.VMEM(shape, BF16)
     return pl.pallas_call(
-        functools.partial(mlp_comm_kernel, ahead, 512),
+        functools.partial(mlp_comm_kernel, ahead, 512, shards),
         out_shape=[
             shaped((rows, width), BF16), shaped((rows, width), F32), shaped((8, width), F32),
-            shaped((chunks - 1, up_part, chunk), BF16), shaped((chunks - 1, down_part, width), BF16),
+            shaped((slices - 1, up_part, chunk), BF16), shaped((slices - 1, down_part, width), BF16),
             shaped((2, 2, up_part, chunk), BF16), shaped((2, 2, down_part, width), BF16),
         ],
         in_specs=vmem_spec(3) + any_spec(4),
-        out_specs=vmem_spec(7),
+        out_specs=any_spec(2) + vmem_spec(1) + any_spec(2) + vmem_spec(2),
         scratch_shapes=[
-            pltpu.VMEM((chunks, width, chunk), BF16), pltpu.VMEM((chunks, chunk, width), BF16),
-            pltpu.VMEM((rows, width), BF16), pltpu.VMEM((rows, width), F32),
-            pltpu.VMEM((rows, chunk), BF16), pltpu.VMEM((rows, chunk), BF16),
+            vm(rows, width), pltpu.VMEM((rows, width), F32),
+            vm(slices - 1, up_part, chunk), vm(slices - 1, down_part, width),
+            vm(slices, width, chunk), vm(slices, chunk, width),
+            vm(rows, width), pltpu.VMEM((rows, width), F32), vm(rows, chunk), vm(rows, chunk),
         ]
-        + scatter_scratch(chunks, up_part, chunk)
-        + scatter_scratch(chunks, down_part, width)
-        + dma((late, 9), (late, 9), (late,), (chunks, 5), (chunks, 5), (chunks, 5), (chunks, 5), (2 * ahead,)),
+        + scatter_scratch(slices, up_part, chunk)
+        + scatter_scratch(slices, down_part, width)
+        + dma((late, 17), (late, 17), (late,), (slices, 5), (slices, 5), (slices, 5), (slices, 5), (2 * ahead,),
+              (4 + rows // 256,)),
         compiler_params=pltpu.CompilerParams(
             vmem_limit_bytes=VMEM_LIMIT, collective_id=2, has_side_effects=True
         ),
@@ -998,16 +1097,17 @@
 
 def back_comm_kernel(
     block, tile, group,
-    length_ref, pass_ref, inputs, rows_in, out_w, log_rows, attended, hidden_grad, mlp_gain_grad,
-    up_done, down_done, up_half, down_half, qkv_in, joined_in,
-    grad_input, small_sum, up_total, down_total, attn_total,
+    length_ref, pass_ref, rows_in, log_rows, mlp_gain_grad, up_done, down_done, up_half, down_half,
+    hidden_grad_in, out_in, attended_in, normed_in, joined_in, qkv_in, inputs_in,
+    grad_input_out, small_sum, up_total, down_total, attn_total,
+    hidden_grad, out_w, attended, inputs, grad_input,
     qkv_w, joined, branch_grad, attended_grad, normed, joined_grad, key_bias, key_total, value_total,
     grads, first, in_x, in_y, last, block_sum,
     up_x, up_y, up_last, up_block, down_x, down_y, down_last, down_block,
     up_in, up_mid, up_out, down_in, down_mid, down_out, attn_in, attn_mid, attn_out,
     small_own, small_slots, small_plane, small_reps,
     sends, recvs, up_sends, up_recvs, down_sends, down_recvs, z_sends, z_recvs,
-    plane_sends, plane_recvs, rep_sends, rep_recvs, loads,
+    plane_sends, plane_recvs, rep_sends, rep_recvs, loads, saves,
 ):
     place = Place()
     rows, width = inputs.shape
@@ -1019,13 +1119,16 @@
     per_group = group // PAIR
     others = [lax.rem(place.me + shift, shards) for shift in range(1, shards)]
     others_z = [lax.rem(place.z + shift, reps) for shift in range(1, reps)]
-    enter(place, others, others_z)
     take = [
-        pltpu.make_async_copy(joined_in, joined, loads.at[0]),
-        pltpu.make_async_copy(qkv_in, qkv_w, loads.at[1]),
+        pltpu.make_async_copy(source, target, loads.at[index])
+        for index, (source, target) in enumerate((
+            (hidden_grad_in, hidden_grad), (out_in, out_w), (attended_in, attended), (joined_in, joined),
+            (normed_in, normed), (qkv_in, qkv_w), (inputs_in, inputs),
+        ))
     ]
     for copy in take:
         copy.start()
+    enter(place, others, others_z)
 
     up_late = Scatter(place, None, up_half, up_x, up_y, up_last, up_sends, up_recvs, 0)
     down_late = Scatter(place, None, down_half, down_x, down_y, down_last, down_sends, down_recvs, 0)
@@ -1061,7 +1164,8 @@
         lines["u", index].begin()
 
     fill_bias(length_ref[0], key_bias)
-    norm_rows(inputs, rows_in[0:1, :], rows_in[1:2, :], normed)
+    take[0].wait()
+    take[1].wait()
 
     @pl.loop(0, rows // tile)
     def _(step):
@@ -1071,10 +1175,11 @@
         attended_grad[at, :] = mm(shown, out_w[...], NT).astype(BF16)
 
     lines["d", 0].cross()
-    down_late.fold()
+    take[2].wait()
     grads[0] = mm(attended[...], branch_grad[...], TN).astype(BF16).reshape(grads.shape[1:])
     out_msg.swap()
-    for copy in take:
+    down_late.fold()
+    for copy in take[3:]:
         copy.wait()
 
     def late_close(message, target, key):
@@ -1090,16 +1195,15 @@
         message(index).spread()
 
     after_pair = [
-        lambda: (lines["u", 0].cross(), send(0), up_late.fold(), lines["d", 1].cross()),
-        lambda: (late_close(down_late, down_block, ("d", 2)), lines["u", 1].cross(), lines["d", 0].settle(),
-                 lines["u", 0].settle(), out_msg.fold()),
-        lambda: (send(1), late_close(up_late, up_block, ("u", 2)), lines["d", 2].cross(), lines["d", 1].settle(),
-                 lines["u", 1].settle(), lines["d", 0].finish(), lines["u", 0].finish()),
-        lambda: (close(0), qkv_msg[0].fold(), lines["u", 2].cross(), lines["d", 2].settle(),
-                 lines["d", 1].finish(), lines["u", 1].finish()),
-        lambda: (send(2), close(1), lines["a", 0].cross(), lines["u", 2].settle()),
-        lambda: (qkv_msg[1].fold(), lines["a", 1].cross(), lines["a", 0].settle(), lines["d", 2].finish(),
-                 lines["u", 2].finish()),
+        lambda: (lines["u", 0].cross(), up_late.fold(), send(0), lines["d", 0].settle()),
+        lambda: (lines["d", 1].cross(), lines["u", 1].cross(), late_close(down_late, down_block, ("d", 2)),
+                 late_close(up_late, up_block, ("u", 2)), lines["u", 0].settle(), out_msg.fold()),
+        lambda: (send(1),),
+        lambda: (lines["d", 1].settle(), lines["u", 1].settle(), lines["d", 2].cross(), lines["u", 2].cross(),
+                 close(0), qkv_msg[0].fold()),
+        lambda: (send(2), close(1)),
+        lambda: (lines["a", 0].cross(), lines["d", 2].settle(), lines["u", 2].settle(), lines["a", 1].cross(),
+                 qkv_msg[1].fold()),
     ]
 
     @pl.loop(0, pairs)
@@ -1134,11 +1238,12 @@
 
         @pl.when(step == 1)
         def _():
-            lines["a", 1].settle()
-
-        @pl.when(step == 2)
+            lines["a", 0].settle()
+
+        @pl.when(step == 3)
         def _():
             qkv_msg[2].fold()
+            lines["a", 1].settle()
             lines["a", 2].cross()
 
     @pl.loop(0, rows // 256)
@@ -1152,9 +1257,9 @@
         grad_input[at, :] = total
         small_own[5:6, :] += jnp.sum(grad * unit, axis=0, keepdims=True)
         small_own[0:1, :] += jnp.sum(total, axis=0, keepdims=True)
+        pltpu.make_async_copy(grad_input.at[at, :], grad_input_out.at[at, :], saves.at[step]).start()
         after_rows(step)
 
-    close(3)
     places = lax.broadcasted_iota(jnp.int32, small_own.shape, 0)
     own = small_own[...]
     table = jnp.where((places == pass_ref[0]) & (places < 5), own[0:1], 0.0)
@@ -1167,8 +1272,8 @@
     ]
     for copy in plane_copies:
         copy.start()
+    close(3)
     lines["a", 2].settle()
-    lines["a", 3].cross()
     for copy in plane_copies:
         copy.wait_recv()
     total = small_slots[0]
@@ -1182,25 +1287,29 @@
     ]
     for copy in rep_copies:
         copy.start()
-    lines["a", 3].settle()
+    lines["a", 3].cross()
     for copy in rep_copies:
         copy.wait_recv()
     total = small_reps[0]
     for rep in range(1, reps):
         total = total + small_reps[rep]
     small_sum[...] = total
-    for index in range(1 + groups):
-        lines["a", index].finish()
+    lines["a", 3].settle()
+    for key in lines:
+        lines[key].finish()
     for index in range(1 + groups):
         message(index).drain()
     up_late.drain(swapped=False)
     down_late.drain(swapped=False)
     for copy in plane_copies + rep_copies:
         copy.wait_send()
-
-
-def back_comm(reps, seq_lens, pass_idx, inputs, rows_in, out_w, log_rows, attended, hidden_grad, mlp_gain_grad,
-              up_done, down_done, up_half, down_half, qkv_w, joined):
+    for step in range(rows // 256):
+        at = pl.ds(step * 256, 256)
+        pltpu.make_async_copy(grad_input.at[at, :], grad_input_out.at[at, :], saves.at[step]).wait()
+
+
+def back_comm(reps, seq_lens, pass_idx, rows_in, log_rows, mlp_gain_grad, up_done, down_done, up_half, down_half,
+              hidden_grad, out_w, attended, normed, joined, qkv_w, inputs):
     rows, width = inputs.shape
     _, _, up_part, chunk = up_half.shape
     down_part = down_half.shape[2]
@@ -1210,17 +1319,19 @@
     count = 1 + width // group
     wide = 3 * group
     vm = lambda *shape: pltpu.VMEM(shape, BF16)
+    vf = lambda *shape: pltpu.VMEM(shape, F32)
     return pl.pallas_call(
         functools.partial(back_comm_kernel, 256, 512, group),
         out_shape=[
             shaped((rows, width), F32), shaped((8, width), F32), shaped((chunks, up_part, chunk), BF16),
             shaped((chunks, down_part, width), BF16), shaped((count, up_part, wide), BF16),
         ],
-        in_specs=smem_spec(2) + vmem_spec(11) + any_spec(2),
-        out_specs=vmem_spec(5),
+        in_specs=smem_spec(2) + vmem_spec(7) + any_spec(7),
+        out_specs=any_spec(1) + vmem_spec(4),
         scratch_shapes=[
+            vf(rows, width), vm(width, width), vm(rows, width), vm(rows, width), vf(rows, width),
             vm(3, width, width), vm(3, rows, width), vm(rows, width), vm(rows, width), vm(rows, width),
-            vm(3, rows, width), vm(rows, PAIR), pltpu.VMEM((rows, PAIR), F32), pltpu.VMEM((rows, PAIR), F32),
+            vm(3, rows, width), vm(rows, PAIR), vf(rows, PAIR), vf(rows, PAIR),
         ]
         + scatter_scratch(count, up_part, wide)
         + [
@@ -1231,54 +1342,121 @@
         + [vm(chunks, up_part, chunk)] * 3
         + [vm(chunks, down_part, width)] * 3
         + [vm(count, up_part, wide)] * 3
-        + [
-            pltpu.VMEM((8, width), F32), pltpu.VMEM((shards, 8, width), F32), pltpu.VMEM((8, width), F32),
-            pltpu.VMEM((reps, 8, width), F32),
-        ]
+        + [vf(8, width), vf(shards, 8, width), vf(8, width), vf(reps, 8, width)]
         + dma((count, 5), (count, 5), (1, 5), (1, 5), (1, 5), (1, 5), (2 * chunks + count, 3), (2 * chunks + count, 3),
-              (shards - 1,), (shards - 1,), (reps - 1,), (reps - 1,), (2,)),
+              (shards - 1,), (shards - 1,), (reps - 1,), (reps - 1,), (7,), (rows // 256,)),
         compiler_params=pltpu.CompilerParams(
             vmem_limit_bytes=VMEM_LIMIT, collective_id=3, has_side_effects=True
         ),
-    )(seq_lens, pass_idx, inputs, rows_in, out_w, log_rows, attended, hidden_grad, mlp_gain_grad,
-      up_done, down_done, up_half, down_half, qkv_w, joined)
+    )(seq_lens, pass_idx, rows_in, log_rows, mlp_gain_grad, up_done, down_done, up_half, down_half,
+      hidden_grad, out_w, attended, normed, joined, qkv_w, inputs)
+
+
+def place_kernel(
+    small_sum, outputs_in, grad_input_in, up_in, down_in, attn_in,
+    table_out, attn_gain_out, mlp_gain_out, outputs_out, grad_input_out, qkv_out, out_out, up_out, down_out,
+    outputs, grad_input, up_total, down_total, attn_total, qkv, out, up, down, loads, saves,
+):
+    slices, part, chunk = up_in.shape
+    width = small_sum.shape[1]
+    shards = width // part
+    lanes = chunk // shards
+    groups = attn_in.shape[0] - 1
+    group = attn_in.shape[2] // 3
+    take = [
+        pltpu.make_async_copy(source, target, loads.at[index])
+        for index, (source, target) in enumerate((
+            (grad_input_in, grad_input), (up_in, up_total), (attn_in, attn_total), (down_in, down_total),
+            (outputs_in, outputs),
+        ))
+    ]
+    give = [
+        pltpu.make_async_copy(source, target, saves.at[index])
+        for index, (source, target) in enumerate((
+            (grad_input, grad_input_out), (up, up_out), (qkv, qkv_out), (out, out_out), (down, down_out),
+            (outputs, outputs_out),
+        ))
+    ]
+    for copy in take:
+        copy.start()
+    first = lax.axis_index("shard") * part
+    rows_at = lax.broadcasted_iota(jnp.int32, (width, part), 0)
+    lanes_at = lax.broadcasted_iota(jnp.int32, (width, part), 1)
+    chosen = (rows_at == lanes_at + first).astype(F32)
+    own = lax.dot_general(small_sum[...], chosen, NN, precision=lax.Precision.HIGHEST, preferred_element_type=F32)
+    table_out[...] = own[0 : table_out.shape[0]]
+    attn_gain_out[...] = own[5:6]
+    mlp_gain_out[...] = own[6:7]
+    take[0].wait()
+    give[0].start()
+    take[1].wait()
+    for index in range(slices):
+        for shard in range(shards):
+            up[:, (slices * shard + index) * lanes : (slices * shard + index + 1) * lanes] = up_total[
+                index, :, shard * lanes : (shard + 1) * lanes
+            ].astype(F32)
+    give[1].start()
+    take[2].wait()
+    for index in range(groups):
+        for plane in range(3):
+            start = plane * width + index * group
+            qkv[:, start : start + group] = attn_total[1 + index, :, plane * group : (plane + 1) * group].astype(F32)
+    out[...] = attn_total[0].astype(F32)
+    give[2].start()
+    give[3].start()
+    take[3].wait()
+    count = down_total.shape[1]
+    for index in range(slices):
+        down[index * count : (index + 1) * count, :] = down_total[index].astype(F32)
+    give[4].start()
+    take[4].wait()
+    give[5].start()
+    for copy in give:
+        copy.wait()
+
+
+def finish_places(passes, small_sum, outputs, grad_input, up_total, down_total, attn_total):
+    rows, width = outputs.shape
+    slices, part, chunk = up_total.shape
+    down_rows = slices * down_total.shape[1]
+    vf = lambda *shape: pltpu.VMEM(shape, F32)
+    like = lambda ref: pltpu.VMEM(ref.shape, ref.dtype)
+    return pl.pallas_call(
+        place_kernel,
+        out_shape=[
+            shaped((passes, part), F32), shaped((1, part), F32), shaped((1, part), F32), shaped((rows, width), BF16),
+            shaped((rows, width), F32), shaped((part, 3 * width), F32), shaped((part, width), F32),
+            shaped((part, slices * chunk), F32), shaped((down_rows, width), F32),
+        ],
+        in_specs=vmem_spec(1) + any_spec(5),
+        out_specs=vmem_spec(3) + any_spec(6),
+        scratch_shapes=[
+            like(outputs), like(grad_input), like(up_total), like(down_total), like(attn_total),
+            vf(part, 3 * width), vf(part, width), vf(part, slices * chunk), vf(down_rows, width),
+        ]
+        + dma((5,), (6,)),
+        compiler_params=pltpu.CompilerParams(vmem_limit_bytes=VMEM_LIMIT),
+    )(small_sum, outputs, grad_input, up_total, down_total, attn_total)
 
 
 def direct(reps, inputs, seq_lens, pass_idx, pass_table, gain_attn, w_qkv, w_out, gain_mlp, w_up, w_down, cotangent):
-    _, rows, width = inputs.shape
-    me = lax.axis_index("shard")
-    part = w_out.shape[0]
-    shards = width // part
     slices = 3
-    passes = pass_table.shape[0]
-    lanes = w_up.shape[1] // (slices * shards)
-    own = jnp.concatenate(
-        [pass_table, jnp.zeros((8 - passes, part), BF16), gain_attn[None], gain_mlp[None], jnp.zeros((6, part), BF16)]
-    )
-    small = jnp.where(jnp.arange(width)[None, :] // part == me, jnp.tile(own, (1, shards)), BF16(0))
-    qkv = w_qkv.reshape(part, 3, width).transpose(1, 0, 2)
-    up = w_up.reshape(part, shards, slices, lanes).transpose(2, 0, 1, 3).reshape(slices, part, shards * lanes)
-    down = w_down.reshape(slices, w_down.shape[0] // slices, width)
     ahead = 2
-    rows_in, log_rows, joined, attended, hidden, qkv_w, out_w, up_have, down_have = front_comm(
-        ahead, seq_lens, pass_idx, inputs[0], small, qkv, w_out, up, down
+    rows_in, log_rows, normed, joined, attended, hidden, qkv_w, out_w, up_have, down_have = front_comm(
+        ahead, slices, seq_lens, pass_idx, inputs[0], pass_table, gain_attn[None], gain_mlp[None], w_qkv, w_out,
+        w_up, w_down,
     )
     outputs, hidden_grad, mlp_gain_grad, up_done, down_done, up_half, down_half = mlp_comm(
-        ahead, hidden, cotangent[0], rows_in, up_have, down_have, up, down
+        ahead, slices, hidden, cotangent[0], rows_in, up_have, down_have, w_up, w_down
     )
     grad_input, small_sum, up_total, down_total, attn_total = back_comm(
-        reps, seq_lens, pass_idx, inputs[0], rows_in, out_w, log_rows, attended, hidden_grad, mlp_gain_grad,
-        up_done, down_done, up_half, down_half, qkv_w, joined,
+        reps, seq_lens, pass_idx, rows_in, log_rows, mlp_gain_grad, up_done, down_done, up_half, down_half,
+        hidden_grad, out_w, attended, normed, joined, qkv_w, inputs[0],
     )
-    small_own = lax.dynamic_slice(small_sum, (0, me * part), (8, part))
-    up_grad = up_total.reshape(slices, part, shards, lanes).transpose(1, 2, 0, 3).reshape(w_up.shape)
-    down_grad = down_total.reshape(w_down.shape)
-    group = attn_total.shape[2] // 3
-    qkv_grad = attn_total[1:].reshape(width // group, part, 3, group).transpose(1, 2, 0, 3).reshape(w_qkv.shape)
-    return (
-        outputs[None], grad_input[None], small_own[:passes], small_own[5], qkv_grad.astype(F32),
-        attn_total[0].astype(F32), small_own[6], up_grad.astype(F32), down_grad.astype(F32),
+    table, attn_gain, mlp_gain, outputs, grad_input, qkv, out, up, down = finish_places(
+        pass_table.shape[0], small_sum, outputs, grad_input, up_total, down_total, attn_total
     )
+    return (outputs[None], grad_input[None], table, attn_gain[0], qkv, out, mlp_gain[0], up, down)
 
 
 def solution(mesh):

time: 238 us -> 208 us (0.87)
  local copies, waits for them, and re-layouts: 17.4 us -> 0 us
  Pallas kernels: 214 us -> 205 us
  other arithmetic: 4.48 us -> 0 us
    pallas_call x1, Pallas kernels: 87.7 us -> 75 us  [back_comm(): pl.pallas_call(functools.partial(back_comm_kernel, 256, 512, group), out_...]
    unnamed x13 -> x0, local copies, waits for them, and re-layouts: 4.97 us -> none
    convert_element_type x5 -> x0, local copies, waits for them, and re-layouts: 4.89 us -> none  [the longest x3 2.6 us: direct(): qkv_grad.astype(F32)]
    reshape x3 -> x0, local copies, waits for them, and re-layouts: 4.69 us -> none  [the longest x2 2.89 us: direct(): w_up.reshape(part, shards, slices, lanes).transpose(2, 0, 1, 3)]
    convert_element_type x3 -> x0, other arithmetic: 3.85 us -> none  [the longest x1 1.64 us: direct(): attn_total[0].astype(F32)]
    pallas_call x1 -> x2, Pallas kernels: 59.1 us -> 62.9 us  [the longest x1 56.3 us: mlp_comm(): pl.pallas_call(functools.partial(mlp_comm_kernel, ahead, 512, shards), ou...]
where the time goes in v3:
time: 208 us; the launch traced here: 207 us
  Pallas kernels  205 us (99%)
  between operations  2.14 us (1%)
    pallas_call x1, Pallas kernels, back_comm(): pl.pallas_call(functools.partial(back_comm_kernel, 256, 512, group), out_...  75 us
    pallas_call x1, Pallas kernels, front_comm(): pl.pallas_call(functools.partial(front_comm_kernel, ahead, 256, 512, grou...  67.4 us
    pallas_call x1, Pallas kernels, mlp_comm(): pl.pallas_call(functools.partial(mlp_comm_kernel, ahead, 512, shards), ou...  56.3 us
    pallas_call x1, Pallas kernels, finish_places(): pl.pallas_call(place_kernel, out_shape=[shaped((passes, part), F32), shap...  6.6 us

profile of v3, /device:TPU:0, one launch (start us, length us, event | category | flops | bytes accessed | tf_op | source)
XLA Modules:
  0.0 207.4 jit_solution(9665299762639406023)
XLA Ops:
  1.9 67.4 %shard_map.178 = (f32[8,768]{1,0:T(8,128)}, f32[16,1024]{1,0:T(8,128)}, bf16[1024,768]{1,0:T(8,128)(2,1)}, bf16[3,1024,768]{2,1,0:T(8,128)(2,1)}, bf16[1024,768]...) custom-call(s32[1]{0:T(128)S(6)} %copy.20.length_ref, ...), custom_call_target="tpu_custom_call" | custom-call | tf_op jit(solution)/shard_map/pallas_call | solution.py:700
  69.3 56.3 %shard_map.179 = (bf16[1024,768]{1,0:T(8,128)(2,1)}, f32[1024,768]{1,0:T(8,128)}, f32[8,768]{1,0:T(8,128)}, bf16[2,96,1024]{2,1,0:T(8,128)(2,1)}, bf16[2,128,768...) custom-call(f32[1024,768]{1,0:T(8,128)} %get-tuple-element.42.hidden, ...), custom_call_target="tpu_custom_call" | custom-call | tf_op jit(solution)/shard_map/pallas_call | solution.py:986
  125.6 75.0 %shard_map.180 = (f32[1024,768]{1,0:T(8,128)}, f32[8,768]{1,0:T(8,128)}, bf16[3,96,1024]{2,1,0:T(8,128)(2,1)}, bf16[3,128,768]{2,1,0:T(8,128)(2,1)}, bf16[4,96,768]{2,1,0:T(8,128)(2,1)}) custom-call(s32[1]{0:T(128)S(6)} %copy.20.length_ref, s32[1]{0:T(128)S(6)} %copy.21.pass_ref, f32[8,768]{1,0:T(8,128)} %get-tuple-element.40.rows_in, ...), custom_call_target="tpu_custom_call" | custom-call | tf_op jit(solution)/shard_map/pallas_call | solution.py:1323
  200.7 6.6 %shard_map.181 = (f32[5,96]{1,0:T(8,128)}, f32[1,96]{1,0:T(1,128)}, f32[1,96]{1,0:T(1,128)}, bf16[1024,768]{1,0:T(8,128)(2,1)}, f32[1024,768]{1,0:T(8,128)}, /*i...) custom-call(f32[8,768]{1,0:T(8,128)} %get-tuple-element.56.small_sum, ...), custom_call_target="tpu_custom_call" | custom-call | tf_op jit(solution)/shard_map/pallas_call | solution.py:1424

commit v4 on v3

--- a/solution.py
+++ b/solution.py
@@ -483,16 +483,20 @@
     return [(own.at[pl.ds(index * count, count), :], ref.at[index, rows, :])]
 
 
-def attention_rows(joined, attended, log_rows, key_bias, pair, block):
-    rows = attended.shape[0]
-    columns = pl.ds(pl.multiple_of(pair * PAIR, PAIR), PAIR)
-    keys = joined[1, :, columns]
-    values = joined[2, :, columns]
+def pair_columns(pair, width):
+    return [pl.ds(pl.multiple_of(plane * width + pair * PAIR, PAIR), PAIR) for plane in range(3)]
+
+
+def attention_rows(joined, attended, log_rows, key_bias, pair, block, between):
+    rows, width = attended.shape
+    columns, key_columns, value_columns = pair_columns(pair, width)
+    keys = joined[:, key_columns]
+    values = joined[:, value_columns]
     bias = key_bias[...]
     biased = [key_with_bias(keys, bias, head)[0] for head in range(2)]
     for first in range(0, rows, block):
         live = first + block
-        query = joined[0, pl.ds(first, block), columns]
+        query = joined[pl.ds(first, block), columns]
         mixed = []
         sums = []
         for head in range(2):
@@ -512,6 +516,7 @@
         turned = jnp.transpose(jnp.where(lanes < HEAD_DIM, sums[0], sums[1]))
         log_rows[pl.ds(pair * 2, 1), pl.ds(first, block)] = turned[0:1]
         log_rows[pl.ds(pair * 2 + 1, 1), pl.ds(first, block)] = turned[HEAD_DIM : HEAD_DIM + 1]
+        between(first // block)
 
 
 def norm_rows(inputs, pass_row, gain, normed):
@@ -530,19 +535,52 @@
 
 SHARED = (False, True, True, False, True, True, False, True, True, False)
 
-
-def front_comm_kernel(
-    ahead, block, tile, group,
-    length_ref, pass_ref, inputs, table_own, attn_gain_own, mlp_gain_own, qkv_own, out_own, up_own, down_own,
-    rows_out, log_out, normed_out, joined_out, attended_out, hidden_out, qkv_out, out_out, up_out, down_out,
-    slots, small_wide, small_own, normed, joined, attended, hidden, qkv_w, out_w, up_w, down_w, key_bias,
-    sends, recvs, local, small_sends, small_recvs, saves,
+PLAN = {
+    "begin": "r0 s2",
+    "normed": "f0 r1",
+    (0, 0): "s3",
+    (0, 1): "f1",
+    (0, 2): "r2",
+    (0, 3): "s4",
+    (1, 2): "a1",
+    (1, 3): "r3 f2",
+    (2, 0): "s5",
+    (2, 1): "r4",
+    (2, 3): "a2 f3",
+    (3, 0): "s6",
+    (3, 3): "f4 r5",
+    (4, 0): "s7",
+    (4, 3): "a4 f5 r6",
+    (5, 0): "s8",
+    (5, 3): "r7",
+    "row 1": "a5 f6 s9",
+    "mlp 0 0": "f7 r8",
+    "mlp 0 1": "r9",
+    "mlp 0 down": "a7 f8",
+    "mlp 0 up": "f9",
+    "mlp 1 0": "a8",
+}
+
+
+def fore_comm_kernel(
+    block, tile, group, slices,
+    length_ref, pass_ref, table_own, attn_gain_own, mlp_gain_own,
+    inputs_in, cotangent_in, qkv_own, out_own, up_own, down_own,
+    rows_out, log_out, gain_grad,
+    up_half, down_half, normed_out, joined_out, attended_out, qkv_out, out_out, outputs_out, hidden_grad_out,
+    up_done_out, down_done_out,
+    inputs, cotangent, slots, small_wide, small_own, normed, joined, attended, hidden, qkv_w, out_w, up_w, down_w,
+    key_bias, mixed, hidden_grad, up_done, down_done,
+    up_grads, up_first, up_x, up_y, up_last, down_grads, down_first, down_x, down_y, down_last,
+    sends, recvs, local, small_sends, small_recvs, up_sends, up_recvs, down_sends, down_recvs, loads, saves,
 ):
     place = Place()
     rows, width = inputs.shape
     shards = slots.shape[0]
     part = qkv_own.shape[0]
     groups = width // group
+    pairs = width // PAIR
+    per_group = group // PAIR
 
     pieces = []
 
@@ -559,13 +597,19 @@
         ]
         add(part_of(qkv_w, part, (slice(None),), index * group, group), fills)
     add(part_of(out_w, part, (), 0, width), [(out_own, out_w.at[own_rows, :])])
-    for index in range(ahead):
+    for index in range(slices):
         add(part_of(up_w, part, (index,), 0, up_w.shape[2]), up_fills(up_own, up_w, index, place, shards))
         add(part_of(down_w, down_w.shape[1] // shards, (index,), 0, width),
             down_fills(down_own, down_w, index, place, shards))
     count = len(pieces)
-    for piece in pieces:
+    take = [
+        pltpu.make_async_copy(inputs_in, inputs, loads.at[0]), pltpu.make_async_copy(cotangent_in, cotangent, loads.at[1]),
+    ]
+    pieces[0].fill()
+    take[0].start()
+    for piece in pieces[1:]:
         piece.fill()
+    take[1].start()
 
     chosen = select_lanes(place, part, width).astype(BF16)
     small_wide[...] = jnp.zeros_like(small_wide)
@@ -586,15 +630,22 @@
         copy.start()
     pieces[1].start()
 
-    def tick(index):
-        if index < count:
-            pieces[index].relay()
-        if index + 2 < count:
-            pieces[index + 2].start()
-        if 0 <= index - 1 < count:
-            pieces[index - 1].finish()
-        if 0 <= index - 2 < count:
-            pieces[index - 2].across()
+    def step_on(point):
+        for what in PLAN.get(point, "").split():
+            piece = pieces[int(what[1:])]
+            {"s": piece.start, "r": piece.relay, "f": piece.finish, "a": piece.across}[what[0]]()
+
+    def up_message(index):
+        return Scatter(
+            place, up_grads.at[lax.rem(index, 2)], up_first.at[index], up_x.at[index], up_y.at[index], up_last.at[index],
+            up_sends, up_recvs, index,
+        )
+
+    def down_message(index):
+        return Scatter(
+            place, down_grads.at[lax.rem(index, 2)], down_first.at[index], down_x.at[index], down_y.at[index], down_last.at[index],
+            down_sends, down_recvs, index,
+        )
 
     fill_bias(length_ref[0], key_bias)
     for copy in smalls:
@@ -607,23 +658,18 @@
     rows_out[1:3, :] = total[8:10]
     rows_out[3:8, :] = jnp.zeros((5, width), F32)
 
-    tick(0)
+    take[0].wait()
+    step_on("begin")
     norm_rows(inputs, rows_out[0:1, :], rows_out[1:2, :], normed)
-    tick(1)
-
-    keep = []
-
-    def save(source, target):
-        keep.append(pltpu.make_async_copy(source, target, saves.at[len(keep)]))
-        return keep[-1]
-
-    save(normed, normed_out).start()
-    pairs = width // PAIR
-    per_group = group // PAIR
-    joined_saves = [
-        save(joined.at[:, :, pl.ds(index * group, group)], joined_out.at[:, :, pl.ds(index * group, group)])
-        for index in range(groups)
-    ]
+    step_on("normed")
+
+    keep = {}
+
+    def save(source, target, name=None):
+        keep[name or len(keep)] = copy = pltpu.make_async_copy(source, target, saves.at[len(keep)])
+        return copy
+
+    save(normed, normed_out, "normed").start()
     qkv_save = save(qkv_w, qkv_out)
 
     @pl.loop(0, pairs)
@@ -641,37 +687,152 @@
 
             @pl.loop(0, 3)
             def _(plane):
-                joined[plane, :, columns] = mm(normed[...], qkv_w[plane, :, columns]).astype(BF16)
-
-        attention_rows(joined, attended, log_out, key_bias, pair, block)
-        for index in range(pairs):
-            @pl.when(pair == index)
-            def _(index=index):
-                if index % per_group == 0:
-                    joined_saves[index // per_group].start()
-                tick(index + 2)
-
-    save(attended, attended_out).start()
+                target = pl.ds(pl.multiple_of(plane * width + pair * PAIR, group), group)
+                joined[:, target] = mm(normed[...], qkv_w[plane, :, columns]).astype(BF16)
+
+        def between(place_at):
+            for index in range(pairs):
+                if (index, place_at) in PLAN:
+                    @pl.when(pair == index)
+                    def _(index=index):
+                        step_on((index, place_at))
+
+        attention_rows(joined, attended, log_out, key_bias, pair, block, between)
+
+    chunk = up_w.shape[2]
+    second = attended
+    active, rising_grad = joined.at[:, pl.ds(0, chunk)], joined.at[:, pl.ds(chunk, chunk)]
+    save(attended, attended_out, "attended").start()
+    save(joined, joined_out, "joined").start()
     pieces[groups].ready()
     save(out_w, out_out).start()
+    gain = rows_out[2:3, :]
     for step in range(rows // tile):
         at = pl.ds(step * tile, tile)
         entered = inputs[at, :].astype(F32) + rows_out[0:1, :]
         hidden[at, :] = entered + mm(attended[at, :], out_w[...])
-        save(hidden.at[at, :], hidden_out.at[at, :]).start()
-        tick(pairs + 2 + step)
-    for index in range(pairs + 2 + rows // tile, count + 2):
-        tick(index)
-    late = [(ref.at[index], target.at[index]) for index in range(ahead) for ref, target in ((up_w, up_out), (down_w, down_out))]
-    for piece, (source, target) in zip(pieces[groups + 1 :], late):
-        piece.ready()
-        save(source, target).start()
+        step_on("row %d" % step)
+        if step == 0:
+            keep["attended"].wait()
+
+        @pl.loop(0, tile // 256)
+        def _(step_in):
+            at = pl.ds(step * tile + step_in * 256, 256)
+            values = hidden[at, :]
+            second[at, :] = (norm_parts(values)[0] * gain).astype(BF16)
+            mixed[at, :] = values
+            hidden_grad[at, :] = jnp.zeros((256, width), F32)
+
+    take[1].wait()
+    keep["joined"].wait()
+
+    @pl.loop(0, slices)
+    def _(index_at):
+        for index in range(slices):
+            @pl.when(index_at == index)
+            def _(index=index):
+                pieces[groups + 1 + 2 * index].ready()
+                pieces[groups + 2 + 2 * index].ready()
+
+        @pl.loop(0, rows // tile)
+        def _(step):
+            at = pl.ds(step * tile, tile)
+            rising = mm(second[at, :], up_w[index_at])
+            active_grad = mm(cotangent[at, :], down_w[index_at], NT)
+            bent, slope = gelu_both(rising)
+            shown = bent.astype(BF16)
+            moved = (slope * active_grad).astype(BF16)
+            active[at, :] = shown
+            rising_grad[at, :] = moved
+            mixed[at, :] += mm(shown, down_w[index_at])
+            hidden_grad[at, :] += mm(moved, up_w[index_at], NT)
+
+            for index in range(slices):
+                for inner in range(rows // tile):
+                    if "mlp %d %d" % (index, inner) in PLAN:
+                        @pl.when((index_at == index) & (step == inner))
+                        def _(index=index, inner=inner):
+                            step_on("mlp %d %d" % (index, inner))
+
+            @pl.when((index_at > 0) & (step == 0))
+            def _():
+                message = up_message(index_at - 1)
+                message.merge()
+                message.spread()
+
+            @pl.when((index_at > 0) & (step == 1))
+            def _():
+                down_message(index_at - 1).fold()
+
+        @pl.when(index_at > 1)
+        def _():
+            down_message(index_at - 2).swap_copy().wait_send()
+            up_message(index_at - 2).swap_copy().wait_send()
+
+        slot = lax.rem(index_at, 2)
+        down_grads[slot] = mm(active[...], cotangent[...], TN).astype(BF16).reshape(down_grads.shape[1:])
+        down_message(index_at).swap()
+
+        @pl.when(index_at == 0)
+        def _():
+            step_on("mlp 0 down")
+
+        @pl.when(index_at > 0)
+        def _():
+            up_message(index_at - 1).fold()
+
+        up_grads[slot] = mm(second[...], rising_grad[...], TN).astype(BF16).reshape(up_grads.shape[1:])
+        up_message(index_at).swap()
+
+        @pl.when(index_at == 0)
+        def _():
+            step_on("mlp 0 up")
+
+        @pl.when(index_at < slices - 1)
+        def _():
+            message = down_message(index_at)
+            message.merge()
+            message.spread()
+
+        @pl.when(index_at > 0)
+        def _():
+            down_message(index_at - 1).close(down_done.at[index_at - 1])
+            up_message(index_at - 1).close(up_done.at[index_at - 1])
+
+    down_message(slices - 1).merge()
+    save(down_first.at[slices - 1], down_half).start()
+    save(up_done, up_done_out).start()
+    save(down_done, down_done_out).start()
+    gain_grad[...] = jnp.zeros_like(gain_grad)
+    keep["normed"].wait()
+    first_row = len(keep) + 2
+
+    @pl.loop(0, rows // 256)
+    def _(step):
+        at = pl.ds(step * 256, 256)
+        normed[at, :] = mixed[at, :].astype(BF16)
+        unit, scale = norm_parts(hidden[at, :])
+        grad = hidden_grad[at, :]
+        hidden_grad[at, :] = cotangent[at, :].astype(F32) + norm_back(unit, scale, grad, gain)
+        gain_grad[0:1, :] += jnp.sum(grad * unit, axis=0, keepdims=True)
+        pltpu.make_async_copy(hidden_grad.at[at, :], hidden_grad_out.at[at, :], saves.at[first_row + step]).start()
+
+    save(normed, outputs_out).start()
+    up_message(slices - 1).merge()
+    save(up_first.at[slices - 1], up_half).start()
+    for step in range(rows // 256):
+        at = pl.ds(step * 256, 256)
+        pltpu.make_async_copy(hidden_grad.at[at, :], hidden_grad_out.at[at, :], saves.at[first_row + step]).wait()
     for piece in pieces:
         piece.drain()
     for copy in smalls:
         copy.wait_send()
-    for copy in keep:
-        copy.wait()
+    for index in range(slices):
+        up_message(index).drain(index >= slices - 2, index < slices - 1)
+        down_message(index).drain(index >= slices - 2, index < slices - 1)
+    for name, copy in keep.items():
+        if name not in ("normed", "attended", "joined"):
+            copy.wait()
 
 
 def any_spec(count):
@@ -688,35 +849,6 @@
 
 def shaped(shape, kind):
     return jax.ShapeDtypeStruct(shape, kind)
-
-
-def front_comm(ahead, slices, seq_lens, pass_idx, inputs, table, attn_gain, mlp_gain, qkv, out, up, down):
-    rows, width = inputs.shape
-    shards = width // out.shape[0]
-    chunk = up.shape[1] // slices
-    group = 4 * HEAD_DIM
-    count = width // group + 1 + 2 * ahead
-    vm = lambda *shape: pltpu.VMEM(shape, BF16)
-    return pl.pallas_call(
-        functools.partial(front_comm_kernel, ahead, 256, 512, group),
-        out_shape=[
-            shaped((8, width), F32), shaped((16, rows), F32), shaped((rows, width), BF16),
-            shaped((3, rows, width), BF16), shaped((rows, width), BF16), shaped((rows, width), F32),
-            shaped((3, width, width), BF16), shaped((width, width), BF16), shaped((ahead, width, chunk), BF16),
-            shaped((ahead, chunk, width), BF16),
-        ],
-        in_specs=smem_spec(2) + vmem_spec(4) + any_spec(4),
-        out_specs=vmem_spec(2) + any_spec(8),
-        scratch_shapes=[
-            vm(shards, 16, width), pltpu.VMEM((16, width), F32), vm(16, width), vm(rows, width), vm(3, rows, width),
-            vm(rows, width), pltpu.VMEM((rows, width), F32), vm(3, width, width), vm(width, width),
-            vm(ahead, width, chunk), vm(ahead, chunk, width), vm(rows, PAIR),
-        ]
-        + dma((count, 17), (count, 17), (count,), (shards,), (shards,), (9 + width // group + 2 * ahead,)),
-        compiler_params=pltpu.CompilerParams(
-            vmem_limit_bytes=VMEM_LIMIT, collective_id=1, has_side_effects=True
-        ),
-    )(seq_lens, pass_idx, inputs, table, attn_gain, mlp_gain, qkv, out, up, down)
 
 
 class Scatter:
@@ -791,182 +923,9 @@
                 copy.wait_send()
 
 
-def mlp_comm_kernel(
-    ahead, tile, shards,
-    hidden, cotangent, rows_in, up_have, down_have, up_own, down_own,
-    outputs_out, hidden_grad_out, gain_grad, up_done_out, down_done_out, up_half, down_half,
-    outputs, hidden_grad, up_done, down_done, up_w, down_w, second, mixed, active, rising_grad,
-    up_grads, up_first, up_x, up_y, up_last, down_grads, down_first, down_x, down_y, down_last,
-    gather_sends, gather_recvs, gather_local, up_sends, up_recvs, down_sends, down_recvs, loads, saves,
-):
-    place = Place()
-    rows, width = hidden.shape
-    chunks, chunk = down_w.shape[0], down_w.shape[1]
-    gain = rows_in[2:3, :]
-
-    pieces = []
-    for index in range(ahead, chunks):
-        for kind in range(2):
-            row = len(pieces)
-            if kind == 0:
-                part_at = part_of(up_w, width // shards, (index,), 0, chunk)
-                fills = up_fills(up_own, up_w, index, place, shards)
-            else:
-                part_at = part_of(down_w, chunk // shards, (index,), 0, width)
-                fills = down_fills(down_own, down_w, index, place, shards)
-            pieces.append(
-                Gather(place, part_at, fills, gather_sends, gather_recvs, gather_local, row, SHARED[row + 4 + 2 * ahead])
-            )
-    for piece in pieces:
-        piece.fill()
-    have = []
-    for index in range(ahead):
-        for ref, weights in ((up_have, up_w), (down_have, down_w)):
-            have.append(pltpu.make_async_copy(ref.at[index], weights.at[index], loads.at[len(have)]))
-    for copy in have:
-        copy.start()
-    enter(place, [place.by_x, place.by_y, place.by_core], [place.by_z])
-    for piece in pieces:
-        piece.start()
-    keep = []
-
-    def save(source, target):
-        keep.append(pltpu.make_async_copy(source, target, saves.at[len(keep)]))
-        return keep[-1]
-
-    def up_message(index):
-        return Scatter(
-            place, up_grads.at[index], up_first.at[index], up_x.at[index], up_y.at[index], up_last.at[index],
-            up_sends, up_recvs, index,
-        )
-
-    def down_message(index):
-        return Scatter(
-            place, down_grads.at[index], down_first.at[index], down_x.at[index], down_y.at[index], down_last.at[index],
-            down_sends, down_recvs, index,
-        )
-
-    @pl.loop(0, rows // 256)
-    def _(step):
-        at = pl.ds(step * 256, 256)
-        second[at, :] = (norm_parts(hidden[at, :])[0] * gain).astype(BF16)
-        mixed[at, :] = hidden[at, :]
-        hidden_grad[at, :] = jnp.zeros((256, width), F32)
-
-    @pl.loop(0, chunks)
-    def _(part):
-        for index in range(ahead):
-            @pl.when(part == index)
-            def _(index=index):
-                have[2 * index].wait()
-                have[2 * index + 1].wait()
-        for index in range(ahead, chunks):
-            @pl.when(part == index)
-            def _(index=index):
-                pieces[2 * (index - ahead)].ready()
-                pieces[2 * (index - ahead) + 1].ready()
-
-        @pl.loop(0, rows // tile)
-        def _(step):
-            at = pl.ds(step * tile, tile)
-            rising = mm(second[at, :], up_w[part])
-            active_grad = mm(cotangent[at, :], down_w[part], NT)
-            bent, slope = gelu_both(rising)
-            shown = bent.astype(BF16)
-            moved = (slope * active_grad).astype(BF16)
-            active[at, :] = shown
-            rising_grad[at, :] = moved
-            mixed[at, :] += mm(shown, down_w[part])
-            hidden_grad[at, :] += mm(moved, up_w[part], NT)
-
-            @pl.when((part == 0) & (step == 0))
-            def _():
-                for piece in pieces[:2]:
-                    piece.relay()
-
-            @pl.when((part == 0) & (step == 1))
-            def _():
-                for piece in pieces[:2]:
-                    piece.finish()
-                for piece in pieces[2:]:
-                    piece.relay()
-
-            @pl.when((part == 1) & (step == 0))
-            def _():
-                for piece in pieces[2:]:
-                    piece.across()
-
-            @pl.when((part > 0) & (step == 0))
-            def _():
-                message = up_message(part - 1)
-                message.merge()
-                message.spread()
-
-            @pl.when((part > 0) & (step == 1))
-            def _():
-                down_message(part - 1).fold()
-
-        down_grads[part] = mm(active[...], cotangent[...], TN).astype(BF16).reshape(down_grads.shape[1:])
-        down_message(part).swap()
-
-        @pl.when(part == 0)
-        def _():
-            for piece in pieces[:2]:
-                piece.across()
-            for piece in pieces[2:]:
-                piece.finish()
-
-        @pl.when(part > 0)
-        def _():
-            up_message(part - 1).fold()
-
-        up_grads[part] = mm(second[...], rising_grad[...], TN).astype(BF16).reshape(up_grads.shape[1:])
-        up_message(part).swap()
-
-        @pl.when(part < chunks - 1)
-        def _():
-            message = down_message(part)
-            message.merge()
-            message.spread()
-
-        @pl.when(part > 0)
-        def _():
-            down_message(part - 1).close(down_done.at[part - 1])
-            up_message(part - 1).close(up_done.at[part - 1])
-
-    down_message(chunks - 1).merge(down_half)
-    save(up_done, up_done_out).start()
-    save(down_done, down_done_out).start()
-    gain_grad[...] = jnp.zeros_like(gain_grad)
-
-    @pl.loop(0, rows // 256)
-    def _(step):
-        at = pl.ds(step * 256, 256)
-        outputs[at, :] = mixed[at, :].astype(BF16)
-        unit, scale = norm_parts(hidden[at, :])
-        grad = hidden_grad[at, :]
-        hidden_grad[at, :] = cotangent[at, :].astype(F32) + norm_back(unit, scale, grad, gain)
-        gain_grad[0:1, :] += jnp.sum(grad * unit, axis=0, keepdims=True)
-        pltpu.make_async_copy(hidden_grad.at[at, :], hidden_grad_out.at[at, :], saves.at[4 + step]).start()
-
-    save(outputs, outputs_out).start()
-    for step in range(rows // 256):
-        at = pl.ds(step * 256, 256)
-        pltpu.make_async_copy(hidden_grad.at[at, :], hidden_grad_out.at[at, :], saves.at[4 + step]).wait()
-
-    up_message(chunks - 1).merge(up_half)
-    for piece in pieces:
-        piece.drain()
-    for index in range(chunks):
-        up_message(index).drain(True, index < chunks - 1)
-        down_message(index).drain(True, index < chunks - 1)
-    for copy in keep:
-        copy.wait()
-
-
-def scatter_scratch(count, part, columns):
+def scatter_scratch(count, part, columns, slots=None):
     return [
-        pltpu.VMEM((count, 2, 2, 2, part, columns), BF16), pltpu.VMEM((count, 2, 2, part, columns), BF16),
+        pltpu.VMEM((slots or count, 2, 2, 2, part, columns), BF16), pltpu.VMEM((count, 2, 2, part, columns), BF16),
         pltpu.VMEM((count, 2, part, columns // 2), BF16), pltpu.VMEM((count, 2, part, columns // 2), BF16),
         pltpu.VMEM((count, part, columns), BF16),
     ]
@@ -976,36 +935,42 @@
     return [pltpu.SemaphoreType.DMA(shape) for shape in shapes]
 
 
-def mlp_comm(ahead, slices, hidden, cotangent, rows_in, up_have, down_have, up, down):
-    rows, width = hidden.shape
+def fore_comm(slices, seq_lens, pass_idx, table, attn_gain, mlp_gain, inputs, cotangent, qkv, out, up, down):
+    rows, width = inputs.shape
     up_part, chunk = up.shape[0], up.shape[1] // slices
     down_part = down.shape[0] // slices
     shards = width // up_part
-    late = max(1, 2 * (slices - ahead))
+    group = 4 * HEAD_DIM
+    groups = width // group
+    count = groups + 1 + 2 * slices
     vm = lambda *shape: pltpu.VMEM(shape, BF16)
+    vf = lambda *shape: pltpu.VMEM(shape, F32)
     return pl.pallas_call(
-        functools.partial(mlp_comm_kernel, ahead, 512, shards),
+        functools.partial(fore_comm_kernel, 256, 512, group, slices),
         out_shape=[
-            shaped((rows, width), BF16), shaped((rows, width), F32), shaped((8, width), F32),
-            shaped((slices - 1, up_part, chunk), BF16), shaped((slices - 1, down_part, width), BF16),
+            shaped((8, width), F32), shaped((16, rows), F32), shaped((8, width), F32),
             shaped((2, 2, up_part, chunk), BF16), shaped((2, 2, down_part, width), BF16),
+            shaped((rows, width), BF16), shaped((rows, 3 * width), BF16), shaped((rows, width), BF16),
+            shaped((3, width, width), BF16), shaped((width, width), BF16), shaped((rows, width), BF16),
+            shaped((rows, width), F32), shaped((slices - 1, up_part, chunk), BF16),
+            shaped((slices - 1, down_part, width), BF16),
         ],
-        in_specs=vmem_spec(3) + any_spec(4),
-        out_specs=any_spec(2) + vmem_spec(1) + any_spec(2) + vmem_spec(2),
+        in_specs=smem_spec(2) + vmem_spec(3) + any_spec(6),
+        out_specs=vmem_spec(3) + any_spec(11),
         scratch_shapes=[
-            vm(rows, width), pltpu.VMEM((rows, width), F32),
+            vm(rows, width), vm(rows, width), vm(shards, 16, width), vf(16, width), vm(16, width), vm(rows, width),
+            vm(rows, 3 * width), vm(rows, width), vf(rows, width), vm(3, width, width), vm(width, width),
+            vm(slices, width, chunk), vm(slices, chunk, width), vm(rows, PAIR), vf(rows, width), vf(rows, width),
             vm(slices - 1, up_part, chunk), vm(slices - 1, down_part, width),
-            vm(slices, width, chunk), vm(slices, chunk, width),
-            vm(rows, width), pltpu.VMEM((rows, width), F32), vm(rows, chunk), vm(rows, chunk),
         ]
-        + scatter_scratch(slices, up_part, chunk)
-        + scatter_scratch(slices, down_part, width)
-        + dma((late, 17), (late, 17), (late,), (slices, 5), (slices, 5), (slices, 5), (slices, 5), (2 * ahead,),
-              (4 + rows // 256,)),
+        + scatter_scratch(slices, up_part, chunk, 2)
+        + scatter_scratch(slices, down_part, width, 2)
+        + dma((count, 17), (count, 17), (count,), (shards,), (shards,), (slices, 5), (slices, 5), (slices, 5),
+              (slices, 5), (2,), (10 + rows // 256,)),
         compiler_params=pltpu.CompilerParams(
-            vmem_limit_bytes=VMEM_LIMIT, collective_id=2, has_side_effects=True
+            vmem_limit_bytes=VMEM_LIMIT, collective_id=1, has_side_effects=True
         ),
-    )(hidden, cotangent, rows_in, up_have, down_have, up, down)
+    )(seq_lens, pass_idx, table, attn_gain, mlp_gain, inputs, cotangent, qkv, out, up, down)
 
 
 class Column:
@@ -1060,17 +1025,17 @@
 
 
 def attention_columns(joined, log_rows, grads, joined_grad, key_bias, key_total, value_total, pair, block):
-    rows = grads.shape[0]
-    columns = pl.ds(pl.multiple_of(pair * PAIR, PAIR), PAIR)
-    keys = joined[1, :, columns]
-    values = joined[2, :, columns]
+    rows, width = grads.shape
+    columns, key_columns, value_columns = pair_columns(pair, width)
+    keys = joined[:, key_columns]
+    values = joined[:, value_columns]
     bias = key_bias[...]
     biased = [key_with_bias(keys, bias, head) for head in range(2)]
     key_total[...] = jnp.zeros_like(key_total)
     value_total[...] = jnp.zeros_like(value_total)
     for first in range(0, rows, block):
         live = first + block
-        query = joined[0, pl.ds(first, block), columns]
+        query = joined[pl.ds(first, block), columns]
         grad = grads[pl.ds(first, block), columns]
         query_grad = None
         for head in range(2):
@@ -1330,7 +1295,7 @@
         out_specs=any_spec(1) + vmem_spec(4),
         scratch_shapes=[
             vf(rows, width), vm(width, width), vm(rows, width), vm(rows, width), vf(rows, width),
-            vm(3, width, width), vm(3, rows, width), vm(rows, width), vm(rows, width), vm(rows, width),
+            vm(3, width, width), vm(rows, 3 * width), vm(rows, width), vm(rows, width), vm(rows, width),
             vm(3, rows, width), vm(rows, PAIR), vf(rows, PAIR), vf(rows, PAIR),
         ]
         + scatter_scratch(count, up_part, wide)
@@ -1441,13 +1406,12 @@
 
 def direct(reps, inputs, seq_lens, pass_idx, pass_table, gain_attn, w_qkv, w_out, gain_mlp, w_up, w_down, cotangent):
     slices = 3
-    ahead = 2
-    rows_in, log_rows, normed, joined, attended, hidden, qkv_w, out_w, up_have, down_have = front_comm(
-        ahead, slices, seq_lens, pass_idx, inputs[0], pass_table, gain_attn[None], gain_mlp[None], w_qkv, w_out,
+    (
+        rows_in, log_rows, mlp_gain_grad, up_half, down_half,
+        normed, joined, attended, qkv_w, out_w, outputs, hidden_grad, up_done, down_done,
+    ) = fore_comm(
+        slices, seq_lens, pass_idx, pass_table, gain_attn[None], gain_mlp[None], inputs[0], cotangent[0], w_qkv, w_out,
         w_up, w_down,
-    )
-    outputs, hidden_grad, mlp_gain_grad, up_done, down_done, up_half, down_half = mlp_comm(
-        ahead, slices, hidden, cotangent[0], rows_in, up_have, down_have, w_up, w_down
     )
     grad_input, small_sum, up_total, down_total, attn_total = back_comm(
         reps, seq_lens, pass_idx, rows_in, log_rows, mlp_gain_grad, up_done, down_done, up_half, down_half,

time: 208 us -> 189 us (0.909)
  Pallas kernels: 205 us -> 186 us
    pallas_call x2 -> x1, Pallas kernels: 124 us -> 104 us  [fore_comm(): pl.pallas_call(functools.partial(fore_comm_kernel, 256, 512, group, slice...]
where the time goes in v4:
time: 189 us; the launch traced here: 188 us
  Pallas kernels  186 us (98%)
  between operations  2.13 us (1%)
    pallas_call x1, Pallas kernels, fore_comm(): pl.pallas_call(functools.partial(fore_comm_kernel, 256, 512, group, slice...  104 us
    pallas_call x1, Pallas kernels, back_comm(): pl.pallas_call(functools.partial(back_comm_kernel, 256, 512, group), out_...  75.6 us
    pallas_call x1, Pallas kernels, finish_places(): pl.pallas_call(place_kernel, out_shape=[shaped((passes, part), F32), shap...  6.6 us

profile of v4, /device:TPU:0, one launch (start us, length us, event | category | flops | bytes accessed | tf_op | source)
XLA Modules:
  0.0 188.4 jit_solution(4535948736915311024)
XLA Ops:
  1.9 104.1 %shard_map.178 = (f32[8,768]{1,0:T(8,128)}, f32[16,1024]{1,0:T(8,128)}, f32[8,768]{1,0:T(8,128)}, bf16[2,2,96,1024]{3,2,1,0:T(8,128)(2,1)}, bf16[2,2,128,768]{3,...) custom-call(s32[1]{0:T(128)S(6)} %copy.20.length_ref, ...), custom_call_target="tpu_custom_call" | custom-call | tf_op jit(solution)/shard_map/pallas_call | solution.py:948
  106.1 75.6 %shard_map.179 = (f32[1024,768]{1,0:T(8,128)}, f32[8,768]{1,0:T(8,128)}, bf16[3,96,1024]{2,1,0:T(8,128)(2,1)}, bf16[3,128,768]{2,1,0:T(8,128)(2,1)}, bf16[4,96,768]{2,1,0:T(8,128)(2,1)}) custom-call(s32[1]{0:T(128)S(6)} %copy.20.length_ref, s32[1]{0:T(128)S(6)} %copy.21.pass_ref, f32[8,768]{1,0:T(8,128)} %get-tuple-element.37.rows_in, ...), custom_call_target="tpu_custom_call" | custom-call | tf_op jit(solution)/shard_map/pallas_call | solution.py:1288
  181.7 6.6 %shard_map.180 = (f32[5,96]{1,0:T(8,128)}, f32[1,96]{1,0:T(1,128)}, f32[1,96]{1,0:T(1,128)}, bf16[1024,768]{1,0:T(8,128)(2,1)}, f32[1024,768]{1,0:T(8,128)}, /*i...) custom-call(f32[8,768]{1,0:T(8,128)} %get-tuple-element.50.small_sum, ...), custom_call_target="tpu_custom_call" | custom-call | tf_op jit(solution)/shard_map/pallas_call | solution.py:1389

commit v5 on v4

--- a/solution.py
+++ b/solution.py
@@ -458,9 +458,15 @@
 
 def part_of(ref, rows, lead, start, width):
     def part(shard, side, half):
-        count = rows if side is None else rows // 2
-        first = shard * rows if side is None else shard * rows + side * count
-        left, wide = (start, width) if half is None else (start + half * (width // 2), width // 2)
+        count, first, left, wide = rows, shard * rows, start, width
+        if side is None and half is not None:
+            side, half = half, None
+        if side is not None:
+            count = rows // 2
+            first = first + side * count
+        if half is not None:
+            wide = width // 2
+            left = start + half * wide
         return ref.at[lead + (pl.ds(pl.multiple_of(first, count), count), pl.ds(left, wide))]
 
     return part
@@ -483,20 +489,21 @@
     return [(own.at[pl.ds(index * count, count), :], ref.at[index, rows, :])]
 
 
-def pair_columns(pair, width):
-    return [pl.ds(pl.multiple_of(plane * width + pair * PAIR, PAIR), PAIR) for plane in range(3)]
+def pair_columns(pair):
+    return [pl.ds(pl.multiple_of((3 * pair + plane) * PAIR, PAIR), PAIR) for plane in range(3)]
 
 
 def attention_rows(joined, attended, log_rows, key_bias, pair, block, between):
-    rows, width = attended.shape
-    columns, key_columns, value_columns = pair_columns(pair, width)
+    rows = attended.shape[0]
+    columns = pl.ds(pl.multiple_of(pair * PAIR, PAIR), PAIR)
+    query_columns, key_columns, value_columns = pair_columns(pair)
     keys = joined[:, key_columns]
     values = joined[:, value_columns]
     bias = key_bias[...]
     biased = [key_with_bias(keys, bias, head)[0] for head in range(2)]
     for first in range(0, rows, block):
         live = first + block
-        query = joined[pl.ds(first, block), columns]
+        query = joined[pl.ds(first, block), query_columns]
         mixed = []
         sums = []
         for head in range(2):
@@ -527,43 +534,38 @@
         normed[at, :] = (norm_parts(entered)[0] * gain).astype(BF16)
 
 
-def select_lanes(place, part, width):
-    rows = lax.broadcasted_iota(jnp.int32, (part, width), 0)
-    lanes = lax.broadcasted_iota(jnp.int32, (part, width), 1)
-    return lanes == rows + place.me * part
-
-
-SHARED = (False, True, True, False, True, True, False, True, True, False)
+SHARED = (False, False, True, True, False, True, True, False, True, True, False)
+SPANS = ((0, 1), (1, 1), (2, 2), (4, 2))
 
 PLAN = {
     "begin": "r0 s2",
     "normed": "f0 r1",
-    (0, 0): "s3",
+    (0, 0): "r2 s3",
     (0, 1): "f1",
-    (0, 2): "r2",
-    (0, 3): "s4",
-    (1, 2): "a1",
-    (1, 3): "r3 f2",
-    (2, 0): "s5",
-    (2, 1): "r4",
-    (2, 3): "a2 f3",
-    (3, 0): "s6",
-    (3, 3): "f4 r5",
-    (4, 0): "s7",
-    (4, 3): "a4 f5 r6",
-    (5, 0): "s8",
-    (5, 3): "r7",
-    "row 1": "a5 f6 s9",
-    "mlp 0 0": "f7 r8",
-    "mlp 0 1": "r9",
-    "mlp 0 down": "a7 f8",
-    "mlp 0 up": "f9",
-    "mlp 1 0": "a8",
+    (0, 3): "f2 s4",
+    (1, 1): "r3",
+    (1, 2): "a2",
+    (1, 3): "s5",
+    (2, 0): "f3 r4",
+    (2, 2): "s6",
+    (2, 3): "r5",
+    (3, 1): "a3 f4",
+    (3, 2): "s7",
+    (4, 0): "f5 r6",
+    (4, 3): "s8",
+    (5, 1): "a5 r7 f6",
+    (5, 3): "s9",
+    "row 0": "r8",
+    "row 1": "a6 f7 s10",
+    "mlp 0 0": "f8 r9",
+    "mlp 0 1": "r10",
+    "mlp 0 down": "a8 f9",
+    "mlp 1 0": "a9 f10",
 }
 
 
 def fore_comm_kernel(
-    block, tile, group, slices,
+    block, tile, slices,
     length_ref, pass_ref, table_own, attn_gain_own, mlp_gain_own,
     inputs_in, cotangent_in, qkv_own, out_own, up_own, down_own,
     rows_out, log_out, gain_grad,
@@ -578,9 +580,8 @@
     rows, width = inputs.shape
     shards = slots.shape[0]
     part = qkv_own.shape[0]
-    groups = width // group
+    groups = len(SPANS)
     pairs = width // PAIR
-    per_group = group // PAIR
 
     pieces = []
 
@@ -589,13 +590,13 @@
         pieces.append(Gather(place, part_at, fills, sends, recvs, local, row, SHARED[row]))
 
     own_rows = pl.ds(pl.multiple_of(place.me * part, part), part)
-    for index in range(groups):
-        columns = pl.ds(index * group, group)
+    for start, number in SPANS:
         fills = [
-            (qkv_own.at[:, pl.ds(plane * width + index * group, group)], qkv_w.at[plane, own_rows, columns])
-            for plane in range(3)
+            (qkv_own.at[:, pl.ds(plane * width + pair * PAIR, PAIR)], qkv_w.at[own_rows, columns])
+            for pair in range(start, start + number)
+            for plane, columns in enumerate(pair_columns(pair))
         ]
-        add(part_of(qkv_w, part, (slice(None),), index * group, group), fills)
+        add(part_of(qkv_w, part, (), start * 3 * PAIR, number * 3 * PAIR), fills)
     add(part_of(out_w, part, (), 0, width), [(out_own, out_w.at[own_rows, :])])
     for index in range(slices):
         add(part_of(up_w, part, (index,), 0, up_w.shape[2]), up_fills(up_own, up_w, index, place, shards))
@@ -611,11 +612,10 @@
         piece.fill()
     take[1].start()
 
-    chosen = select_lanes(place, part, width).astype(BF16)
     small_wide[...] = jnp.zeros_like(small_wide)
-    small_wide[0 : table_own.shape[0], :] = mm(table_own[...], chosen)
-    small_wide[8:9, :] = mm(attn_gain_own[...], chosen)
-    small_wide[9:10, :] = mm(mlp_gain_own[...], chosen)
+    small_wide[0 : table_own.shape[0], 0:part] = table_own[...].astype(F32)
+    small_wide[8:9, 0:part] = attn_gain_own[...].astype(F32)
+    small_wide[9:10, 0:part] = mlp_gain_own[...].astype(F32)
     small_own[...] = small_wide[...].astype(BF16)
     slots[place.me] = small_own[...]
 
@@ -625,9 +625,9 @@
         remote(small_own, slots.at[place.me], small_sends, small_recvs, shift, place.at(other))
         for shift, other in enumerate(others)
     ]
-    pieces[0].start()
     for copy in smalls:
         copy.start()
+    pieces[0].start()
     pieces[1].start()
 
     def step_on(point):
@@ -650,9 +650,7 @@
     fill_bias(length_ref[0], key_bias)
     for copy in smalls:
         copy.wait_recv()
-    total = slots[0].astype(F32)
-    for shard in range(1, shards):
-        total = total + slots[shard].astype(F32)
+    total = jnp.concatenate([slots[shard].astype(F32)[:, 0:part] for shard in range(shards)], axis=1)
     places = lax.broadcasted_iota(jnp.int32, total.shape, 0)
     rows_out[0:1, :] = jnp.sum(jnp.where(places == pass_ref[0], total, 0.0), axis=0, keepdims=True)
     rows_out[1:3, :] = total[8:10]
@@ -674,21 +672,18 @@
 
     @pl.loop(0, pairs)
     def _(pair):
-        for index in range(groups):
-            @pl.when(pair == index * per_group)
-            def _(index=index):
+        for index, (start, number) in enumerate(SPANS):
+            @pl.when(pair == start)
+            def _(index=index, start=start, number=number):
                 pieces[index].ready()
                 if index == groups - 1:
                     qkv_save.start()
-
-        @pl.when(lax.rem(pair, per_group) == 0)
-        def _():
-            columns = pl.ds(pl.multiple_of(pair * PAIR, group), group)
-
-            @pl.loop(0, 3)
-            def _(plane):
-                target = pl.ds(pl.multiple_of(plane * width + pair * PAIR, group), group)
-                joined[:, target] = mm(normed[...], qkv_w[plane, :, columns]).astype(BF16)
+                columns = pl.ds(start * 3 * PAIR, number * 3 * PAIR)
+
+                @pl.loop(0, rows // tile)
+                def _(step):
+                    at = pl.ds(step * tile, tile)
+                    joined[at, columns] = mm(normed[at, :], qkv_w[:, columns]).astype(BF16)
 
         def between(place_at):
             for index in range(pairs):
@@ -856,8 +851,8 @@
         self.place, self.grads, self.first = place, grads, first
         self.in_x, self.in_y, self.last = by_x, by_y, last
         self.sends, self.recvs, self.row = sends, recvs, row
-        half = first.shape[-1] // 2
-        self.left, self.right = pl.ds(0, half), pl.ds(half, half)
+        half = first.shape[-2] // 2
+        self.upper, self.lower = pl.ds(0, half), pl.ds(half, half)
 
     def copy(self, slot, src, dst, shard):
         return remote(src, dst, self.sends, self.recvs, (self.row, slot), self.place.at(shard))
@@ -869,15 +864,15 @@
     def spread_copies(self):
         p = self.place
         return [
-            self.copy(1, self.first.at[:, 1 - p.x, :, self.left], self.in_x, p.by_x),
-            self.copy(2, self.first.at[1 - p.y, :, :, self.right], self.in_y, p.by_y),
+            self.copy(1, self.first.at[:, 1 - p.x, self.upper], self.in_x, p.by_x),
+            self.copy(2, self.first.at[1 - p.y, :, self.lower], self.in_y, p.by_y),
         ]
 
     def fold_copies(self):
         p = self.place
         return [
-            self.copy(3, self.in_x.at[1 - p.y], self.last.at[:, self.left], p.by_y),
-            self.copy(4, self.in_y.at[1 - p.x], self.last.at[:, self.right], p.by_x),
+            self.copy(3, self.in_x.at[1 - p.y], self.last.at[self.upper], p.by_y),
+            self.copy(4, self.in_y.at[1 - p.x], self.last.at[self.lower], p.by_x),
         ]
 
     def swap(self):
@@ -901,9 +896,9 @@
         for copy in self.spread_copies():
             copy.wait_recv()
         for other in range(2):
-            total = self.first[other, p.x, :, self.left].astype(F32) + self.in_x[other].astype(F32)
+            total = self.first[other, p.x, self.upper].astype(F32) + self.in_x[other].astype(F32)
             self.in_x[other] = total.astype(BF16)
-            total = self.first[p.y, other, :, self.right].astype(F32) + self.in_y[other].astype(F32)
+            total = self.first[p.y, other, self.lower].astype(F32) + self.in_y[other].astype(F32)
             self.in_y[other] = total.astype(BF16)
         for copy in self.fold_copies():
             copy.start()
@@ -912,8 +907,8 @@
         p = self.place
         for copy in self.fold_copies():
             copy.wait_recv()
-        target[:, self.left] = (self.last[:, self.left].astype(F32) + self.in_x[p.y].astype(F32)).astype(BF16)
-        target[:, self.right] = (self.last[:, self.right].astype(F32) + self.in_y[p.x].astype(F32)).astype(BF16)
+        target[self.upper] = (self.last[self.upper].astype(F32) + self.in_x[p.y].astype(F32)).astype(BF16)
+        target[self.lower] = (self.last[self.lower].astype(F32) + self.in_y[p.x].astype(F32)).astype(BF16)
 
     def drain(self, swapped=True, spread=True):
         if swapped:
@@ -926,7 +921,7 @@
 def scatter_scratch(count, part, columns, slots=None):
     return [
         pltpu.VMEM((slots or count, 2, 2, 2, part, columns), BF16), pltpu.VMEM((count, 2, 2, part, columns), BF16),
-        pltpu.VMEM((count, 2, part, columns // 2), BF16), pltpu.VMEM((count, 2, part, columns // 2), BF16),
+        pltpu.VMEM((count, 2, part // 2, columns), BF16), pltpu.VMEM((count, 2, part // 2, columns), BF16),
         pltpu.VMEM((count, part, columns), BF16),
     ]
 
@@ -940,26 +935,24 @@
     up_part, chunk = up.shape[0], up.shape[1] // slices
     down_part = down.shape[0] // slices
     shards = width // up_part
-    group = 4 * HEAD_DIM
-    groups = width // group
-    count = groups + 1 + 2 * slices
+    count = len(SPANS) + 1 + 2 * slices
     vm = lambda *shape: pltpu.VMEM(shape, BF16)
     vf = lambda *shape: pltpu.VMEM(shape, F32)
     return pl.pallas_call(
-        functools.partial(fore_comm_kernel, 256, 512, group, slices),
+        functools.partial(fore_comm_kernel, 256, 512, slices),
         out_shape=[
             shaped((8, width), F32), shaped((16, rows), F32), shaped((8, width), F32),
             shaped((2, 2, up_part, chunk), BF16), shaped((2, 2, down_part, width), BF16),
             shaped((rows, width), BF16), shaped((rows, 3 * width), BF16), shaped((rows, width), BF16),
-            shaped((3, width, width), BF16), shaped((width, width), BF16), shaped((rows, width), BF16),
+            shaped((width, 3 * width), BF16), shaped((width, width), BF16), shaped((rows, width), BF16),
             shaped((rows, width), F32), shaped((slices - 1, up_part, chunk), BF16),
             shaped((slices - 1, down_part, width), BF16),
         ],
         in_specs=smem_spec(2) + vmem_spec(3) + any_spec(6),
         out_specs=vmem_spec(3) + any_spec(11),
         scratch_shapes=[
-            vm(rows, width), vm(rows, width), vm(shards, 16, width), vf(16, width), vm(16, width), vm(rows, width),
-            vm(rows, 3 * width), vm(rows, width), vf(rows, width), vm(3, width, width), vm(width, width),
+            vm(rows, width), vm(rows, width), vm(shards, 16, PAIR), vf(16, PAIR), vm(16, PAIR), vm(rows, width),
+            vm(rows, 3 * width), vm(rows, width), vf(rows, width), vm(width, 3 * width), vm(width, width),
             vm(slices, width, chunk), vm(slices, chunk, width), vm(rows, PAIR), vf(rows, width), vf(rows, width),
             vm(slices - 1, up_part, chunk), vm(slices - 1, down_part, width),
         ]
@@ -1024,9 +1017,12 @@
             self.out_copy().wait_send()
 
 
-def attention_columns(joined, log_rows, grads, joined_grad, key_bias, key_total, value_total, pair, block):
-    rows, width = grads.shape
-    columns, key_columns, value_columns = pair_columns(pair, width)
+def attention_columns(
+    joined, log_rows, grads, joined_grad, key_bias, key_total, value_total, pair, block, between,
+):
+    rows = grads.shape[0]
+    columns = pl.ds(pl.multiple_of(pair * PAIR, PAIR), PAIR)
+    query_columns, key_columns, value_columns = pair_columns(pair)
     keys = joined[:, key_columns]
     values = joined[:, value_columns]
     bias = key_bias[...]
@@ -1035,7 +1031,7 @@
     value_total[...] = jnp.zeros_like(value_total)
     for first in range(0, rows, block):
         live = first + block
-        query = joined[pl.ds(first, block), columns]
+        query = joined[pl.ds(first, block), query_columns]
         grad = grads[pl.ds(first, block), columns]
         query_grad = None
         for head in range(2):
@@ -1055,13 +1051,17 @@
             key_total[:live, :] += mm(score_grad, asked_only)
             part = mm(score_grad, biased[head][1][:live], TN)
             query_grad = part if query_grad is None else query_grad + part
-        joined_grad[0, pl.ds(first, block), columns] = (query_grad * HEAD_DIM**-0.5).astype(BF16)
-    joined_grad[1, :, columns] = key_total[...].astype(BF16)
-    joined_grad[2, :, columns] = value_total[...].astype(BF16)
+        joined_grad[pl.ds(first, block), query_columns] = (query_grad * HEAD_DIM**-0.5).astype(BF16)
+        if live == rows:
+            joined_grad[:, key_columns] = key_total[...].astype(BF16)
+            joined_grad[:, value_columns] = value_total[...].astype(BF16)
+        if first // block % 2 == 1:
+            between(first // block - 1)
+            between(first // block)
 
 
 def back_comm_kernel(
-    block, tile, group,
+    block, tile,
     length_ref, pass_ref, rows_in, log_rows, mlp_gain_grad, up_done, down_done, up_half, down_half,
     hidden_grad_in, out_in, attended_in, normed_in, joined_in, qkv_in, inputs_in,
     grad_input_out, small_sum, up_total, down_total, attn_total,
@@ -1070,7 +1070,7 @@
     grads, first, in_x, in_y, last, block_sum,
     up_x, up_y, up_last, up_block, down_x, down_y, down_last, down_block,
     up_in, up_mid, up_out, down_in, down_mid, down_out, attn_in, attn_mid, attn_out,
-    small_own, small_slots, small_plane, small_reps,
+    small_own, small_parts, small_slots, small_plane, small_reps,
     sends, recvs, up_sends, up_recvs, down_sends, down_recvs, z_sends, z_recvs,
     plane_sends, plane_recvs, rep_sends, rep_recvs, loads, saves,
 ):
@@ -1079,9 +1079,7 @@
     shards = small_slots.shape[0]
     reps = small_reps.shape[0]
     chunks = up_total.shape[0]
-    groups = width // group
     pairs = width // PAIR
-    per_group = group // PAIR
     others = [lax.rem(place.me + shift, shards) for shift in range(1, shards)]
     others_z = [lax.rem(place.z + shift, reps) for shift in range(1, reps)]
     take = [
@@ -1098,14 +1096,15 @@
     up_late = Scatter(place, None, up_half, up_x, up_y, up_last, up_sends, up_recvs, 0)
     down_late = Scatter(place, None, down_half, down_x, down_y, down_last, down_sends, down_recvs, 0)
 
+    half = 3 * PAIR
+    sent = [(0, 0, 2 * half), (1, 0, 2 * half), (2, 0, 2 * half), (3, 0, half), (3, half, half)]
+
     def message(index):
+        slot, start, wide = sent[index]
+        view = lambda ref: ref.at[(slot,) + (slice(None),) * (len(ref.shape) - 2) + (pl.ds(start, wide),)]
         return Scatter(
-            place, grads.at[index], first.at[index], in_x.at[index], in_y.at[index], last.at[index],
-            sends, recvs, index,
+            place, view(grads), view(first), view(in_x), view(in_y), view(last), sends, recvs, index,
         )
-
-    out_msg = message(0)
-    qkv_msg = [message(1 + index) for index in range(groups)]
 
     lines = {}
 
@@ -1118,9 +1117,10 @@
              down_in.at[index], down_mid.at[index], down_out.at[index], down_total.at[index])
         line(("u", index), up_block if final else up_done.at[index],
              up_in.at[index], up_mid.at[index], up_out.at[index], up_total.at[index])
-    for index in range(1 + groups):
-        line(("a", index), block_sum.at[index], attn_in.at[index], attn_mid.at[index], attn_out.at[index],
-             attn_total.at[index])
+    for index, (slot, start, wide) in enumerate(sent):
+        line(("a", index), *(
+            ref.at[slot, :, pl.ds(start, wide)] for ref in (block_sum, attn_in, attn_mid, attn_out, attn_total)
+        ))
 
     down_late.spread()
     up_late.spread()
@@ -1139,106 +1139,122 @@
         branch_grad[at, :] = shown
         attended_grad[at, :] = mm(shown, out_w[...], NT).astype(BF16)
 
-    lines["d", 0].cross()
     take[2].wait()
     grads[0] = mm(attended[...], branch_grad[...], TN).astype(BF16).reshape(grads.shape[1:])
-    out_msg.swap()
+    message(0).swap()
+    lines["d", 0].cross()
     down_late.fold()
-    for copy in take[3:]:
-        copy.wait()
-
-    def late_close(message, target, key):
-        message.close(target)
+    take[3].wait()
+
+    def late_close(late, target, key):
+        late.close(target)
         lines[key].begin()
 
     def close(index):
-        message(index).close(block_sum.at[index])
+        slot, start, wide = sent[index]
+        message(index).close(block_sum.at[slot, :, pl.ds(start, wide)])
         lines["a", index].begin()
 
     def send(index):
         message(index).merge()
         message(index).spread()
 
-    after_pair = [
-        lambda: (lines["u", 0].cross(), up_late.fold(), send(0), lines["d", 0].settle()),
-        lambda: (lines["d", 1].cross(), lines["u", 1].cross(), late_close(down_late, down_block, ("d", 2)),
-                 late_close(up_late, up_block, ("u", 2)), lines["u", 0].settle(), out_msg.fold()),
-        lambda: (send(1),),
-        lambda: (lines["d", 1].settle(), lines["u", 1].settle(), lines["d", 2].cross(), lines["u", 2].cross(),
-                 close(0), qkv_msg[0].fold()),
-        lambda: (send(2), close(1)),
-        lambda: (lines["a", 0].cross(), lines["d", 2].settle(), lines["u", 2].settle(), lines["a", 1].cross(),
-                 qkv_msg[1].fold()),
-    ]
+    def fold(index):
+        message(index).fold()
+
+    def cross(*keys):
+        for key in keys:
+            lines[key[0], int(key[1])].cross()
+
+    def settle(*keys):
+        for key in keys:
+            lines[key[0], int(key[1])].settle()
+
+    def gradient(index):
+        slot, start, wide = sent[index]
+        columns = pl.ds((slot - 1) * 2 * half + start, wide)
+        part = mm(normed[...], joined_grad[:, columns], TN).astype(BF16)
+        grads[slot, :, :, :, :, pl.ds(start, wide)] = part.reshape(grads.shape[1:5] + (wide,))
+        message(index).swap()
+
+    plan = {
+        (0, 1): lambda: send(0),
+        (0, 2): lambda: (cross("u0"), up_late.fold()),
+        (0, 3): lambda: late_close(down_late, down_block, ("d", 2)),
+        (1, 0): lambda: settle("d0"),
+        (1, 2): lambda: (cross("d1"), fold(0)),
+        (1, 3): lambda: (late_close(up_late, up_block, ("u", 2)), settle("u0"), take[4].wait(), gradient(1)),
+        (2, 0): lambda: (cross("u1"), close(0)),
+        (2, 2): lambda: (send(1), settle("d1")),
+        (2, 3): lambda: cross("d2"),
+        (3, 2): lambda: (settle("u1"), cross("u2")),
+        (3, 3): lambda: (fold(1), gradient(2)),
+        (4, 0): lambda: (cross("a0"), settle("d2")),
+        (4, 1): lambda: send(2),
+        (4, 2): lambda: close(1),
+        (4, 3): lambda: (settle("u2"), gradient(3)),
+        (5, 0): lambda: fold(2),
+        (5, 1): lambda: (send(3), settle("a0")),
+        (5, 2): lambda: cross("a1"),
+        (5, 3): lambda: (close(2), gradient(4), fold(3)),
+    }
 
     @pl.loop(0, pairs)
     def _(pair):
+        def between(place_at):
+            for index in range(pairs):
+                if (index, place_at) in plan:
+                    @pl.when(pair == index)
+                    def _(index=index):
+                        plan[index, place_at]()
+
         attention_columns(
-            joined, log_rows, attended_grad, joined_grad, key_bias, key_total, value_total, pair, block
+            joined, log_rows, attended_grad, joined_grad, key_bias, key_total, value_total, pair, block, between
         )
 
-        @pl.when(lax.rem(pair, per_group) == per_group - 1)
-        def _():
-            index = pair // per_group
-            columns = pl.ds(pl.multiple_of(index * group, group), group)
-            for plane in range(3):
-                part = mm(normed[...], joined_grad[plane, :, columns], TN).astype(BF16)
-                grads[1 + index, :, :, :, :, pl.ds(plane * group, group)] = part.reshape(
-                    grads.shape[1:5] + (group,)
-                )
-            message(1 + index).swap()
-
-        for index in range(pairs):
-            @pl.when(pair == index)
-            def _(index=index):
-                after_pair[index]()
-
     small_own[...] = jnp.zeros_like(small_own)
-
-    def after_rows(step):
-        @pl.when(step == 0)
-        def _():
-            send(3)
-            close(2)
-
-        @pl.when(step == 1)
-        def _():
-            lines["a", 0].settle()
-
-        @pl.when(step == 3)
-        def _():
-            qkv_msg[2].fold()
-            lines["a", 1].settle()
-            lines["a", 2].cross()
+    take[5].wait()
+    take[6].wait()
+    after_rows = [
+        lambda: (send(4), settle("a1")),
+        lambda: (close(3), cross("a2")),
+        lambda: fold(4),
+        lambda: cross("a3"),
+    ]
 
     @pl.loop(0, rows // 256)
     def _(step):
         at = pl.ds(step * 256, 256)
-        grad = mm(joined_grad[0, at, :], qkv_w[0], NT)
-        grad = grad + mm(joined_grad[1, at, :], qkv_w[1], NT)
-        grad = grad + mm(joined_grad[2, at, :], qkv_w[2], NT)
+        grad = mm(joined_grad[at, :], qkv_w[...], NT)
         unit, scale = norm_parts(inputs[at, :].astype(F32) + rows_in[0:1, :])
         total = hidden_grad[at, :] + norm_back(unit, scale, grad, rows_in[1:2, :])
         grad_input[at, :] = total
         small_own[5:6, :] += jnp.sum(grad * unit, axis=0, keepdims=True)
         small_own[0:1, :] += jnp.sum(total, axis=0, keepdims=True)
         pltpu.make_async_copy(grad_input.at[at, :], grad_input_out.at[at, :], saves.at[step]).start()
-        after_rows(step)
+        for index in range(rows // 256):
+            @pl.when(step == index)
+            def _(index=index):
+                after_rows[index]()
 
     places = lax.broadcasted_iota(jnp.int32, small_own.shape, 0)
     own = small_own[...]
     table = jnp.where((places == pass_ref[0]) & (places < 5), own[0:1], 0.0)
     own = jnp.where(places == 5, own, table)
-    small_own[...] = jnp.where(places == 6, mlp_gain_grad[0:1], own)
-    small_slots[place.me] = small_own[...]
+    own = jnp.where(places == 6, mlp_gain_grad[0:1], own)
+    part = width // shards
+    small_parts[...] = jnp.zeros_like(small_parts)
+    for shard in range(shards):
+        small_parts[shard, :, 0:part] = own[:, shard * part : (shard + 1) * part]
+    small_slots[place.me] = small_parts[place.me]
     plane_copies = [
-        remote(small_own, small_slots.at[place.me], plane_sends, plane_recvs, shift, place.at(other))
+        remote(small_parts.at[other], small_slots.at[place.me], plane_sends, plane_recvs, shift, place.at(other))
         for shift, other in enumerate(others)
     ]
     for copy in plane_copies:
         copy.start()
-    close(3)
-    lines["a", 2].settle()
+    close(4)
+    settle("a2")
     for copy in plane_copies:
         copy.wait_recv()
     total = small_slots[0]
@@ -1252,17 +1268,18 @@
     ]
     for copy in rep_copies:
         copy.start()
-    lines["a", 3].cross()
+    settle("a3")
+    cross("a4")
     for copy in rep_copies:
         copy.wait_recv()
     total = small_reps[0]
     for rep in range(1, reps):
         total = total + small_reps[rep]
     small_sum[...] = total
-    lines["a", 3].settle()
+    settle("a4")
     for key in lines:
         lines[key].finish()
-    for index in range(1 + groups):
+    for index in range(len(sent)):
         message(index).drain()
     up_late.drain(swapped=False)
     down_late.drain(swapped=False)
@@ -1286,29 +1303,30 @@
     vm = lambda *shape: pltpu.VMEM(shape, BF16)
     vf = lambda *shape: pltpu.VMEM(shape, F32)
     return pl.pallas_call(
-        functools.partial(back_comm_kernel, 256, 512, group),
+        functools.partial(back_comm_kernel, 256, 512),
         out_shape=[
-            shaped((rows, width), F32), shaped((8, width), F32), shaped((chunks, up_part, chunk), BF16),
+            shaped((rows, width), F32), shaped((8, PAIR), F32), shaped((chunks, up_part, chunk), BF16),
             shaped((chunks, down_part, width), BF16), shaped((count, up_part, wide), BF16),
         ],
         in_specs=smem_spec(2) + vmem_spec(7) + any_spec(7),
         out_specs=any_spec(1) + vmem_spec(4),
         scratch_shapes=[
             vf(rows, width), vm(width, width), vm(rows, width), vm(rows, width), vf(rows, width),
-            vm(3, width, width), vm(rows, 3 * width), vm(rows, width), vm(rows, width), vm(rows, width),
-            vm(3, rows, width), vm(rows, PAIR), vf(rows, PAIR), vf(rows, PAIR),
+            vm(width, 3 * width), vm(rows, 3 * width), vm(rows, width), vm(rows, width), vm(rows, width),
+            vm(rows, 3 * width), vm(rows, PAIR), vf(rows, PAIR), vf(rows, PAIR),
         ]
         + scatter_scratch(count, up_part, wide)
         + [
             vm(count, up_part, wide),
-            vm(2, up_part, chunk // 2), vm(2, up_part, chunk // 2), vm(up_part, chunk), vm(up_part, chunk),
-            vm(2, down_part, width // 2), vm(2, down_part, width // 2), vm(down_part, width), vm(down_part, width),
+            vm(2, up_part // 2, chunk), vm(2, up_part // 2, chunk), vm(up_part, chunk), vm(up_part, chunk),
+            vm(2, down_part // 2, width), vm(2, down_part // 2, width), vm(down_part, width), vm(down_part, width),
         ]
         + [vm(chunks, up_part, chunk)] * 3
         + [vm(chunks, down_part, width)] * 3
         + [vm(count, up_part, wide)] * 3
-        + [vf(8, width), vf(shards, 8, width), vf(8, width), vf(reps, 8, width)]
-        + dma((count, 5), (count, 5), (1, 5), (1, 5), (1, 5), (1, 5), (2 * chunks + count, 3), (2 * chunks + count, 3),
+        + [vf(8, width), vf(shards, 8, PAIR), vf(shards, 8, PAIR), vf(8, PAIR), vf(reps, 8, PAIR)]
+        + dma((count + 1, 5), (count + 1, 5), (1, 5), (1, 5), (1, 5), (1, 5), (2 * chunks + count + 1, 3),
+              (2 * chunks + count + 1, 3),
               (shards - 1,), (shards - 1,), (reps - 1,), (reps - 1,), (7,), (rows // 256,)),
         compiler_params=pltpu.CompilerParams(
             vmem_limit_bytes=VMEM_LIMIT, collective_id=3, has_side_effects=True
@@ -1323,11 +1341,9 @@
     outputs, grad_input, up_total, down_total, attn_total, qkv, out, up, down, loads, saves,
 ):
     slices, part, chunk = up_in.shape
-    width = small_sum.shape[1]
+    width = outputs.shape[1]
     shards = width // part
     lanes = chunk // shards
-    groups = attn_in.shape[0] - 1
-    group = attn_in.shape[2] // 3
     take = [
         pltpu.make_async_copy(source, target, loads.at[index])
         for index, (source, target) in enumerate((
@@ -1344,14 +1360,9 @@
     ]
     for copy in take:
         copy.start()
-    first = lax.axis_index("shard") * part
-    rows_at = lax.broadcasted_iota(jnp.int32, (width, part), 0)
-    lanes_at = lax.broadcasted_iota(jnp.int32, (width, part), 1)
-    chosen = (rows_at == lanes_at + first).astype(F32)
-    own = lax.dot_general(small_sum[...], chosen, NN, precision=lax.Precision.HIGHEST, preferred_element_type=F32)
-    table_out[...] = own[0 : table_out.shape[0]]
-    attn_gain_out[...] = own[5:6]
-    mlp_gain_out[...] = own[6:7]
+    table_out[...] = small_sum[0 : table_out.shape[0], 0:part]
+    attn_gain_out[...] = small_sum[5:6, 0:part]
+    mlp_gain_out[...] = small_sum[6:7, 0:part]
     take[0].wait()
     give[0].start()
     take[1].wait()
@@ -1362,10 +1373,11 @@
             ].astype(F32)
     give[1].start()
     take[2].wait()
-    for index in range(groups):
+    for pair in range(width // PAIR):
         for plane in range(3):
-            start = plane * width + index * group
-            qkv[:, start : start + group] = attn_total[1 + index, :, plane * group : (plane + 1) * group].astype(F32)
+            start = plane * width + pair * PAIR
+            source = (3 * (pair % 2) + plane) * PAIR
+            qkv[:, start : start + PAIR] = attn_total[1 + pair // 2, :, source : source + PAIR].astype(F32)
     out[...] = attn_total[0].astype(F32)
     give[2].start()
     give[3].start()

time: 189 us -> 182 us (0.963)
  Pallas kernels: 186 us -> 180 us
    pallas_call x2, Pallas kernels: 180 us -> 173 us  [the longest x1 101 us: fore_comm(): pl.pallas_call(functools.partial(fore_comm_kernel, 256, 512, slices), out...]
where the time goes in v5:
time: 182 us
  Pallas kernels  180 us (99%)
  between operations  2.13 us (1%)
    pallas_call x1, Pallas kernels, fore_comm(): pl.pallas_call(functools.partial(fore_comm_kernel, 256, 512, slices), out...  101 us
    pallas_call x1, Pallas kernels, back_comm(): pl.pallas_call(functools.partial(back_comm_kernel, 256, 512), out_shape=[...  72.2 us
    pallas_call x1, Pallas kernels, finish_places(): pl.pallas_call(place_kernel, out_shape=[shaped((passes, part), F32), shap...  6.54 us

profile of v5, /device:TPU:0, one launch (start us, length us, event | category | flops | bytes accessed | tf_op | source)
XLA Modules:
  0.0 181.8 jit_solution(12446831176094538292)
XLA Ops:
  1.9 100.9 %shard_map.178 = (f32[8,768]{1,0:T(8,128)}, f32[16,1024]{1,0:T(8,128)}, f32[8,768]{1,0:T(8,128)}, bf16[2,2,96,1024]{3,2,1,0:T(8,128)(2,1)}, bf16[2,2,128,768]{3,...) custom-call(s32[1]{0:T(128)S(6)} %copy.20.length_ref, ...), custom_call_target="tpu_custom_call" | custom-call | tf_op jit(solution)/shard_map/pallas_call | solution.py:941
  102.9 72.2 %shard_map.179 = (f32[1024,768]{1,0:T(8,128)}, f32[8,128]{1,0:T(8,128)}, bf16[3,96,1024]{2,1,0:T(8,128)(2,1)}, bf16[3,128,768]{2,1,0:T(8,128)(2,1)}, bf16[4,96,768]{2,1,0:T(8,128)(2,1)}) custom-call(s32[1]{0:T(128)S(6)} %copy.20.length_ref, s32[1]{0:T(128)S(6)} %copy.21.pass_ref, f32[8,768]{1,0:T(8,128)} %get-tuple-element.37.rows_in, ...), custom_call_target="tpu_custom_call" | custom-call | tf_op jit(solution)/shard_map/pallas_call | solution.py:1305
  175.1 6.5 %shard_map.180 = (f32[5,96]{1,0:T(8,128)}, f32[1,96]{1,0:T(1,128)}, f32[1,96]{1,0:T(1,128)}, bf16[1024,768]{1,0:T(8,128)(2,1)}, f32[1024,768]{1,0:T(8,128)}, /*i...) custom-call(f32[8,128]{1,0:T(8,128)} %get-tuple-element.50.small_sum, ...), custom_call_target="tpu_custom_call" | custom-call | tf_op jit(solution)/shard_map/pallas_call | solution.py:1401

commit v6 on v5

--- a/solution.py
+++ b/solution.py
@@ -1064,8 +1064,8 @@
     block, tile,
     length_ref, pass_ref, rows_in, log_rows, mlp_gain_grad, up_done, down_done, up_half, down_half,
     hidden_grad_in, out_in, attended_in, normed_in, joined_in, qkv_in, inputs_in,
-    grad_input_out, small_sum, up_total, down_total, attn_total,
-    hidden_grad, out_w, attended, inputs, grad_input,
+    grad_input_out, small_sum, up_total_out, down_total_out, attn_total,
+    hidden_grad, out_w, attended, inputs, grad_input, up_total, down_total,
     qkv_w, joined, branch_grad, attended_grad, normed, joined_grad, key_bias, key_total, value_total,
     grads, first, in_x, in_y, last, block_sum,
     up_x, up_y, up_last, up_block, down_x, down_y, down_last, down_block,
@@ -1255,6 +1255,15 @@
         copy.start()
     close(4)
     settle("a2")
+    early = [key for key in lines if key[0] != "a" or key[1] < 2]
+    for key in early:
+        lines[key].finish()
+    give = [
+        pltpu.make_async_copy(source, target, saves.at[rows // 256 + index])
+        for index, (source, target) in enumerate(((up_total, up_total_out), (down_total, down_total_out)))
+    ]
+    for copy in give:
+        copy.start()
     for copy in plane_copies:
         copy.wait_recv()
     total = small_slots[0]
@@ -1278,7 +1287,10 @@
     small_sum[...] = total
     settle("a4")
     for key in lines:
-        lines[key].finish()
+        if key not in early:
+            lines[key].finish()
+    for copy in give:
+        copy.wait()
     for index in range(len(sent)):
         message(index).drain()
     up_late.drain(swapped=False)
@@ -1309,9 +1321,10 @@
             shaped((chunks, down_part, width), BF16), shaped((count, up_part, wide), BF16),
         ],
         in_specs=smem_spec(2) + vmem_spec(7) + any_spec(7),
-        out_specs=any_spec(1) + vmem_spec(4),
+        out_specs=any_spec(1) + vmem_spec(1) + any_spec(2) + vmem_spec(1),
         scratch_shapes=[
             vf(rows, width), vm(width, width), vm(rows, width), vm(rows, width), vf(rows, width),
+            vm(chunks, up_part, chunk), vm(chunks, down_part, width),
             vm(width, 3 * width), vm(rows, 3 * width), vm(rows, width), vm(rows, width), vm(rows, width),
             vm(rows, 3 * width), vm(rows, PAIR), vf(rows, PAIR), vf(rows, PAIR),
         ]
@@ -1327,7 +1340,7 @@
         + [vf(8, width), vf(shards, 8, PAIR), vf(shards, 8, PAIR), vf(8, PAIR), vf(reps, 8, PAIR)]
         + dma((count + 1, 5), (count + 1, 5), (1, 5), (1, 5), (1, 5), (1, 5), (2 * chunks + count + 1, 3),
               (2 * chunks + count + 1, 3),
-              (shards - 1,), (shards - 1,), (reps - 1,), (reps - 1,), (7,), (rows // 256,)),
+              (shards - 1,), (shards - 1,), (reps - 1,), (reps - 1,), (7,), (rows // 256 + 2,)),
         compiler_params=pltpu.CompilerParams(
             vmem_limit_bytes=VMEM_LIMIT, collective_id=3, has_side_effects=True
         ),

time: 182 us -> 182 us (level)
  no operation moved by 1% of the time
where the time goes in v6:
time: 182 us; the launch traced here: 181 us
  Pallas kernels  179 us (98%)
  between operations  2.13 us (1%)
    pallas_call x1, Pallas kernels, fore_comm(): pl.pallas_call(functools.partial(fore_comm_kernel, 256, 512, slices), out...  101 us
    pallas_call x1, Pallas kernels, back_comm(): pl.pallas_call(functools.partial(back_comm_kernel, 256, 512), out_shape=[...  71.8 us
    pallas_call x1, Pallas kernels, finish_places(): pl.pallas_call(place_kernel, out_shape=[shaped((passes, part), F32), shap...  6.54 us

profile of v6, /device:TPU:0, one launch (start us, length us, event | category | flops | bytes accessed | tf_op | source)
XLA Modules:
  0.0 181.4 jit_solution(11461875536168387684)
XLA Ops:
  1.9 100.9 %shard_map.178 = (f32[8,768]{1,0:T(8,128)}, f32[16,1024]{1,0:T(8,128)}, f32[8,768]{1,0:T(8,128)}, bf16[2,2,96,1024]{3,2,1,0:T(8,128)(2,1)}, bf16[2,2,128,768]{3,...) custom-call(s32[1]{0:T(128)S(6)} %copy.20.length_ref, ...), custom_call_target="tpu_custom_call" | custom-call | tf_op jit(solution)/shard_map/pallas_call | solution.py:941
  102.9 71.8 %shard_map.179 = (f32[1024,768]{1,0:T(8,128)}, f32[8,128]{1,0:T(8,128)}, bf16[3,96,1024]{2,1,0:T(8,128)(2,1)}, bf16[3,128,768]{2,1,0:T(8,128)(2,1)}, bf16[4,96,768]{2,1,0:T(8,128)(2,1)}) custom-call(s32[1]{0:T(128)S(6)} %copy.20.length_ref, s32[1]{0:T(128)S(6)} %copy.21.pass_ref, f32[8,768]{1,0:T(8,128)} %get-tuple-element.37.rows_in, ...), custom_call_target="tpu_custom_call" | custom-call | tf_op jit(solution)/shard_map/pallas_call | solution.py:1317
  174.7 6.5 %shard_map.180 = (f32[5,96]{1,0:T(8,128)}, f32[1,96]{1,0:T(1,128)}, f32[1,96]{1,0:T(1,128)}, bf16[1024,768]{1,0:T(8,128)(2,1)}, f32[1024,768]{1,0:T(8,128)}, /*i...) custom-call(f32[8,128]{1,0:T(8,128)} %get-tuple-element.50.small_sum, ...), custom_call_target="tpu_custom_call" | custom-call | tf_op jit(solution)/shard_map/pallas_call | solution.py:1414
